TPU v7x, 512 devices: a whole 4x8x8 slice. The times are simulated.
512 devices in a mesh: row: 8 (over z), col: 16 (over y, core), vox: 4 (over x).
Axes of the slice: x: 4, y: 8, z: 8, core: 2. Of those that a mesh axis runs over, the one named last changes fastest.
Arguments:
- panel_top: bfloat16 [1024, 1024], P('row', ('col', 'vox')), may hold values from -0.059814453 to 0.059814453
- panel_low: bfloat16 [8192, 1024], P('row', ('col', 'vox')), may hold values from -1.1953125 to 1.1953125
- panel_next: bfloat16 [8192, 1024], P('row', ('col', 'vox')), may hold values from -1.1953125 to 1.1953125
- gram_rest: bfloat16 [8192, 8192], P('row', ('col', 'vox')), may hold values from -18 to 18
- inverses: bfloat16 [2, 1024, 1024], P(None, 'row'), as said below
- right_top: bfloat16 [2, 1024, 8192], P(None, None, ('col', 'vox')), may hold values from -1.796875 to 1.796875
- right_low: bfloat16 [8192, 8192], P('row', ('col', 'vox')), may hold values from -24 to 24
Outputs:
- factor: bfloat16 [2, 8192, 1024], P(None, 'row', ('col', 'vox'))
- solved: bfloat16 [2, 1024, 8192], P(None, None, ('col', 'vox'))
- trailing: float32 [8192, 8192], P('row', ('col', 'vox'))
- residual: float32 [8192, 8192], P('row', ('col', 'vox'))
Inputs may be any that keep to these rules, and one draw needn't show every extreme that they name: Each inverses[k] is lower triangular with diagonal entries from 1 to 2.
All inputs are finite; a program needn't handle non-finite values.
Results may differ from a plain program's by a relative error of at most 0.0057.
Values may be sent and summed in bfloat16 or wider, within the bound.
No kernel may reach another device: no remote copies, remote signals or barrier semaphores. Data moves between devices by JAX's collectives and lax.ppermute only.
A program may use at most 64 MiB of HBM per device.

v0:
```python
import jax
import jax.numpy as jnp
from jax import lax
from jax.sharding import PartitionSpec as P


def spread(block, axis, source):
    block = jnp.where(lax.axis_index(axis) == source, block, jnp.zeros_like(block))
    return lax.psum(block, axis)


def contract(left, right):
    return lax.dot_general(
        left, right, (((1,), (1,)), ((), ())), preferred_element_type=jnp.float32
    )


def per_device(panel_top, panel_low, panel_next, gram_rest, inverses, right_top, right_low):
    col_index = lax.axis_index(("col", "vox"))
    row_index = lax.axis_index("row")
    col_width = panel_low.shape[1]
    top_rows = panel_top.shape[0]
    low_rows = panel_low.shape[0]
    rest_cols = gram_rest.shape[1]
    root_row = col_index * rest_cols // low_rows
    whole_inverses = lax.all_gather(inverses, "row", axis=1, tiled=True)
    own_rows = lax.dynamic_slice_in_dim(whole_inverses, col_index * col_width, col_width, 1)
    rows_used = own_rows[0]
    own_top = contract(lax.all_gather(panel_top, ("col", "vox"), axis=1, tiled=True), rows_used)
    own_low = contract(lax.all_gather(panel_low, ("col", "vox"), axis=1, tiled=True), rows_used)
    first_top, first_low = (
        lax.all_gather(own_top.astype(jnp.bfloat16), ("col", "vox"), axis=1, tiled=True),
        lax.all_gather(own_low.astype(jnp.bfloat16), ("col", "vox"), axis=1, tiled=True),
    )
    outgoing = (
        lax.dynamic_slice_in_dim(
            first_top, col_index * col_width - root_row * top_rows, col_width, 0
        ),
        lax.dynamic_slice_in_dim(
            first_low, col_index * rest_cols - root_row * low_rows, rest_cols, 0
        ),
    )
    owner_top, owner_low = (
        spread(outgoing[0], "row", root_row),
        spread(outgoing[1], "row", root_row),
    )
    updated = (panel_next.astype(jnp.float32) - contract(first_low, owner_top)).astype(jnp.bfloat16)
    rows_used = own_rows[1]
    own_next = contract(lax.all_gather(updated, ("col", "vox"), axis=1, tiled=True), rows_used)
    second_low = lax.all_gather(own_next.astype(jnp.bfloat16), ("col", "vox"), axis=1, tiled=True)
    owner_next = spread(
        lax.dynamic_slice_in_dim(
            second_low, col_index * rest_cols - root_row * low_rows, rest_cols, 0
        ),
        "row",
        root_row,
    )
    trailing = (
        gram_rest.astype(jnp.float32)
        - contract(first_low, owner_low)
        - contract(second_low, owner_next)
    )
    first_solve = jnp.dot(
        whole_inverses[0], right_top[0], preferred_element_type=jnp.float32
    ).astype(jnp.bfloat16)
    top_slice = lax.dynamic_slice_in_dim(right_top[1], row_index * top_rows, top_rows, 0)
    top_part = (
        top_slice.astype(jnp.float32)
        - jnp.dot(first_top, first_solve, preferred_element_type=jnp.float32)
    ).astype(jnp.bfloat16)
    top_new = lax.all_gather(top_part, "row", axis=0, tiled=True)
    second_solve = jnp.dot(whole_inverses[1], top_new, preferred_element_type=jnp.float32).astype(
        jnp.bfloat16
    )
    residual = (
        right_low.astype(jnp.float32)
        - jnp.dot(first_low, first_solve, preferred_element_type=jnp.float32)
        - jnp.dot(second_low, second_solve, preferred_element_type=jnp.float32)
    )
    factor = jnp.stack(
        [
            lax.dynamic_slice_in_dim(first_low, col_index * col_width, col_width, 1),
            lax.dynamic_slice_in_dim(second_low, col_index * col_width, col_width, 1),
        ]
    )
    solved = jnp.stack([first_solve, second_solve])
    return (factor, solved, trailing, residual)


def solution(mesh):
    in_specs = (
        P("row", ("col", "vox")),
        P("row", ("col", "vox")),
        P("row", ("col", "vox")),
        P("row", ("col", "vox")),
        P(None, "row", None),
        P(None, None, ("col", "vox")),
        P("row", ("col", "vox")),
    )
    out_specs = (
        P(None, "row", ("col", "vox")),
        P(None, None, ("col", "vox")),
        P("row", ("col", "vox")),
        P("row", ("col", "vox")),
    )
    return jax.shard_map(
        per_device, mesh=mesh, in_specs=in_specs, out_specs=out_specs, check_vma=False
    )
```

profile of v0, /device:TPU:1, one launch (start us, length us, event | category | flops | bytes accessed | tf_op | source)
XLA Modules:
  0.0 584.4 jit_solution(6978349543570293704)
XLA Ops:
  7.2 0.0 copy-start.7
  7.2 0.0 all-gather.8.cloned.1.call-start
  7.2 0.7 all-gather.8.cloned.1.call-update
  7.9 0.0 all-gather.6.cloned.1.call-start
  8.0 0.7 all-gather.6.cloned.1.call-update
  8.7 0.0 copy-start.6
  8.7 0.0 all-gather.10.cloned.1.call-start
  8.7 90.9 %all-gather.8.cloned.1.call-done = bf16[1024,1024]{0,1:T(8,128)(2,1)} async-done(((bf16[1024,16]{0,1:T(8,128)(2,1)}), bf16[1024,1024]{0,1:T(8,128)(2,1)}) %all-gather.8.cloned.1.call-update) | async-done | bytes 2097168 | tf_op jit(solution)/shard_map/all_gather | solution.py:30
  99.7 58.0 %all-gather.6.cloned.1.call-done = bf16[2,1024,1024]{2,1,0:T(8,128)(2,1)} async-done(((bf16[2,128,1024]{2,1,0:T(8,128)(2,1)}), bf16[2,1024,1024]{2,1,0:T(8,128)(2,1)}) %all-gather.6.cloned.1.call-update) | async-done | bytes 4194320 | tf_op jit(solution)/shard_map/all_gather | solution.py:26
  157.7 2.6 fusion.6
  160.3 0.0 all-gather.10.cloned.1.call-update
  160.4 0.0 all-gather.12.cloned.1.call-start
  160.4 0.0 copy-done.7
  160.4 69.6 %all_gather.27 = bf16[128,1024]{0,1:T(8,128)(2,1)S(1)} all-gather(bf16[128,16]{0,1:T(8,128)(2,1)S(1)} %copy-done.7), channel_id=1, replica_groups=mesh['row'=8,'col'=16,'vox'=4] {'col','vox'}, dimensions={1}, use_global_device_ids=true | all-gather | bytes 266240 | tf_op jit(solution)/shard_map/all_gather | solution.py:29
  230.0 0.9 fusion.7
  230.9 67.5 %all_gather.28 = bf16[128,1024]{0,1:T(8,128)(2,1)S(1)} all-gather(bf16[128,16]{0,1:T(8,128)(2,1)S(1)} %fusion.7), channel_id=1, replica_groups=mesh['row'=8,'col'=16,'vox'=4] {'col','vox'}, dimensions={1}, use_global_device_ids=true | all-gather | bytes 266240 | tf_op jit(solution)/shard_map/all_gather | solution.py:32
  298.4 0.1 dynamic-slice_select_fusion.2
  298.5 23.2 %psum.21 = bf16[16,1024]{0,1:T(8,128)(2,1)S(1)} all-reduce(bf16[16,1024]{0,1:T(8,128)(2,1)S(1)} %dynamic-slice_select_fusion.2), channel_id=1, replica_groups=mesh['row'=8,'col'=16,'vox'=4] {'row'}, use_global_device_ids=true, to_apply=%region_0.1 | all-reduce | flops 16384 | bytes 65536 | tf_op jit(solution)/shard_map/psum | solution.py:9
  321.7 0.0 copy-start.4
  321.7 0.0 all-gather.10.cloned.1.call-done
  321.8 0.0 copy-done.6
  321.8 2.7 fusion.4
  324.5 0.0 all-gather.12.cloned.1.call-update
  324.5 0.0 all-gather.14.cloned.1.call-start
  324.5 89.5 %all-gather.12.cloned.1.call-done = bf16[1024,1024]{0,1:T(8,128)(2,1)} async-done(((bf16[1024,16]{0,1:T(8,128)(2,1)}), bf16[1024,1024]{0,1:T(8,128)(2,1)}) %all-gather.12.cloned.1.call-update) | async-done | bytes 2097168 | tf_op jit(solution)/shard_map/all_gather | solution.py:49
  414.0 2.6 convolution_convert_fusion
  416.6 0.0 all-gather.14.cloned.1.call-update
  416.6 0.0 all-reduce.3.cloned.1.call-start
  416.7 0.0 slice-start
  416.7 0.0 copy-done.4
  416.7 2.4 fusion.2
  419.2 0.3 fusion.5
  419.5 21.2 %all_gather.31 = bf16[1024,128]{1,0:T(8,128)(2,1)S(1)} all-gather(bf16[128,128]{1,0:T(8,128)(2,1)S(1)} %fusion.5), channel_id=1, replica_groups=mesh['row'=8,'col'=16,'vox'=4] {'row'}, dimensions={0}, use_global_device_ids=true | all-gather | bytes 294912 | tf_op jit(solution)/shard_map/all_gather | solution.py:71
  440.6 0.7 fusion.3
  441.4 0.8 pad_maximum_fusion
  442.2 0.0 copy-done
  442.2 0.8 dynamic-slice_select_fusion.1
  443.0 0.7 convolution_subtract_fusion.1
  443.7 54.5 %all-gather.14.cloned.1.call-done = bf16[1024,1024]{0,1:T(8,128)(2,1)} async-done(((bf16[1024,16]{0,1:T(8,128)(2,1)}), bf16[1024,1024]{0,1:T(8,128)(2,1)}) %all-gather.14.cloned.1.call-update) | async-done | bytes 2097168 | tf_op jit(solution)/shard_map/all_gather | solution.py:50
  498.3 1.7 dynamic-slice_select_fusion
  499.9 0.0 all-reduce.3.cloned.1.call-update
  500.0 0.8 dynamic-slice_bitcast_fusion.3
  500.7 0.6 pad_maximum_fusion.1
  501.4 3.2 convolution_subtract_fusion
  504.5 69.6 %all-reduce.3.cloned.1.call-done = (bf16[128,1024]{0,1:T(8,128)(2,1)}, bf16[128,1024]{0,1:T(8,128)(2,1)}) async-done(((bf16[128,1024]{0,1:T(8,128)(2,1)}, bf16[128,1024]{0,1:T(8,128)(2,1)}), (bf16[128,1024]{0,1:T(8,128)(2,1)}, bf16[128,1024]{0,1:T(8,128)(2,1)})) %all-reduce.3.cloned.1.call-update) | async-done | bytes 524304 | tf_op jit(solution)/shard_map/psum | solution.py:9
  574.1 0.0 copy-done.3
  574.1 1.8 convolution_subtract_fusion.3
  576.0 1.5 convolution_subtract_fusion.2
  (12 shorter events, 0.0 us)
Async XLA Ops:
  7.2 153.3 %copy-start.7 = (bf16[128,16]{0,1:T(8,128)(2,1)S(1)}, bf16[128,16]{0,1:T(8,128)(2,1)}, u32[]{:S(2)}) copy-start(bf16[128,16]{0,1:T(8,128)(2,1)} %param.7) | copy-start | bytes 12292
  7.2 92.5 %all-gather.8.cloned.1.call-start = ((), (), s32[]{:S(2)}) async-start(), calls=%async_computation.1 | async-start | bytes 2129920 | tf_op jit(solution)/shard_map/all_gather | solution.py:30
  7.9 149.8 %all-gather.6.cloned.1.call-start = ((), (), s32[]{:S(2)}) async-start(), calls=%async_computation | async-start | bytes 4718592 | tf_op jit(solution)/shard_map/all_gather | solution.py:26
  8.7 313.1 %copy-start.6 = (bf16[1024,16]{0,1:T(8,128)(2,1)S(1)}, bf16[1024,16]{0,1:T(8,128)(2,1)}, u32[]{:S(2)}) copy-start(bf16[1024,16]{0,1:T(8,128)(2,1)} %param.9) | copy-start | bytes 98308
  8.7 313.1 %all-gather.10.cloned.1.call-start = ((), (), s32[]{:S(2)}) async-start(), calls=%async_computation.2 | async-start | bytes 2129920 | tf_op jit(solution)/shard_map/all_gather | solution.py:33
  160.4 253.6 %all-gather.12.cloned.1.call-start = ((), (), s32[]{:S(2)}) async-start(), calls=%async_computation.3 | async-start | bytes 2129920 | tf_op jit(solution)/shard_map/all_gather | solution.py:49
  321.7 95.0 %copy-start.4 = (bf16[2,1024,128]{2,1,0:T(8,128)(2,1)S(1)}, bf16[2,1024,128]{2,1,0:T(8,128)(2,1)}, u32[]{:S(2)}) copy-start(bf16[2,1024,128]{2,1,0:T(8,128)(2,1)} %param.12) | copy-start | bytes 1572868
  324.5 173.8 %all-gather.14.cloned.1.call-start = ((), (), s32[]{:S(2)}) async-start(), calls=%async_computation.4 | async-start | bytes 2129920 | tf_op jit(solution)/shard_map/all_gather | solution.py:50
  416.6 157.5 %all-reduce.3.cloned.1.call-start = ((), (), s32[]{:S(2)}) async-start(), calls=%async_computation.5 | async-start | bytes 1048576 | tf_op jit(solution)/shard_map/psum | solution.py:9
  416.7 2.5 slice-start
  416.7 23.9 %copy-start.8 = (bf16[2,1024,1024]{2,1,0:T(8,128)(2,1)S(1)}, bf16[2,1024,1024]{2,1,0:T(8,128)(2,1)}, u32[]{:S(2)}) copy-start(bf16[2,1024,1024]{2,1,0:T(8,128)(2,1)} %all-gather.6.cloned.1.call-done) | copy-start | bytes 12582916
  440.6 1.6 copy-start
  440.6 2.4 copy-start.2
  501.4 72.8 %copy-start.3 = (bf16[1024,128]{1,0:T(8,128)(2,1)S(1)}, bf16[1024,128]{1,0:T(8,128)(2,1)}, u32[]{:S(2)}) copy-start(bf16[1024,128]{1,0:T(8,128)(2,1)} %param.10) | copy-start | bytes 786436
  574.1 1.8 copy-start.1
  574.1 1.9 copy-start.5
Sparse Core Ops, SparseCore 0:
  11.4 88.2 all-gather.7
  101.7 55.9 all-gather.5
  161.6 80.8 all-gather.9
  324.6 89.3 all-gather.11
  417.8 80.4 all-gather.13
  501.1 73.0 all-reduce.2
where the time goes:
time: 588 us; the launch traced here: 584 us
  waiting for transfers between devices  364 us (62%)
  blocking collectives  181 us (31%)
  matrix products  19.5 us (3%)
  between operations  14.3 us (2%)
    all_gather x1, waiting for transfers between devices, per_device(): lax.all_gather(panel_low, ('col', 'vox'), axis=1, tiled=True)  90.9 us
    all_gather x1, waiting for transfers between devices, per_device(): lax.all_gather(updated, ('col', 'vox'), axis=1, tiled=True)  89.5 us
    psum x1, waiting for transfers between devices, spread(): return lax.psum(block, axis)  69.6 us
    all_gather x1, blocking collectives, per_device(): lax.all_gather(panel_top, ('col', 'vox'), axis=1, tiled=True)  69.6 us
    all_gather x1, blocking collectives, per_device(): lax.all_gather(own_top.astype(jnp.bfloat16), ('col', 'vox'), axis=1, tile...  67.5 us
    all_gather x1, waiting for transfers between devices, per_device(): whole_inverses = lax.all_gather(inverses, 'row', axis=1, tiled=True)  58 us
    all_gather x1, waiting for transfers between devices, per_device(): lax.all_gather(own_next.astype(jnp.bfloat16), ('col', 'vox'), axis=1, til...  54.5 us
    psum x1, blocking collectives, spread(): return lax.psum(block, axis)  23.2 us
  transfers between devices with their start and end apart: 6, of which 5 were waited for; matrix products, arithmetic and copies ran while one was open for 2% of the time, Pallas kernels for 0%

commit v1 on v0

v1 whole, which is shorter than its diff:
```python
import jax
import jax.numpy as jnp
import numpy as np
from jax import lax
from jax.sharding import Mesh
from jax.sharding import PartitionSpec as P


def contract(left, right, dims):
    return lax.dot_general(left, right, (dims, ((), ())), preferred_element_type=jnp.float32)


def gather_small(block, axis, size):
    out = lax.all_to_all(jnp.tile(block, (size, 1)), axis, 0, 0, tiled=True)
    return out.reshape((size,) + block.shape)


def per_device(sizes, panel_top, panel_low, panel_next, gram_rest, inverses, right_top, right_low):
    rows, ys, cores, voxes = sizes
    axes = ("row", "y", "core", "vox")
    order = np.arange(rows * ys * cores * voxes).reshape(sizes)
    swap = list(zip(order.ravel().tolist(), order.transpose(1, 0, 2, 3).ravel().tolist()))
    y = lax.axis_index("y")
    core = lax.axis_index("core")
    vox = lax.axis_index("vox")
    width = panel_low.shape[1]
    rest_cols = gram_rest.shape[1]
    bf16 = jnp.bfloat16

    whole = lax.all_gather(inverses, "row", axis=1, tiled=True)
    top = gather_small(panel_top.T, "row", rows).transpose(1, 0, 2).reshape(width, -1)
    panels = jnp.stack([top, panel_low.T, panel_next.T])
    panels = lax.all_gather(panels, ("y", "core", "vox"), axis=1, tiled=True)

    low = panels[0:2].transpose(1, 0, 2).reshape(panels.shape[1], -1)
    first = contract(whole[0], low, ((1,), (0,))).astype(bf16)
    first_top, first_low = first[:, : panels.shape[2]], first[:, panels.shape[2] :]
    updated = (
        panels[2].astype(jnp.float32) - contract(first_top, first_low, ((0,), (0,)))
    ).astype(bf16)
    second_low = contract(whole[1], updated, ((1,), (0,))).astype(bf16)

    start = (core * voxes + vox) * rest_cols
    first_rows = lax.ppermute(lax.dynamic_slice_in_dim(first_low, start, rest_cols, 1), axes, swap)
    second_rows = lax.ppermute(lax.dynamic_slice_in_dim(second_low, start, rest_cols, 1), axes, swap)

    first_solve = contract(whole[0], right_top[0], ((1,), (0,))).astype(bf16)
    top_new = (
        right_top[1].astype(jnp.float32) - contract(first_top, first_solve, ((0,), (0,)))
    ).astype(bf16)
    second_solve = contract(whole[1], top_new, ((1,), (0,))).astype(bf16)

    residual = (
        right_low.astype(jnp.float32)
        - contract(first_low, first_solve, ((0,), (0,)))
        - contract(second_low, second_solve, ((0,), (0,)))
    )
    trailing = (
        gram_rest.astype(jnp.float32)
        - contract(first_low, first_rows, ((0,), (0,)))
        - contract(second_low, second_rows, ((0,), (0,)))
    )
    own = ((y * cores + core) * voxes + vox) * width
    factor = jnp.stack(
        [
            lax.dynamic_slice_in_dim(first_low, own, width, 0).T,
            lax.dynamic_slice_in_dim(second_low, own, width, 0).T,
        ]
    )
    solved = jnp.stack([first_solve, second_solve])
    return (factor, solved, trailing, residual)


def solution(mesh):
    cores = 2
    sizes = (mesh.shape["row"], mesh.shape["col"] // cores, cores, mesh.shape["vox"])
    split = Mesh(mesh.devices.reshape(sizes), ("row", "y", "core", "vox"))
    cols = ("y", "core", "vox")
    in_specs = (
        P("row", cols),
        P("row", cols),
        P("row", cols),
        P("row", cols),
        P(None, "row", None),
        P(None, None, cols),
        P("row", cols),
    )
    out_specs = (
        P(None, "row", cols),
        P(None, None, cols),
        P("row", cols),
        P("row", cols),
    )

    def body(*args):
        return per_device(sizes, *args)

    return jax.shard_map(body, mesh=split, in_specs=in_specs, out_specs=out_specs, check_vma=False)
```

time: 588 us -> 261 us (0.44)
  the two profiles are of different devices: /device:TPU:1 before, /device:TPU:16 now
where the time goes in v1:
time: 261 us; the launch traced here: 260 us
  waiting for transfers between devices  168 us (64%)
  matrix products  29.4 us (11%)
  blocking collectives  18.1 us (7%)
  local copies, waits for them, and re-layouts  17.6 us (7%)
  between operations  14.1 us (5%)
  starting transfers between devices  8.8 us (3%)
  other arithmetic  3.86 us (1%)
    all_gather x1, waiting for transfers between devices, per_device(): panels = lax.all_gather(panels, ('y', 'core', 'vox'), axis=1, tiled=True)  85.2 us
    all_gather x1, waiting for transfers between devices, per_device(): whole = lax.all_gather(inverses, 'row', axis=1, tiled=True)  44.6 us
    ppermute x1, waiting for transfers between devices, per_device(): lax.ppermute(lax.dynamic_slice_in_dim(second_low, start, rest_cols, 1), a...  33.1 us
    dot_general x8, matrix products, contract(): lax.dot_general(left, right, (dims, ((), ())), preferred_element_type=jnp...  29.4 us
    all_to_all x1, blocking collectives, gather_small(): out = lax.all_to_all(jnp.tile(block, (size, 1)), axis, 0, 0, tiled=True)  18.1 us
    unnamed x9, local copies, waits for them, and re-layouts  8.24 us
    ppermute x1, starting transfers between devices, per_device(): lax.ppermute(lax.dynamic_slice_in_dim(second_low, start, rest_cols, 1), a...  5.48 us
  transfers between devices with their start and end apart: 4, of which 4 were waited for; matrix products, arithmetic and copies ran while one was open for 6% of the time, Pallas kernels for 0%

profile of v1, /device:TPU:16, one launch (start us, length us, event | category | flops | bytes accessed | tf_op | source)
XLA Modules:
  0.0 259.9 jit_solution(18153763955404550325)
XLA Ops:
  7.2 0.0 all-gather.5.cloned.1.call-start
  7.2 0.7 all-gather.5.cloned.1.call-update
  7.9 0.0 all-gather.3.cloned.1.call-start
  7.9 0.7 tile.2
  8.6 18.1 %all_to_all.6 = bf16[8,16,128]{2,1,0:T(8,128)(2,1)S(1)} all-to-all(bf16[8,16,128]{2,1,0:T(8,128)(2,1)S(1)} %tile.2), channel_id=1, replica_groups=mesh['row'=8,'y'=8,'core'=2,'vox'=4] {'row'}, dimensions={0} | all-to-all | bytes 65536 | tf_op jit(solution)/shard_map/all_to_all | solution.py:14
  26.8 1.4 pad_maximum_fusion.1
  28.2 0.0 all-gather.3.cloned.1.call-update
  28.3 44.6 %all-gather.5.cloned.1.call-done = bf16[2,1024,1024]{2,1,0:T(8,128)(2,1)} async-done(((bf16[2,128,1024]{2,1,0:T(8,128)(2,1)}), bf16[2,1024,1024]{2,1,0:T(8,128)(2,1)}) %all-gather.5.cloned.1.call-update) | async-done | bytes 4194320 | tf_op jit(solution)/shard_map/all_gather | solution.py:30
  72.9 2.3 fusion.17
  75.2 0.0 copy-start.2
  75.2 85.2 %all-gather.3.cloned.1.call-done = bf16[3,1024,1024]{2,1,0:T(8,128)(2,1)} async-done(((bf16[3,16,1024]{2,1,0:T(8,128)(2,1)}), bf16[3,1024,1024]{2,1,0:T(8,128)(2,1)}) %all-gather.3.cloned.1.call-update) | async-done | bytes 6291472 | tf_op jit(solution)/shard_map/all_gather | solution.py:33
  160.4 4.7 %slice.34 = bf16[2,1024,1024]{2,1,0:T(8,128)(2,1)} slice(bf16[3,1024,1024]{2,1,0:T(8,128)(2,1)} %all-gather.3.cloned.1.call-done), slice={[0:2], [0:1024], [0:1024]} | slice | bytes 8388608 | tf_op jit(solution)/shard_map/slice | solution.py:35
  165.1 6.2 %copy.22 = bf16[2,1024,1024]{1,2,0:T(8,128)(2,1)} copy(bf16[2,1024,1024]{2,1,0:T(8,128)(2,1)} %slice.34) | data formatting | bytes 8388608
  171.3 7.4 %convert_bitcast_fusion = bf16[1024,2048]{1,0:T(8,128)(2,1)S(1)} fusion(bf16[1024,2048]{0,1:T(8,128)(2,1)} %bitcast.62, bf16[2,1024,1024]{2,1,0:T(8,128)(2,1)} %all-gather.5.cloned.1.call-done), kind=kOutput, calls=%fused_computation.2 | convolution fusion | flops 4297064448 | bytes 10485760 | tf_op jit(solution)/shard_map/dot_general | solution.py:10
  178.7 0.0 copy-start
  178.7 2.0 copy-done
  180.7 1.5 slice.36
  182.2 8.0 %fusion.3 = bf16[1024,1024]{0,1:T(8,128)(2,1)S(1)} fusion(bf16[3,1024,1024]{2,1,0:T(8,128)(2,1)} %all-gather.3.cloned.1.call-done, bf16[2,1024,1024]{2,1,0:T(8,128)(2,1)} %all-gather.5.cloned.1.call-done, bf16[1024,2048]{1,0:T(8,128)(2,1)} %copy-done), kind=kOutput, calls=%fused_computation.7 | convolution fusion | flops 4299161600 | bytes 10485760 | tf_op jit(solution)/shard_map/dot_general | solution.py:10
  190.2 0.8 dynamic-slice_bitcast_fusion.2
  191.0 0.8 dynamic-slice_bitcast_fusion
  191.8 1.0 constant_dynamic-slice_fusion
  192.8 5.5 %collective-permute-start.1 = (bf16[1024,128]{1,0:T(8,128)(2,1)}, bf16[1024,128]{1,0:T(8,128)(2,1)S(1)}, u32[]{:S(2)}, u32[]{:S(2)}) collective-permute-start(bf16[1024,128]{1,0:T(8,128)(2,1)} %dynamic-slice_bitcast_fusion), channel_id=1, source_target_pairs={{0,0},{1,1},{2,2},{3,3},{4,4},{5,5},{6,6},{7,7},{8,64},{9,65},{10,... | collective-permute-start | bytes 786440 | tf_op jit(solution)/shard_map/ppermute | solution.py:45
  198.2 3.2 %collective-permute-start = (bf16[1024,128]{1,0:T(8,128)(2,1)S(1)}, bf16[1024,128]{1,0:T(8,128)(2,1)}, u32[]{:S(2)}, u32[]{:S(2)}) collective-permute-start(bf16[1024,128]{1,0:T(8,128)(2,1)S(1)} %constant_dynamic-slice_fusion), channel_id=1, source_target_pairs={{0,0},{1,1},{2,2},{3,3},{4,4},{5,5},{6,6},{7,7},{8,64},{9,65},{10,... | collective-permute-start | bytes 786440 | tf_op jit(solution)/shard_map/ppermute | solution.py:44
  201.5 0.6 pad_maximum_fusion.2
  202.1 0.0 copy-done.2
  202.1 2.3 convolution_subtract_fusion.1
  204.5 4.5 %fusion.16 = bf16[128,1024]{0,1:T(8,128)(2,1)S(1)} fusion(bf16[2,1024,1024]{2,1,0:T(8,128)(2,1)} %all-gather.5.cloned.1.call-done, bf16[1024,128]{1,0:T(8,128)(2,1)} %copy-done.2, bf16[1024,2048]{1,0:T(8,128)(2,1)} %copy-done, bf16[2,1024,128]{2,1,0:T(8,128)(2,1)} %param.12), kind=kOutput, calls=%fused_computation.19 | convolution fusion | flops 537395200 | bytes 4980736 | tf_op jit(solution)/shard_map/dot_general | solution.py:10
  209.0 1.8 pad_maximum_fusion
  210.8 0.0 copy-start.1
  210.8 0.0 copy-start.3
  210.8 1.5 convolution_subtract_fusion
  212.3 33.1 %collective-permute-done.1 = bf16[1024,128]{1,0:T(8,128)(2,1)S(1)} collective-permute-done((bf16[1024,128]{1,0:T(8,128)(2,1)}, bf16[1024,128]{1,0:T(8,128)(2,1)S(1)}, u32[]{:S(2)}, u32[]{:S(2)}) %collective-permute-start.1) | collective-permute-done | bytes 262176 | tf_op jit(solution)/shard_map/ppermute | solution.py:45
  245.4 0.7 fusion.36
  246.2 4.4 %collective-permute-done = bf16[1024,128]{1,0:T(8,128)(2,1)} collective-permute-done((bf16[1024,128]{1,0:T(8,128)(2,1)S(1)}, bf16[1024,128]{1,0:T(8,128)(2,1)}, u32[]{:S(2)}, u32[]{:S(2)}) %collective-permute-start) | collective-permute-done | bytes 262176 | tf_op jit(solution)/shard_map/ppermute | solution.py:44
  250.6 0.0 copy-done.1
  250.6 0.0 copy-done.3
  250.6 2.5 fusion.15
  (3 shorter events, 0.0 us)
Async XLA Ops:
  7.2 65.7 %all-gather.5.cloned.1.call-start = ((), (), s32[]{:S(2)}) async-start(), calls=%async_computation.2 | async-start | bytes 4718592 | tf_op jit(solution)/shard_map/all_gather | solution.py:30
  7.9 152.5 %all-gather.3.cloned.1.call-start = ((), (), s32[]{:S(2)}) async-start(), calls=%async_computation.1 | async-start | bytes 6389760 | tf_op jit(solution)/shard_map/all_gather | solution.py:33
  75.2 127.0 %copy-start.2 = (bf16[1024,128]{1,0:T(8,128)(2,1)}, bf16[1024,128]{1,0:T(8,128)(2,1)S(1)}, u32[]{:S(2)}) copy-start(bf16[1024,128]{1,0:T(8,128)(2,1)S(1)} %fusion.17) | copy-start | bytes 786436
  178.7 2.1 copy-start
  192.8 52.7 %collective-permute-start.1 = (bf16[1024,128]{1,0:T(8,128)(2,1)}, bf16[1024,128]{1,0:T(8,128)(2,1)S(1)}, u32[]{:S(2)}, u32[]{:S(2)}) collective-permute-start(bf16[1024,128]{1,0:T(8,128)(2,1)} %dynamic-slice_bitcast_fusion), channel_id=1, source_target_pairs={{0,0},{1,1},{2,2},{3,3},{4,4},{5,5},{6,6},{7,7},{8,64},{9,65},{10,... | collective-permute-start | bytes 786440 | tf_op jit(solution)/shard_map/ppermute | solution.py:45
  198.2 52.3 %collective-permute-start = (bf16[1024,128]{1,0:T(8,128)(2,1)S(1)}, bf16[1024,128]{1,0:T(8,128)(2,1)}, u32[]{:S(2)}, u32[]{:S(2)}) collective-permute-start(bf16[1024,128]{1,0:T(8,128)(2,1)S(1)} %constant_dynamic-slice_fusion), channel_id=1, source_target_pairs={{0,0},{1,1},{2,2},{3,3},{4,4},{5,5},{6,6},{7,7},{8,64},{9,65},{10,... | collective-permute-start | bytes 786440 | tf_op jit(solution)/shard_map/ppermute | solution.py:44
  210.8 39.7 %copy-start.1 = (bf16[1024,2048]{1,0:T(8,128)(2,1)S(1)}, bf16[1024,2048]{1,0:T(8,128)(2,1)}, u32[]{:S(2)}) copy-start(bf16[1024,2048]{1,0:T(8,128)(2,1)} %copy-done) | copy-start | bytes 12582916
  210.8 39.7 %copy-start.3 = (bf16[1024,128]{1,0:T(8,128)(2,1)S(1)}, bf16[1024,128]{1,0:T(8,128)(2,1)}, u32[]{:S(2)}) copy-start(bf16[1024,128]{1,0:T(8,128)(2,1)} %param.10) | copy-start | bytes 786436
Sparse Core Ops, SparseCore 0:
  10.1 62.7 all-gather.4
  76.8 83.5 all-gather.2

commit v2 on v1

v2 whole, which is shorter than its diff:
```python
import functools

import jax
import jax.numpy as jnp
import numpy as np
from jax import lax
from jax.experimental import pallas as pl
from jax.experimental.pallas import tpu as pltpu
from jax.sharding import Mesh
from jax.sharding import PartitionSpec as P

TILE = 256


def factor_kernel(
    at_ref, inv_own, inv_other, panel_own, panel_other, side_one, side_two, gram, right,
    factor, solved, trailing, residual,
    inv, panels, side, top, first, updated, second, sems,
):
    z, core, own = at_ref[0], at_ref[1], at_ref[2]
    blocks = inv_own.shape[0]
    size = first.shape[0]
    f32, bf16 = jnp.float32, jnp.bfloat16

    inv_copies = []
    for i in range(blocks):
        spot = lax.rem(z + (blocks - i), blocks)
        for side_of, ref, half in ((0, inv_own, core), (1, inv_other, 1 - core)):
            inv_copies.append(
                pltpu.make_async_copy(ref.at[i], inv.at[half, spot], sems.at[2 * i + side_of])
            )
    panel_copies = []
    for p in range(panels.shape[0]):
        for side_of, ref, half in ((0, panel_own, core), (1, panel_other, 1 - core)):
            panel_copies.append(
                pltpu.make_async_copy(
                    ref.at[:, :, p],
                    panels.at[p, :, half],
                    sems.at[2 * blocks + 2 * p + side_of],
                )
            )
    side_copies = [
        pltpu.make_async_copy(side_one, side.at[0], sems.at[2 * blocks + 6]),
        pltpu.make_async_copy(side_two, side.at[1], sems.at[2 * blocks + 7]),
    ]
    for copy in inv_copies + panel_copies[:2] + panel_copies[2:4] + side_copies + panel_copies[4:]:
        copy.start()
    for copy in inv_copies:
        copy.wait()

    def inverse(k, i):
        rows = inv[k, 2 * i : 2 * i + 2].reshape(TILE, size)
        return rows[:, : (i + 1) * TILE]

    def lower(k, load, store):
        for i in range(size // TILE):
            store(i, jnp.dot(inverse(k, i), load((i + 1) * TILE), preferred_element_type=f32))

    def at(t):
        return pl.ds(pl.multiple_of(t * TILE, TILE), TILE)

    flat = panels.reshape(3, size, size)

    for copy in panel_copies[:2]:
        copy.wait()

    @pl.loop(0, size // TILE)
    def _(t):
        def store(i, x):
            top[at(t), i * TILE : (i + 1) * TILE] = x.astype(bf16).T

        lower(0, lambda n: flat[0, :n, at(t)], store)

    for copy in panel_copies[2:4] + side_copies:
        copy.wait()

    @pl.loop(0, size // TILE)
    def _(t):
        def store(i, x):
            first[i * TILE : (i + 1) * TILE, at(t)] = x.astype(bf16)

        lower(0, lambda n: flat[1, :n, at(t)], store)

    def store_side_one(i, x):
        first[i * TILE : (i + 1) * TILE, size:] = x.astype(bf16)

    lower(0, lambda n: side[0, :n, :], store_side_one)
    solved[0] = first[:, size + TILE // 2 :]

    for copy in panel_copies[4:]:
        copy.wait()

    def subtract(minuend, cols):
        for i in range(size // TILE):
            rows = slice(i * TILE, (i + 1) * TILE)
            change = jnp.dot(top[rows, :], first[:, cols], preferred_element_type=f32)
            updated[rows, cols] = (minuend(rows).astype(f32) - change).astype(bf16)

    @pl.loop(0, size // TILE)
    def _(t):
        subtract(lambda rows: flat[2, rows, at(t)], at(t))

        def store(i, x):
            second[i * TILE : (i + 1) * TILE, at(t)] = x.astype(bf16)

        lower(1, lambda n: updated[:n, at(t)], store)

    subtract(lambda rows: side[1, rows, :], slice(size, size + TILE))

    def store_side_two(i, x):
        second[i * TILE : (i + 1) * TILE, size:] = x.astype(bf16)

    lower(1, lambda n: updated[:n, size:], store_side_two)
    solved[1] = second[:, size + TILE // 2 :]

    rows = pl.ds(pl.multiple_of(own, 16), factor.shape[1])
    factor[0] = first[rows, :size]
    factor[1] = second[rows, :size]

    one = first[:, size:].T
    two = second[:, size:].T

    @pl.loop(0, size // TILE)
    def _(t):
        change = jnp.dot(one, first[:, at(t)], preferred_element_type=f32)
        change += jnp.dot(two, second[:, at(t)], preferred_element_type=f32)
        change = change.T
        trailing[at(t), :] = gram[at(t), :].astype(f32) - change[:, : TILE // 2]
        residual[at(t), :] = right[at(t), :].astype(f32) - change[:, TILE // 2 :]


def gather_small(block, axis, size):
    flat = block.reshape(1, -1, block.shape[-1])
    out = lax.all_to_all(jnp.tile(flat, (size, 1, 1)), axis, 0, 0, tiled=True)
    return out.reshape((size,) + block.shape)


def shift(block, axis, size, by):
    return lax.ppermute(block, axis, [(i, (i + by) % size) for i in range(size)])


def per_device(sizes, panel_top, panel_low, panel_next, gram_rest, inverses, right_top, right_low):
    rows, ys, cores, voxes = sizes
    axes = ("row", "y", "core", "vox")
    order = np.arange(rows * ys * cores * voxes).reshape(sizes)
    swap = list(zip(order.ravel().tolist(), order.transpose(1, 0, 2, 3).ravel().tolist()))
    z, y = lax.axis_index("row"), lax.axis_index("y")
    core, vox = lax.axis_index("core"), lax.axis_index("vox")
    size, width = inverses.shape[2], panel_low.shape[1]
    cols = gram_rest.shape[1]
    bf16 = jnp.bfloat16
    other = [(0, 1), (1, 0)]

    low, following = panel_low.T, panel_next.T
    pair = jnp.stack([low, following])
    swapped = lax.ppermute(pair, axes, swap)

    top = gather_small(panel_top.T, "row", rows).transpose(1, 0, 2).reshape(width, -1)
    panels = gather_small(jnp.stack([top, low, following]), "vox", voxes)
    panels, swapped = lax.optimization_barrier((panels, swapped))
    panel_own = lax.all_gather(panels, "y", axis=0)

    mine = lax.dynamic_index_in_dim(inverses, core, 0, False)
    blocks = swapped.reshape(2, width, cores * voxes, cols).transpose(2, 0, 1, 3)
    up, down = shift(mine, "row", rows, 1), shift(mine, "row", rows, -1)
    blocks = lax.all_to_all(blocks, ("core", "vox"), 0, 0, tiled=True)
    pieces = {0: mine, 1: up, rows - 1: down}
    for k in range(2, rows // 2 + 1):
        if k == 2:
            up, down, blocks = lax.optimization_barrier((up, down, blocks))
        if k == 3:
            up, down, matching = lax.optimization_barrier((up, down, matching))
        pieces[k] = up = shift(up, "row", rows, 1)
        if k < rows - k:
            pieces[rows - k] = down = shift(down, "row", rows, -1)
        if k == 2:
            matching = gather_small(blocks, "row", rows)
    inv_own = jnp.stack([pieces[k] for k in range(rows)])
    inv_other = lax.ppermute(inv_own, "core", other)
    matching = jnp.moveaxis(matching, 2, 0)
    matching = matching.reshape(2, size, cols)
    sides = [jnp.concatenate([matching[k], right_top[k]], axis=1) for k in range(2)]

    panel_own, inv_other, sides = lax.optimization_barrier((panel_own, inv_other, sides))
    panel_other = lax.ppermute(panel_own, "core", other)

    own = ((y * cores + core) * voxes + vox) * width
    where = jnp.stack([z, core, own]).astype(jnp.int32)
    height = panel_low.shape[0]
    any_space = pl.BlockSpec(memory_space=pl.ANY)
    local = pl.BlockSpec(memory_space=pltpu.VMEM)
    vmem = pltpu.VMEM
    flops = 2 * size * size * (2 * size + TILE + 2 * (size + TILE) + 2 * TILE)
    factor, solved, trailing, residual = pl.pallas_call(
        factor_kernel,
        out_shape=(
            jax.ShapeDtypeStruct((2, width, height), bf16),
            jax.ShapeDtypeStruct((2, size, cols), bf16),
            jax.ShapeDtypeStruct((height, cols), jnp.float32),
            jax.ShapeDtypeStruct((height, cols), jnp.float32),
        ),
        in_specs=[pl.BlockSpec(memory_space=pltpu.SMEM)] + [any_space] * 6 + [local] * 2,
        out_specs=(local,) * 4,
        scratch_shapes=[
            vmem((2, rows, size // rows, size), bf16),
            vmem((3, ys, cores, voxes, width, height), bf16),
            vmem((2, size, TILE), bf16),
            vmem((size, size), bf16),
            vmem((size, height + TILE), bf16),
            vmem((size, height + TILE), bf16),
            vmem((size, height + TILE), bf16),
            pltpu.SemaphoreType.DMA((2 * rows + 8,)),
        ],
        compiler_params=pltpu.CompilerParams(vmem_limit_bytes=48 * 1024 * 1024),
        cost_estimate=pl.CostEstimate(flops=flops, bytes_accessed=14 << 20, transcendentals=0),
        name="factor_and_update",
    )(where, inv_own, inv_other, panel_own, panel_other, sides[0], sides[1], gram_rest, right_low)
    return (factor.transpose(0, 2, 1), solved, trailing, residual)


def solution(mesh):
    cores = 2
    sizes = (mesh.shape["row"], mesh.shape["col"] // cores, cores, mesh.shape["vox"])
    split = Mesh(mesh.devices.reshape(sizes), ("row", "y", "core", "vox"))
    cols = ("y", "core", "vox")
    in_specs = (
        P("row", cols),
        P("row", cols),
        P("row", cols),
        P("row", cols),
        P(None, "row", None),
        P(None, None, cols),
        P("row", cols),
    )
    out_specs = (
        P(None, "row", cols),
        P(None, None, cols),
        P("row", cols),
        P("row", cols),
    )
    return jax.shard_map(
        functools.partial(per_device, sizes),
        mesh=split,
        in_specs=in_specs,
        out_specs=out_specs,
        check_vma=False,
    )
```

time: 261 us -> 158 us (0.61)
  the two profiles are of different devices: /device:TPU:16 before, /device:TPU:1 now
where the time goes in v2:
time: 158 us; the launch traced here: 155 us
  starting transfers between devices  51.3 us (32%)
  waiting for transfers between devices  42.7 us (27%)
  blocking collectives  17.5 us (11%)
  Pallas kernels  16.3 us (10%)
  between operations  14.3 us (9%)
  local copies, waits for them, and re-layouts  11.6 us (7%)
  other arithmetic  1.76 us (1%)
    ppermute x7, waiting for transfers between devices, shift(): lax.ppermute(block, axis, [(i, (i + by) % size) for i in range(size)])  23.9 us
    ppermute x7, starting transfers between devices, shift(): lax.ppermute(block, axis, [(i, (i + by) % size) for i in range(size)])  22.5 us
    all_to_all x1, blocking collectives, gather_small(): out = lax.all_to_all(jnp.tile(flat, (size, 1, 1)), axis, 0, 0, tiled=True)  17.5 us
    pallas_call x1, Pallas kernels, per_device(): pl.pallas_call(factor_kernel, out_shape=(jax.ShapeDtypeStruct((2, width,...  16.3 us
    all_to_all x2, starting transfers between devices, gather_small(): out = lax.all_to_all(jnp.tile(flat, (size, 1, 1)), axis, 0, 0, tiled=True)  10.4 us
    all_to_all x1, starting transfers between devices, per_device(): blocks = lax.all_to_all(blocks, ('core', 'vox'), 0, 0, tiled=True)  10 us
    unnamed x25, local copies, waits for them, and re-layouts  8.37 us
    ppermute x1, waiting for transfers between devices, per_device(): panel_other = lax.ppermute(panel_own, 'core', other)  5.52 us
  transfers between devices with their start and end apart: 14, of which 8 were waited for; matrix products, arithmetic and copies ran while one was open for 4% of the time, Pallas kernels for 0%

profile of v2, /device:TPU:1, one launch (start us, length us, event | category | flops | bytes accessed | tf_op | source)
XLA Modules:
  0.0 155.5 jit_solution(7720631439603368298)
XLA Ops:
  7.2 0.7 tile.10
  7.9 17.5 %all_to_all.20 = bf16[8,16,128]{2,1,0:T(8,128)(2,1)S(1)} all-to-all(bf16[8,16,128]{2,1,0:T(8,128)(2,1)S(1)} %tile.10), channel_id=1, replica_groups=mesh['row'=8,'y'=8,'core'=2,'vox'=4] {'row'}, dimensions={0} | all-to-all | bytes 65536 | tf_op jit(solution)/shard_map/all_to_all | solution.py:134
  25.5 0.8 pad_maximum_fusion.2
  26.3 0.8 tile.24
  27.1 4.0 %all-to-all-start.1 = ((bf16[4,48,1024]{2,1,0:T(8,128)(2,1)}), bf16[4,48,1024]{2,1,0:T(8,128)(2,1)S(1)}, u32[]{:S(2)}, u32[]{:S(2)}) async-start(bf16[4,48,1024]{2,1,0:T(8,128)(2,1)} %tile.24), calls=%async_computation.1 | async-start | bytes 786432 | tf_op jit(solution)/shard_map/all_to_all | solution.py:134
  31.1 0.8 pad_maximum_fusion.3
  31.9 0.7 collective-permute-start.2
  32.5 0.0 collective-permute-done.2
  32.5 4.8 %all-to-all-done.1 = bf16[4,48,1024]{2,1,0:T(8,128)(2,1)S(1)} async-done(((bf16[4,48,1024]{2,1,0:T(8,128)(2,1)}), bf16[4,48,1024]{2,1,0:T(8,128)(2,1)S(1)}, u32[]{:S(2)}, u32[]{:S(2)}) %all-to-all-start.1) | async-done | bytes 393248 | tf_op jit(solution)/shard_map/all_to_all | solution.py:134
  37.3 0.7 copy-done.4
  38.1 0.0 all-gather.3.cloned.1.call-update
  38.1 0.1 dynamic-slice_bitcast_fusion
  38.2 5.6 %collective-permute-start.1 = (bf16[128,1024]{1,0:T(8,128)(2,1)S(1)}, bf16[128,1024]{1,0:T(8,128)(2,1)S(1)}, u32[]{:S(2)}, u32[]{:S(2)}) collective-permute-start(bf16[128,1024]{1,0:T(8,128)(2,1)S(1)} %get-tuple-element.40), channel_id=1, source_target_pairs={{0,448},{64,0},{128,64},{192,128},{256,192},{320,256},{384,320},{4... | collective-permute-start | bytes 786440 | tf_op jit(solution)/shard_map/ppermute | solution.py:139
  43.8 1.9 %collective-permute-start = (bf16[128,1024]{1,0:T(8,128)(2,1)S(1)}, bf16[128,1024]{1,0:T(8,128)(2,1)S(1)}, u32[]{:S(2)}, u32[]{:S(2)}) collective-permute-start(bf16[128,1024]{1,0:T(8,128)(2,1)S(1)} %get-tuple-element.40), channel_id=1, source_target_pairs={{0,64},{64,128},{128,192},{192,256},{256,320},{320,384},{384,448},... | collective-permute-start | bytes 786440 | tf_op jit(solution)/shard_map/ppermute | solution.py:139
  45.7 0.6 copy.14
  46.4 10.0 %all-to-all-start.2 = ((bf16[8,2,16,128]{3,2,1,0:T(8,128)(2,1)}), bf16[8,2,16,128]{3,2,1,0:T(8,128)(2,1)S(1)}, u32[]{:S(2)}, u32[]{:S(2)}) async-start(bf16[8,2,16,128]{3,2,1,0:T(8,128)(2,1)} %copy.14), calls=%async_computation.2 | async-start | bytes 131072 | tf_op jit(solution)/shard_map/all_to_all | solution.py:166
  56.4 0.0 collective-permute-done.1
  56.4 0.0 collective-permute-done
  56.4 0.0 copy-start.6
  56.4 4.9 %all-to-all-done.2 = bf16[8,2,16,128]{3,2,1,0:T(8,128)(2,1)S(1)} async-done(((bf16[8,2,16,128]{3,2,1,0:T(8,128)(2,1)}), bf16[8,2,16,128]{3,2,1,0:T(8,128)(2,1)S(1)}, u32[]{:S(2)}, u32[]{:S(2)}) %all-to-all-start.2) | async-done | bytes 65568 | tf_op jit(solution)/shard_map/all_to_all | solution.py:166
  61.4 0.9 tile.26
  62.2 6.4 %all-to-all-start.3 = ((bf16[8,256,128]{2,1,0:T(8,128)(2,1)}), bf16[8,256,128]{2,1,0:T(8,128)(2,1)S(1)}, u32[]{:S(2)}, u32[]{:S(2)}) async-start(bf16[8,256,128]{2,1,0:T(8,128)(2,1)} %tile.26), calls=%async_computation.3 | async-start | bytes 1048576 | tf_op jit(solution)/shard_map/all_to_all | solution.py:134
  68.7 3.5 %collective-permute-start.3 = (bf16[128,1024]{1,0:T(8,128)(2,1)}, bf16[128,1024]{1,0:T(8,128)(2,1)S(1)}, u32[]{:S(2)}, u32[]{:S(2)}) collective-permute-start(bf16[128,1024]{1,0:T(8,128)(2,1)} %copy-done.6), channel_id=1, source_target_pairs={{0,64},{64,128},{128,192},{192,256},{256,320},{320,384},{384,448},... | collective-permute-start | bytes 786440 | tf_op jit(solution)/shard_map/ppermute | solution.py:139
  72.2 3.1 %collective-permute-start.4 = (bf16[128,1024]{1,0:T(8,128)(2,1)S(1)}, bf16[128,1024]{1,0:T(8,128)(2,1)}, u32[]{:S(2)}, u32[]{:S(2)}) collective-permute-start(bf16[128,1024]{1,0:T(8,128)(2,1)S(1)} %collective-permute-done.1), channel_id=1, source_target_pairs={{0,448},{64,0},{128,64},{192,128},{256,192},{320,256},{384,320},{4... | collective-permute-start | bytes 786440 | tf_op jit(solution)/shard_map/ppermute | solution.py:139
  75.3 13.4 %collective-permute-done.3 = bf16[128,1024]{1,0:T(8,128)(2,1)S(1)} collective-permute-done((bf16[128,1024]{1,0:T(8,128)(2,1)}, bf16[128,1024]{1,0:T(8,128)(2,1)S(1)}, u32[]{:S(2)}, u32[]{:S(2)}) %collective-permute-start.3) | collective-permute-done | bytes 262176 | tf_op jit(solution)/shard_map/ppermute | solution.py:139
  88.7 0.7 copy-done.7
  89.4 0.0 collective-permute-done.4
  89.4 0.0 all-to-all-done.3
  89.4 1.9 %collective-permute-start.5 = (bf16[128,1024]{1,0:T(8,128)(2,1)}, bf16[128,1024]{1,0:T(8,128)(2,1)S(1)}, u32[]{:S(2)}, u32[]{:S(2)}) collective-permute-start(bf16[128,1024]{1,0:T(8,128)(2,1)} %copy-done.7), channel_id=1, source_target_pairs={{0,64},{64,128},{128,192},{192,256},{256,320},{320,384},{384,448},... | collective-permute-start | bytes 786440 | tf_op jit(solution)/shard_map/ppermute | solution.py:139
  91.4 1.0 bitcast_dynamic-update-slice_fusion.6
  92.3 6.9 %collective-permute-done.5 = bf16[128,1024]{1,0:T(8,128)(2,1)S(1)} collective-permute-done((bf16[128,1024]{1,0:T(8,128)(2,1)}, bf16[128,1024]{1,0:T(8,128)(2,1)S(1)}, u32[]{:S(2)}, u32[]{:S(2)}) %collective-permute-start.5) | collective-permute-done | bytes 262176 | tf_op jit(solution)/shard_map/ppermute | solution.py:139
  99.2 1.9 %collective-permute-start.6 = (bf16[128,1024]{1,0:T(8,128)(2,1)S(1)}, bf16[128,1024]{1,0:T(8,128)(2,1)S(1)}, u32[]{:S(2)}, u32[]{:S(2)}) collective-permute-start(bf16[128,1024]{1,0:T(8,128)(2,1)S(1)} %collective-permute-done.5), channel_id=1, source_target_pairs={{0,64},{64,128},{128,192},{192,256},{256,320},{320,384},{384,448},... | collective-permute-start | bytes 786440 | tf_op jit(solution)/shard_map/ppermute | solution.py:139
  101.2 1.0 bitcast_dynamic-update-slice_fusion.5
  102.1 4.6 %collective-permute-start.7 = (bf16[128,1024]{1,0:T(8,128)(2,1)}, bf16[128,1024]{1,0:T(8,128)(2,1)S(1)}, u32[]{:S(2)}, u32[]{:S(2)}) collective-permute-start(bf16[128,1024]{1,0:T(8,128)(2,1)} %collective-permute-done.4), channel_id=1, source_target_pairs={{0,448},{64,0},{128,64},{192,128},{256,192},{320,256},{384,320},{4... | collective-permute-start | bytes 786440 | tf_op jit(solution)/shard_map/ppermute | solution.py:139
  106.7 1.2 collective-permute-done.6
  107.9 2.4 %collective-permute-done.7 = bf16[128,1024]{1,0:T(8,128)(2,1)S(1)} collective-permute-done((bf16[128,1024]{1,0:T(8,128)(2,1)}, bf16[128,1024]{1,0:T(8,128)(2,1)S(1)}, u32[]{:S(2)}, u32[]{:S(2)}) %collective-permute-start.7) | collective-permute-done | bytes 262176 | tf_op jit(solution)/shard_map/ppermute | solution.py:139
  110.3 1.0 bitcast_dynamic-update-slice_fusion.1
  111.3 0.0 copy-start.2
  111.4 5.4 %collective-permute-start.8 = (bf16[8,128,1024]{2,1,0:T(8,128)(2,1)S(1)}, bf16[8,128,1024]{2,1,0:T(8,128)(2,1)S(1)}, u32[]{:S(2)}, u32[]{:S(2)}) collective-permute-start(bf16[8,128,1024]{2,1,0:T(8,128)(2,1)S(1)} %bitcast_dynamic-update-slice_fusion.inv_own), channel_id=1, source_target_pairs={{0,4},{4,0},{1,5},{5,1},{2,6},{6,2},{3,7},{7,3},{8,12},{12,8},{9,1... | collective-permute-start | bytes 6291464 | tf_op jit(solution)/shard_map/ppermute | solution.py:179
  116.9 0.1 pad_maximum_fusion
  117.0 3.5 %collective-permute-done.8.inv_other = bf16[8,128,1024]{2,1,0:T(8,128)(2,1)S(1)} collective-permute-done((bf16[8,128,1024]{2,1,0:T(8,128)(2,1)S(1)}, bf16[8,128,1024]{2,1,0:T(8,128)(2,1)S(1)}, u32[]{:S(2)}, u32[]{:S(2)}) %collective-permute-start.8) | collective-permute-done | bytes 2097184 | tf_op jit(solution)/shard_map/ppermute | solution.py:179
  120.5 1.4 copy-done
  121.9 2.3 %collective-permute-start.9 = (bf16[8,4,3,16,1024]{4,3,2,1,0:T(8,128)(2,1)}, bf16[8,4,3,16,1024]{4,3,2,1,0:T(8,128)(2,1)}, u32[]{:S(2)}, u32[]{:S(2)}) collective-permute-start(bf16[8,4,3,16,1024]{4,3,2,1,0:T(8,128)(2,1)} %bitcast.62), channel_id=1, source_target_pairs={{0,4},{4,0},{1,5},{5,1},{2,6},{6,2},{3,7},{7,3},{8,12},{12,8},{9,1... | collective-permute-start | bytes 9437192 | tf_op jit(solution)/shard_map/ppermute | solution.py:185
  124.2 0.1 pad_add_fusion.at_ref
  124.3 5.5 %collective-permute-done.9.panel_other = bf16[8,4,3,16,1024]{4,3,2,1,0:T(8,128)(2,1)} collective-permute-done((bf16[8,4,3,16,1024]{4,3,2,1,0:T(8,128)(2,1)}, bf16[8,4,3,16,1024]{4,3,2,1,0:T(8,128)(2,1)}, u32[]{:S(2)}, u32[]{:S(2)}) %collective-permute-start.9) | collective-permute-done | bytes 3145760 | tf_op jit(solution)/shard_map/ppermute | solution.py:185
  129.8 1.6 %copy-done.1 = bf16[8,128,1024]{2,1,0:T(8,128)(2,1)S(1)} copy-done((bf16[8,128,1024]{2,1,0:T(8,128)(2,1)S(1)}, bf16[8,128,1024]{2,1,0:T(8,128)(2,1)}, u32[]{:S(2)}) %copy-start.1) | copy-done | bytes 2097176
  131.4 0.9 copy-done.3
  132.3 16.3 %factor_and_update.1 = (bf16[2,16,1024]{2,1,0:T(8,128)(2,1)}, bf16[2,1024,128]{2,1,0:T(8,128)(2,1)}, f32[1024,128]{1,0:T(8,128)}, f32[1024,128]{1,0:T(8,128)}) custom-call(s32[3]{0:T(128)S(1)} %pad_add_fusion.at_ref, bf16[8,128,1024]{2,1,0:T(8,128)(2,1)S(1)} %bitcast_dynamic-update-slice_fusion.inv_own, bf16[8,128,1024]{2,1,0:T(8,128)(2,1)S(1)} %copy-done.1, ...), custom_call_target="tpu_custom_call" | custom-call | flops 11274289152 | bytes 14680064 | tf_op jit(solution)/shard_map/factor_and_update/pallas_call | solution.py:194
  (23 shorter events, 0.2 us)
Async XLA Ops:
  7.2 30.9 %copy-start.8 = (bf16[2,128,1024]{2,1,0:T(8,128)(2,1)S(1)}, bf16[2,128,1024]{2,1,0:T(8,128)(2,1)}, u32[]{:S(2)}) copy-start(bf16[2,128,1024]{2,1,0:T(8,128)(2,1)} %param.11) | copy-start | bytes 1572868
  27.1 10.2 %all-to-all-start.1 = ((bf16[4,48,1024]{2,1,0:T(8,128)(2,1)}), bf16[4,48,1024]{2,1,0:T(8,128)(2,1)S(1)}, u32[]{:S(2)}, u32[]{:S(2)}) async-start(bf16[4,48,1024]{2,1,0:T(8,128)(2,1)} %tile.24), calls=%async_computation.1 | async-start | bytes 786432 | tf_op jit(solution)/shard_map/all_to_all | solution.py:134
  31.1 90.8 %all-gather.3.cloned.1.call-start = ((), (), s32[]{:S(2)}) async-start(), calls=%async_computation.4 | async-start | bytes 3538944 | tf_op jit(solution)/shard_map/all_gather | solution.py:161
  31.9 0.7 collective-permute-start.2
  37.3 0.7 copy-start.4
  38.2 18.2 %collective-permute-start.1 = (bf16[128,1024]{1,0:T(8,128)(2,1)S(1)}, bf16[128,1024]{1,0:T(8,128)(2,1)S(1)}, u32[]{:S(2)}, u32[]{:S(2)}) collective-permute-start(bf16[128,1024]{1,0:T(8,128)(2,1)S(1)} %get-tuple-element.40), channel_id=1, source_target_pairs={{0,448},{64,0},{128,64},{192,128},{256,192},{320,256},{384,320},{4... | collective-permute-start | bytes 786440 | tf_op jit(solution)/shard_map/ppermute | solution.py:139
  43.8 12.6 %collective-permute-start = (bf16[128,1024]{1,0:T(8,128)(2,1)S(1)}, bf16[128,1024]{1,0:T(8,128)(2,1)S(1)}, u32[]{:S(2)}, u32[]{:S(2)}) collective-permute-start(bf16[128,1024]{1,0:T(8,128)(2,1)S(1)} %get-tuple-element.40), channel_id=1, source_target_pairs={{0,64},{64,128},{128,192},{192,256},{256,320},{320,384},{384,448},... | collective-permute-start | bytes 786440 | tf_op jit(solution)/shard_map/ppermute | solution.py:139
  46.4 15.0 %all-to-all-start.2 = ((bf16[8,2,16,128]{3,2,1,0:T(8,128)(2,1)}), bf16[8,2,16,128]{3,2,1,0:T(8,128)(2,1)S(1)}, u32[]{:S(2)}, u32[]{:S(2)}) async-start(bf16[8,2,16,128]{3,2,1,0:T(8,128)(2,1)} %copy.14), calls=%async_computation.2 | async-start | bytes 131072 | tf_op jit(solution)/shard_map/all_to_all | solution.py:166
  56.4 5.8 %copy-start.6 = (bf16[128,1024]{1,0:T(8,128)(2,1)}, bf16[128,1024]{1,0:T(8,128)(2,1)S(1)}, u32[]{:S(2)}) copy-start(bf16[128,1024]{1,0:T(8,128)(2,1)S(1)} %collective-permute-done) | copy-start | bytes 786436
  62.2 27.2 %all-to-all-start.3 = ((bf16[8,256,128]{2,1,0:T(8,128)(2,1)}), bf16[8,256,128]{2,1,0:T(8,128)(2,1)S(1)}, u32[]{:S(2)}, u32[]{:S(2)}) async-start(bf16[8,256,128]{2,1,0:T(8,128)(2,1)} %tile.26), calls=%async_computation.3 | async-start | bytes 1048576 | tf_op jit(solution)/shard_map/all_to_all | solution.py:134
  68.7 48.1 %copy-start.5 = (bf16[2,1024,128]{2,1,0:T(8,128)(2,1)S(1)}, bf16[2,1024,128]{2,1,0:T(8,128)(2,1)}, u32[]{:S(2)}) copy-start(bf16[2,1024,128]{2,1,0:T(8,128)(2,1)} %param.12) | copy-start | bytes 1572868
  68.7 20.1 %collective-permute-start.3 = (bf16[128,1024]{1,0:T(8,128)(2,1)}, bf16[128,1024]{1,0:T(8,128)(2,1)S(1)}, u32[]{:S(2)}, u32[]{:S(2)}) collective-permute-start(bf16[128,1024]{1,0:T(8,128)(2,1)} %copy-done.6), channel_id=1, source_target_pairs={{0,64},{64,128},{128,192},{192,256},{256,320},{320,384},{384,448},... | collective-permute-start | bytes 786440 | tf_op jit(solution)/shard_map/ppermute | solution.py:139
  72.2 17.3 %collective-permute-start.4 = (bf16[128,1024]{1,0:T(8,128)(2,1)S(1)}, bf16[128,1024]{1,0:T(8,128)(2,1)}, u32[]{:S(2)}, u32[]{:S(2)}) collective-permute-start(bf16[128,1024]{1,0:T(8,128)(2,1)S(1)} %collective-permute-done.1), channel_id=1, source_target_pairs={{0,448},{64,0},{128,64},{192,128},{256,192},{320,256},{384,320},{4... | collective-permute-start | bytes 786440 | tf_op jit(solution)/shard_map/ppermute | solution.py:139
  88.7 0.7 copy-start.7
  89.4 9.8 %collective-permute-start.5 = (bf16[128,1024]{1,0:T(8,128)(2,1)}, bf16[128,1024]{1,0:T(8,128)(2,1)S(1)}, u32[]{:S(2)}, u32[]{:S(2)}) collective-permute-start(bf16[128,1024]{1,0:T(8,128)(2,1)} %copy-done.7), channel_id=1, source_target_pairs={{0,64},{64,128},{128,192},{192,256},{256,320},{320,384},{384,448},... | collective-permute-start | bytes 786440 | tf_op jit(solution)/shard_map/ppermute | solution.py:139
  99.2 8.7 %collective-permute-start.6 = (bf16[128,1024]{1,0:T(8,128)(2,1)S(1)}, bf16[128,1024]{1,0:T(8,128)(2,1)S(1)}, u32[]{:S(2)}, u32[]{:S(2)}) collective-permute-start(bf16[128,1024]{1,0:T(8,128)(2,1)S(1)} %collective-permute-done.5), channel_id=1, source_target_pairs={{0,64},{64,128},{128,192},{192,256},{256,320},{320,384},{384,448},... | collective-permute-start | bytes 786440 | tf_op jit(solution)/shard_map/ppermute | solution.py:139
  102.1 8.2 %collective-permute-start.7 = (bf16[128,1024]{1,0:T(8,128)(2,1)}, bf16[128,1024]{1,0:T(8,128)(2,1)S(1)}, u32[]{:S(2)}, u32[]{:S(2)}) collective-permute-start(bf16[128,1024]{1,0:T(8,128)(2,1)} %collective-permute-done.4), channel_id=1, source_target_pairs={{0,448},{64,0},{128,64},{192,128},{256,192},{320,256},{384,320},{4... | collective-permute-start | bytes 786440 | tf_op jit(solution)/shard_map/ppermute | solution.py:139
  111.3 18.5 %copy-start.2 = (bf16[1024,128]{1,0:T(8,128)(2,1)S(1)}, bf16[1024,128]{1,0:T(8,128)(2,1)}, u32[]{:S(2)}) copy-start(bf16[1024,128]{1,0:T(8,128)(2,1)} %gram.1) | copy-start | bytes 786436
  111.4 9.2 %collective-permute-start.8 = (bf16[8,128,1024]{2,1,0:T(8,128)(2,1)S(1)}, bf16[8,128,1024]{2,1,0:T(8,128)(2,1)S(1)}, u32[]{:S(2)}, u32[]{:S(2)}) collective-permute-start(bf16[8,128,1024]{2,1,0:T(8,128)(2,1)S(1)} %bitcast_dynamic-update-slice_fusion.inv_own), channel_id=1, source_target_pairs={{0,4},{4,0},{1,5},{5,1},{2,6},{6,2},{3,7},{7,3},{8,12},{12,8},{9,1... | collective-permute-start | bytes 6291464 | tf_op jit(solution)/shard_map/ppermute | solution.py:179
  120.5 1.4 copy-start
  121.9 7.9 %collective-permute-start.9 = (bf16[8,4,3,16,1024]{4,3,2,1,0:T(8,128)(2,1)}, bf16[8,4,3,16,1024]{4,3,2,1,0:T(8,128)(2,1)}, u32[]{:S(2)}, u32[]{:S(2)}) collective-permute-start(bf16[8,4,3,16,1024]{4,3,2,1,0:T(8,128)(2,1)} %bitcast.62), channel_id=1, source_target_pairs={{0,4},{4,0},{1,5},{5,1},{2,6},{6,2},{3,7},{7,3},{8,12},{12,8},{9,1... | collective-permute-start | bytes 9437192 | tf_op jit(solution)/shard_map/ppermute | solution.py:185
  129.8 1.6 %copy-start.1 = (bf16[8,128,1024]{2,1,0:T(8,128)(2,1)S(1)}, bf16[8,128,1024]{2,1,0:T(8,128)(2,1)}, u32[]{:S(2)}) copy-start(bf16[8,128,1024]{2,1,0:T(8,128)(2,1)} %copy-done) | copy-start | bytes 6291460
  131.4 0.9 copy-start.3
Sparse Core Ops, SparseCore 0:
  38.2 54.7 all-gather.2

commit v3 on v2

v3 whole, which is shorter than its diff:
```python
import functools

import jax
import jax.numpy as jnp
import numpy as np
from jax import lax
from jax.experimental import pallas as pl
from jax.experimental.pallas import tpu as pltpu
from jax.sharding import Mesh
from jax.sharding import PartitionSpec as P

TILE = 256


def factor_kernel(ys, at_ref, whole, *refs):
    pieces, others, refs = refs[:ys], refs[ys : 2 * ys], refs[2 * ys :]
    side_one, side_two, gram, right, factor, solved, trailing, residual = refs[:8]
    inv, panels, side, minuend, top, first, updated, second, sems = refs[8:]
    y, core, own = at_ref[0], at_ref[1], at_ref[2]
    size = first.shape[0]
    f32, bf16 = jnp.float32, jnp.bfloat16

    inv_copies = [
        pltpu.make_async_copy(whole.at[0], inv.at[0], sems.at[0]),
        pltpu.make_async_copy(whole.at[1], inv.at[1], sems.at[1]),
    ]
    panel_copies = [[], [], []]
    for p in range(3):
        for k in range(ys):
            spot = lax.rem(y + (ys - k), ys)
            for ref, half in ((pieces[k], core), (others[k], 1 - core)):
                panel_copies[p].append(
                    pltpu.make_async_copy(
                        ref.at[:, p],
                        panels.at[p, spot, half],
                        sems.at[2 + 2 * ys * p + len(panel_copies[p])],
                    )
                )
    side_copies = [
        pltpu.make_async_copy(side_one, side.at[0], sems.at[2 + 6 * ys]),
        pltpu.make_async_copy(side_two, side.at[1], sems.at[3 + 6 * ys]),
    ]
    late_copies = [
        pltpu.make_async_copy(gram, minuend.at[0], sems.at[4 + 6 * ys]),
        pltpu.make_async_copy(right, minuend.at[1], sems.at[5 + 6 * ys]),
    ]
    for copy in inv_copies + panel_copies[0] + panel_copies[1] + side_copies + panel_copies[2] + late_copies:
        copy.start()
    for copy in inv_copies:
        copy.wait()

    def inverse(k, i):
        return inv[k, i * TILE : (i + 1) * TILE, : (i + 1) * TILE]

    def lower(k, load, store):
        for i in range(size // TILE):
            store(i, jnp.dot(inverse(k, i), load((i + 1) * TILE), preferred_element_type=f32))

    def at(t):
        return pl.ds(pl.multiple_of(t * TILE, TILE), TILE)

    flat = panels.reshape(3, size, size)

    for copy in panel_copies[0]:
        copy.wait()

    @pl.loop(0, size // TILE)
    def _(t):
        def store(i, x):
            top[at(t), i * TILE : (i + 1) * TILE] = x.astype(bf16).T

        lower(0, lambda n: flat[0, :n, at(t)], store)

    for copy in panel_copies[1] + side_copies:
        copy.wait()

    @pl.loop(0, size // TILE)
    def _(t):
        def store(i, x):
            first[i * TILE : (i + 1) * TILE, at(t)] = x.astype(bf16)

        lower(0, lambda n: flat[1, :n, at(t)], store)

    def store_side_one(i, x):
        first[i * TILE : (i + 1) * TILE, size:] = x.astype(bf16)

    lower(0, lambda n: side[0, :n, :], store_side_one)
    solved[0] = first[:, size + TILE // 2 :]

    for copy in panel_copies[2]:
        copy.wait()

    def subtract(load, cols):
        for i in range(size // TILE):
            rows = slice(i * TILE, (i + 1) * TILE)
            change = jnp.dot(top[rows, :], first[:, cols], preferred_element_type=f32)
            updated[rows, cols] = (load(rows).astype(f32) - change).astype(bf16)

    @pl.loop(0, size // TILE)
    def _(t):
        subtract(lambda rows: flat[2, rows, at(t)], at(t))

        def store(i, x):
            second[i * TILE : (i + 1) * TILE, at(t)] = x.astype(bf16)

        lower(1, lambda n: updated[:n, at(t)], store)

    subtract(lambda rows: side[1, rows, :], slice(size, size + TILE))

    def store_side_two(i, x):
        second[i * TILE : (i + 1) * TILE, size:] = x.astype(bf16)

    lower(1, lambda n: updated[:n, size:], store_side_two)
    solved[1] = second[:, size + TILE // 2 :]

    rows = pl.ds(pl.multiple_of(own, 16), factor.shape[1])
    factor[0] = first[rows, :size]
    factor[1] = second[rows, :size]

    for copy in late_copies:
        copy.wait()
    one = first[:, size:].T
    two = second[:, size:].T

    @pl.loop(0, size // TILE)
    def _(t):
        change = jnp.dot(one, first[:, at(t)], preferred_element_type=f32)
        change += jnp.dot(two, second[:, at(t)], preferred_element_type=f32)
        change = change.T
        trailing[at(t), :] = minuend[0, at(t), :].astype(f32) - change[:, : TILE // 2]
        residual[at(t), :] = minuend[1, at(t), :].astype(f32) - change[:, TILE // 2 :]


def gather_small(block, axis, size):
    flat = block.reshape(1, -1, block.shape[-1])
    out = lax.all_to_all(jnp.tile(flat, (size, 1, 1)), axis, 0, 0, tiled=True)
    return out.reshape((size,) + block.shape)


def shift(block, axis, size, by):
    return lax.ppermute(block, axis, [(i, (i + by) % size) for i in range(size)])


def per_device(sizes, panel_top, panel_low, panel_next, gram_rest, inverses, right_top, right_low):
    rows, ys, cores, voxes = sizes
    axes = ("row", "y", "core", "vox")
    order = np.arange(rows * ys * cores * voxes).reshape(sizes)
    swap = list(zip(order.ravel().tolist(), order.transpose(1, 0, 2, 3).ravel().tolist()))
    z, y = lax.axis_index("row"), lax.axis_index("y")
    core, vox = lax.axis_index("core"), lax.axis_index("vox")
    size, width = inverses.shape[2], panel_low.shape[1]
    cols = gram_rest.shape[1]
    bf16 = jnp.bfloat16
    other = [(0, 1), (1, 0)]

    whole = lax.all_gather(inverses, "row", axis=1, tiled=True)
    low, following = panel_low.T, panel_next.T
    pair = jnp.stack([low, following])
    swapped = lax.ppermute(pair, axes, swap)

    top = gather_small(panel_top.T, "row", rows).transpose(1, 0, 2).reshape(width, -1)
    top, swapped = lax.optimization_barrier((top, swapped))
    panels = gather_small(jnp.stack([top, low, following]), "vox", voxes)
    blocks = swapped.reshape(2, width, cores * voxes, cols).transpose(2, 0, 1, 3)

    up = down = panels
    pieces, others = {0: panels}, {}
    for k in range(1, ys // 2 + 1):
        if k == 2:
            up, down, blocks = lax.optimization_barrier((up, down, blocks))
        if k == 4:
            up, matching, whole = lax.optimization_barrier((up, matching, whole))
        if k == 1:
            blocks = lax.all_to_all(blocks, ("core", "vox"), 0, 0, tiled=True)
        if k == 2:
            matching = gather_small(blocks, "row", rows)
        pieces[k] = up = shift(up, "y", ys, 1)
        if k < ys - k:
            pieces[ys - k] = down = shift(down, "y", ys, -1)
    for k in range(ys):
        others[k] = lax.ppermute(pieces[k], "core", other)
    matching = jnp.moveaxis(matching, 2, 0)
    matching = matching.reshape(2, size, cols)
    sides = [jnp.concatenate([matching[k], right_top[k]], axis=1) for k in range(2)]
    pieces = [pieces[k] for k in range(ys)]
    others = [others[k] for k in range(ys)]

    own = ((y * cores + core) * voxes + vox) * width
    where = jnp.stack([y, core, own]).astype(jnp.int32)
    height = panel_low.shape[0]
    any_space = pl.BlockSpec(memory_space=pl.ANY)
    local = pl.BlockSpec(memory_space=pltpu.VMEM)
    vmem = pltpu.VMEM
    flops = 2 * size * size * (2 * size + TILE + 2 * (size + TILE) + 2 * TILE)
    factor, solved, trailing, residual = pl.pallas_call(
        functools.partial(factor_kernel, ys),
        out_shape=(
            jax.ShapeDtypeStruct((2, width, height), bf16),
            jax.ShapeDtypeStruct((2, size, cols), bf16),
            jax.ShapeDtypeStruct((height, cols), jnp.float32),
            jax.ShapeDtypeStruct((height, cols), jnp.float32),
        ),
        in_specs=[pl.BlockSpec(memory_space=pltpu.SMEM)] + [any_space] * (5 + 2 * ys),
        out_specs=(local,) * 4,
        scratch_shapes=[
            vmem((2, size, size), bf16),
            vmem((3, ys, cores, voxes, width, height), bf16),
            vmem((2, size, TILE), bf16),
            vmem((2, height, cols), bf16),
            vmem((size, size), bf16),
            vmem((size, height + TILE), bf16),
            vmem((size, height + TILE), bf16),
            vmem((size, height + TILE), bf16),
            pltpu.SemaphoreType.DMA((6 * ys + 6,)),
        ],
        compiler_params=pltpu.CompilerParams(vmem_limit_bytes=40 * 1024 * 1024),
        cost_estimate=pl.CostEstimate(flops=flops, bytes_accessed=14 << 20, transcendentals=0),
        name="factor_and_update",
    )(where, whole, *pieces, *others, *sides, gram_rest, right_low)
    return (factor.transpose(0, 2, 1), solved, trailing, residual)


def solution(mesh):
    cores = 2
    sizes = (mesh.shape["row"], mesh.shape["col"] // cores, cores, mesh.shape["vox"])
    split = Mesh(mesh.devices.reshape(sizes), ("row", "y", "core", "vox"))
    cols = ("y", "core", "vox")
    in_specs = (
        P("row", cols),
        P("row", cols),
        P("row", cols),
        P("row", cols),
        P(None, "row", None),
        P(None, None, cols),
        P("row", cols),
    )
    out_specs = (
        P(None, "row", cols),
        P(None, None, cols),
        P("row", cols),
        P("row", cols),
    )
    return jax.shard_map(
        functools.partial(per_device, sizes),
        mesh=split,
        in_specs=in_specs,
        out_specs=out_specs,
        check_vma=False,
    )
```

time: 158 us -> 143 us (0.905); the launches traced: 155 us -> 142 us
  waiting for transfers between devices: 42.7 us -> 14 us
  starting transfers between devices: 51.3 us -> 67.1 us
  local copies, waits for them, and re-layouts: 11.6 us -> 6.43 us
  blocking collectives: 17.5 us -> 21.2 us
    ppermute x7, waiting for transfers between devices: 23.9 us -> 7.66 us  [shift(): lax.ppermute(block, axis, [(i, (i + by) % size) for i in range(size)])]
    ppermute x2 -> x8, starting transfers between devices: 7.67 us -> 20.1 us  [per_device(): others[k] = lax.ppermute(pieces[k], 'core', other)]
    all_to_all x2, starting transfers between devices: 10.4 us -> 21.9 us  [gather_small(): out = lax.all_to_all(jnp.tile(flat, (size, 1, 1)), axis, 0, 0, tiled=True)]
    all_to_all x0 -> x1, blocking collectives: none -> 11.1 us  [per_device(): blocks = lax.all_to_all(blocks, ('core', 'vox'), 0, 0, tiled=True)]
    all_to_all x1 -> x0, starting transfers between devices: 10 us -> none  [per_device(): blocks = lax.all_to_all(blocks, ('core', 'vox'), 0, 0, tiled=True)]
    ppermute x2 -> x8, waiting for transfers between devices: 9.05 us -> 0.23 us  [per_device(): others[k] = lax.ppermute(pieces[k], 'core', other)]
    all_to_all x1, blocking collectives: 17.5 us -> 10.1 us  [gather_small(): out = lax.all_to_all(jnp.tile(flat, (size, 1, 1)), axis, 0, 0, tiled=True)]
    unnamed x25 -> x7, local copies, waits for them, and re-layouts: 8.37 us -> 1.92 us
  transfers between devices with their start and end apart: 14 -> 19, of which waited for: 8 -> 4; matrix products, arithmetic and copies ran while one was open for 4% -> 4% of each run, Pallas kernels for 0% -> 0%
where the time goes in v3:
time: 143 us; the launch traced here: 142 us
  starting transfers between devices  67.1 us (47%)
  blocking collectives  21.2 us (15%)
  Pallas kernels  17.4 us (12%)
  between operations  14.3 us (10%)
  waiting for transfers between devices  14 us (10%)
  local copies, waits for them, and re-layouts  6.43 us (4%)
  other arithmetic  1.77 us (1%)
    ppermute x7, starting transfers between devices, shift(): lax.ppermute(block, axis, [(i, (i + by) % size) for i in range(size)])  24.4 us
    all_to_all x2, starting transfers between devices, gather_small(): out = lax.all_to_all(jnp.tile(flat, (size, 1, 1)), axis, 0, 0, tiled=True)  21.9 us
    ppermute x8, starting transfers between devices, per_device(): others[k] = lax.ppermute(pieces[k], 'core', other)  20.1 us
    pallas_call x1, Pallas kernels, per_device(): pl.pallas_call(functools.partial(factor_kernel, ys), out_shape=(jax.Shape...  17.4 us
    all_to_all x1, blocking collectives, per_device(): blocks = lax.all_to_all(blocks, ('core', 'vox'), 0, 0, tiled=True)  11.1 us
    all_to_all x1, blocking collectives, gather_small(): out = lax.all_to_all(jnp.tile(flat, (size, 1, 1)), axis, 0, 0, tiled=True)  10.1 us
    ppermute x7, waiting for transfers between devices, shift(): lax.ppermute(block, axis, [(i, (i + by) % size) for i in range(size)])  7.66 us
    all_to_all x2, waiting for transfers between devices, gather_small(): out = lax.all_to_all(jnp.tile(flat, (size, 1, 1)), axis, 0, 0, tiled=True)  5.44 us
  transfers between devices with their start and end apart: 19, of which 4 were waited for; matrix products, arithmetic and copies ran while one was open for 4% of the time, Pallas kernels for 0%

profile of v3, /device:TPU:1, one launch (start us, length us, event | category | flops | bytes accessed | tf_op | source)
XLA Modules:
  0.0 142.3 jit_solution(14589907917201170544)
XLA Ops:
  7.2 0.0 all-gather.2.cloned.1.call-start
  7.2 0.7 all-gather.2.cloned.1.call-update
  7.9 1.3 tile.10
  9.2 10.9 %all-to-all-start = ((bf16[8,16,128]{2,1,0:T(8,128)(2,1)}), bf16[8,16,128]{2,1,0:T(8,128)(2,1)S(1)}, u32[]{:S(2)}, u32[]{:S(2)}) async-start(bf16[8,16,128]{2,1,0:T(8,128)(2,1)} %tile.10), calls=%async_computation | async-start | bytes 65536 | tf_op jit(solution)/shard_map/all_to_all | solution.py:136
  20.1 0.8 pad_maximum_fusion.3
  20.9 0.7 collective-permute-start
  21.5 5.4 %all-to-all-done = bf16[8,16,128]{2,1,0:T(8,128)(2,1)S(1)} async-done(((bf16[8,16,128]{2,1,0:T(8,128)(2,1)}), bf16[8,16,128]{2,1,0:T(8,128)(2,1)S(1)}, u32[]{:S(2)}, u32[]{:S(2)}) %all-to-all-start) | async-done | bytes 32800 | tf_op jit(solution)/shard_map/all_to_all | solution.py:136
  27.0 0.0 collective-permute-done
  27.0 0.8 pad_maximum_fusion.2
  27.8 10.1 %all_to_all.20 = bf16[4,48,1024]{2,1,0:T(8,128)(2,1)S(1)} all-to-all(bf16[4,48,1024]{2,1,0:T(8,128)(2,1)S(1)} %tile.24), channel_id=1, replica_groups=mesh['row'=8,'y'=8,'core'=2,'vox'=4] {'vox'}, dimensions={0} | all-to-all | bytes 786432 | tf_op jit(solution)/shard_map/all_to_all | solution.py:136
  37.9 7.3 %collective-permute-start.2 = (bf16[4,3,16,1024]{3,2,1,0:T(8,128)(2,1)S(1)}, bf16[4,3,16,1024]{3,2,1,0:T(8,128)(2,1)S(1)}, u32[]{:S(2)}, u32[]{:S(2)}) collective-permute-start(bf16[4,3,16,1024]{3,2,1,0:T(8,128)(2,1)S(1)} %bitcast.37), channel_id=1, source_target_pairs={{0,56},{8,0},{16,8},{24,16},{32,24},{40,32},{48,40},{56,48},{1,57}... | collective-permute-start | bytes 1179656 | tf_op jit(solution)/shard_map/ppermute | solution.py:141
  45.2 1.9 %collective-permute-start.1 = (bf16[4,3,16,1024]{3,2,1,0:T(8,128)(2,1)S(1)}, bf16[4,3,16,1024]{3,2,1,0:T(8,128)(2,1)S(1)}, u32[]{:S(2)}, u32[]{:S(2)}) collective-permute-start(bf16[4,3,16,1024]{3,2,1,0:T(8,128)(2,1)S(1)} %bitcast.38), channel_id=1, source_target_pairs={{0,8},{8,16},{16,24},{24,32},{32,40},{40,48},{48,56},{56,0},{1,9},... | collective-permute-start | bytes 1179656 | tf_op jit(solution)/shard_map/ppermute | solution.py:141
  47.2 11.1 %all_to_all.21 = bf16[8,2,16,128]{3,2,1,0:T(8,128)(2,1)S(1)} all-to-all(bf16[8,2,16,128]{3,2,1,0:T(8,128)(2,1)S(1)} %copy.14), channel_id=1, replica_groups=mesh['row'=8,'y'=8,'core'=2,'vox'=4] {'core','vox'}, dimensions={0} | all-to-all | bytes 131072 | tf_op jit(solution)/shard_map/all_to_all | solution.py:174
  58.3 0.0 collective-permute-done.2.refs_7_
  58.3 0.0 collective-permute-done.1.refs_1_
  58.3 0.9 tile.26
  59.2 11.0 %all-to-all-start.3 = ((bf16[8,256,128]{2,1,0:T(8,128)(2,1)}), bf16[8,256,128]{2,1,0:T(8,128)(2,1)}, u32[]{:S(2)}, u32[]{:S(2)}) async-start(bf16[8,256,128]{2,1,0:T(8,128)(2,1)} %tile.26), calls=%async_computation.3 | async-start | bytes 1048576 | tf_op jit(solution)/shard_map/all_to_all | solution.py:136
  70.2 2.2 %collective-permute-start.3 = (bf16[4,3,16,1024]{3,2,1,0:T(8,128)(2,1)S(1)}, bf16[4,3,16,1024]{3,2,1,0:T(8,128)(2,1)S(1)}, u32[]{:S(2)}, u32[]{:S(2)}) collective-permute-start(bf16[4,3,16,1024]{3,2,1,0:T(8,128)(2,1)S(1)} %collective-permute-done.1.refs_1_), channel_id=1, source_target_pairs={{0,8},{8,16},{16,24},{24,32},{32,40},{40,48},{48,56},{56,0},{1,9},... | collective-permute-start | bytes 1179656 | tf_op jit(solution)/shard_map/ppermute | solution.py:141
  72.4 4.3 %collective-permute-start.6 = (bf16[4,3,16,1024]{3,2,1,0:T(8,128)(2,1)S(1)}, bf16[4,3,16,1024]{3,2,1,0:T(8,128)(2,1)S(1)}, u32[]{:S(2)}, u32[]{:S(2)}) collective-permute-start(bf16[4,3,16,1024]{3,2,1,0:T(8,128)(2,1)S(1)} %collective-permute-done.2.refs_7_), channel_id=1, source_target_pairs={{0,56},{8,0},{16,8},{24,16},{32,24},{40,32},{48,40},{56,48},{1,57}... | collective-permute-start | bytes 1179656 | tf_op jit(solution)/shard_map/ppermute | solution.py:141
  76.7 6.1 %collective-permute-done.3.refs_2_ = bf16[4,3,16,1024]{3,2,1,0:T(8,128)(2,1)S(1)} collective-permute-done((bf16[4,3,16,1024]{3,2,1,0:T(8,128)(2,1)S(1)}, bf16[4,3,16,1024]{3,2,1,0:T(8,128)(2,1)S(1)}, u32[]{:S(2)}, u32[]{:S(2)}) %collective-permute-start.3) | collective-permute-done | bytes 393248 | tf_op jit(solution)/shard_map/ppermute | solution.py:141
  82.7 1.9 %collective-permute-start.4 = (bf16[4,3,16,1024]{3,2,1,0:T(8,128)(2,1)S(1)}, bf16[4,3,16,1024]{3,2,1,0:T(8,128)(2,1)S(1)}, u32[]{:S(2)}, u32[]{:S(2)}) collective-permute-start(bf16[4,3,16,1024]{3,2,1,0:T(8,128)(2,1)S(1)} %collective-permute-done.3.refs_2_), channel_id=1, source_target_pairs={{0,8},{8,16},{16,24},{24,32},{32,40},{40,48},{48,56},{56,0},{1,9},... | collective-permute-start | bytes 1179656 | tf_op jit(solution)/shard_map/ppermute | solution.py:141
  84.7 4.0 %collective-permute-start.8 = (bf16[4,3,16,1024]{3,2,1,0:T(8,128)(2,1)S(1)}, bf16[4,3,16,1024]{3,2,1,0:T(8,128)(2,1)S(1)}, u32[]{:S(2)}, u32[]{:S(2)}) collective-permute-start(bf16[4,3,16,1024]{3,2,1,0:T(8,128)(2,1)S(1)} %bitcast.39), channel_id=1, source_target_pairs={{0,4},{4,0},{1,5},{5,1},{2,6},{6,2},{3,7},{7,3},{8,12},{12,8},{9,1... | collective-permute-start | bytes 1179656 | tf_op jit(solution)/shard_map/ppermute | solution.py:181
  88.6 1.9 %collective-permute-start.15 = (bf16[4,3,16,1024]{3,2,1,0:T(8,128)(2,1)S(1)}, bf16[4,3,16,1024]{3,2,1,0:T(8,128)(2,1)S(1)}, u32[]{:S(2)}, u32[]{:S(2)}) collective-permute-start(bf16[4,3,16,1024]{3,2,1,0:T(8,128)(2,1)S(1)} %collective-permute-done.2.refs_7_), channel_id=1, source_target_pairs={{0,4},{4,0},{1,5},{5,1},{2,6},{6,2},{3,7},{7,3},{8,12},{12,8},{9,1... | collective-permute-start | bytes 1179656 | tf_op jit(solution)/shard_map/ppermute | solution.py:181
  90.6 2.4 %collective-permute-start.9 = (bf16[4,3,16,1024]{3,2,1,0:T(8,128)(2,1)S(1)}, bf16[4,3,16,1024]{3,2,1,0:T(8,128)(2,1)S(1)}, u32[]{:S(2)}, u32[]{:S(2)}) collective-permute-start(bf16[4,3,16,1024]{3,2,1,0:T(8,128)(2,1)S(1)} %collective-permute-done.1.refs_1_), channel_id=1, source_target_pairs={{0,4},{4,0},{1,5},{5,1},{2,6},{6,2},{3,7},{7,3},{8,12},{12,8},{9,1... | collective-permute-start | bytes 1179656 | tf_op jit(solution)/shard_map/ppermute | solution.py:181
  93.0 0.0 collective-permute-done.6.refs_6_
  93.0 4.9 %collective-permute-start.7 = (bf16[4,3,16,1024]{3,2,1,0:T(8,128)(2,1)S(1)}, bf16[4,3,16,1024]{3,2,1,0:T(8,128)(2,1)}, u32[]{:S(2)}, u32[]{:S(2)}) collective-permute-start(bf16[4,3,16,1024]{3,2,1,0:T(8,128)(2,1)S(1)} %collective-permute-done.6.refs_6_), channel_id=1, source_target_pairs={{0,56},{8,0},{16,8},{24,16},{32,24},{40,32},{48,40},{56,48},{1,57}... | collective-permute-start | bytes 1179656 | tf_op jit(solution)/shard_map/ppermute | solution.py:141
  97.9 0.0 all-to-all-done.3
  97.9 0.0 all-gather.2.cloned.1.call-done.whole
  97.9 1.9 %collective-permute-start.5 = (bf16[4,3,16,1024]{3,2,1,0:T(8,128)(2,1)S(1)}, bf16[4,3,16,1024]{3,2,1,0:T(8,128)(2,1)}, u32[]{:S(2)}, u32[]{:S(2)}) collective-permute-start(bf16[4,3,16,1024]{3,2,1,0:T(8,128)(2,1)S(1)} %collective-permute-done.4.refs_3_), channel_id=1, source_target_pairs={{0,8},{8,16},{16,24},{24,32},{32,40},{40,48},{48,56},{56,0},{1,9},... | collective-permute-start | bytes 1179656 | tf_op jit(solution)/shard_map/ppermute | solution.py:141
  99.9 1.2 slice_bitcast_fusion
  101.1 0.0 collective-permute-done.8.refs_8_
  101.1 2.3 %collective-permute-start.10 = (bf16[4,3,16,1024]{3,2,1,0:T(8,128)(2,1)S(1)}, bf16[4,3,16,1024]{3,2,1,0:T(8,128)(2,1)S(1)}, u32[]{:S(2)}, u32[]{:S(2)}) collective-permute-start(bf16[4,3,16,1024]{3,2,1,0:T(8,128)(2,1)S(1)} %collective-permute-done.3.refs_2_), channel_id=1, source_target_pairs={{0,4},{4,0},{1,5},{5,1},{2,6},{6,2},{3,7},{7,3},{8,12},{12,8},{9,1... | collective-permute-start | bytes 1179656 | tf_op jit(solution)/shard_map/ppermute | solution.py:181
  103.4 2.1 %collective-permute-start.14 = (bf16[4,3,16,1024]{3,2,1,0:T(8,128)(2,1)S(1)}, bf16[4,3,16,1024]{3,2,1,0:T(8,128)(2,1)S(1)}, u32[]{:S(2)}, u32[]{:S(2)}) collective-permute-start(bf16[4,3,16,1024]{3,2,1,0:T(8,128)(2,1)S(1)} %collective-permute-done.6.refs_6_), channel_id=1, source_target_pairs={{0,4},{4,0},{1,5},{5,1},{2,6},{6,2},{3,7},{7,3},{8,12},{12,8},{9,1... | collective-permute-start | bytes 1179656 | tf_op jit(solution)/shard_map/ppermute | solution.py:181
  105.6 0.0 collective-permute-done.9.refs_9_
  105.6 2.2 %collective-permute-start.11 = (bf16[4,3,16,1024]{3,2,1,0:T(8,128)(2,1)S(1)}, bf16[4,3,16,1024]{3,2,1,0:T(8,128)(2,1)S(1)}, u32[]{:S(2)}, u32[]{:S(2)}) collective-permute-start(bf16[4,3,16,1024]{3,2,1,0:T(8,128)(2,1)S(1)} %collective-permute-done.4.refs_3_), channel_id=1, source_target_pairs={{0,4},{4,0},{1,5},{5,1},{2,6},{6,2},{3,7},{7,3},{8,12},{12,8},{9,1... | collective-permute-start | bytes 1179656 | tf_op jit(solution)/shard_map/ppermute | solution.py:181
  107.8 2.1 %collective-permute-start.13 = (bf16[4,3,16,1024]{3,2,1,0:T(8,128)(2,1)}, bf16[4,3,16,1024]{3,2,1,0:T(8,128)(2,1)S(1)}, u32[]{:S(2)}, u32[]{:S(2)}) collective-permute-start(bf16[4,3,16,1024]{3,2,1,0:T(8,128)(2,1)} %collective-permute-done.7.refs_5_), channel_id=1, source_target_pairs={{0,4},{4,0},{1,5},{5,1},{2,6},{6,2},{3,7},{7,3},{8,12},{12,8},{9,1... | collective-permute-start | bytes 1179656 | tf_op jit(solution)/shard_map/ppermute | solution.py:181
  109.9 1.6 %collective-permute-done.5.refs_4_ = bf16[4,3,16,1024]{3,2,1,0:T(8,128)(2,1)} collective-permute-done((bf16[4,3,16,1024]{3,2,1,0:T(8,128)(2,1)S(1)}, bf16[4,3,16,1024]{3,2,1,0:T(8,128)(2,1)}, u32[]{:S(2)}, u32[]{:S(2)}) %collective-permute-start.5) | collective-permute-done | bytes 393248 | tf_op jit(solution)/shard_map/ppermute | solution.py:141
  111.5 3.0 %collective-permute-start.12 = (bf16[4,3,16,1024]{3,2,1,0:T(8,128)(2,1)}, bf16[4,3,16,1024]{3,2,1,0:T(8,128)(2,1)S(1)}, u32[]{:S(2)}, u32[]{:S(2)}) collective-permute-start(bf16[4,3,16,1024]{3,2,1,0:T(8,128)(2,1)} %collective-permute-done.5.refs_4_), channel_id=1, source_target_pairs={{0,4},{4,0},{1,5},{5,1},{2,6},{6,2},{3,7},{7,3},{8,12},{12,8},{9,1... | collective-permute-start | bytes 1179656 | tf_op jit(solution)/shard_map/ppermute | solution.py:181
  114.6 0.1 pad_add_fusion.at_ref
  114.6 1.1 fusion
  115.7 0.1 pad_maximum_fusion
  115.8 0.0 collective-permute-done.10.refs_10_
  115.8 0.0 collective-permute-done.14.refs_14_
  115.9 0.0 collective-permute-done.13.refs_13_
  115.9 0.2 collective-permute-done.12.refs_12_
  116.1 0.9 copy-done.1
  117.0 0.9 copy-done.2
  118.0 17.4 %factor_and_update.1 = (bf16[2,16,1024]{2,1,0:T(8,128)(2,1)}, bf16[2,1024,128]{2,1,0:T(8,128)(2,1)}, f32[1024,128]{1,0:T(8,128)}, f32[1024,128]{1,0:T(8,128)}) custom-call(s32[3]{0:T(128)S(1)} %pad_add_fusion.at_ref, bf16[2,1024,1024]{2,1,0:T(8,128)(2,1)S(1)} %copy-done, bf16[4,3,16,1024]{3,2,1,0:T(8,128)(2,1)S(1)} %bitcast.40, ...), custom_call_target="tpu_custom_call" | custom-call | flops 11274289152 | bytes 14680064 | tf_op jit(solution)/shard_map/factor_and_update/pallas_call | solution.py:195
  (13 shorter events, 0.1 us)
Async XLA Ops:
  7.2 90.7 %all-gather.2.cloned.1.call-start = ((), (), s32[]{:S(2)}) async-start(), calls=%async_computation.4 | async-start | bytes 4718592 | tf_op jit(solution)/shard_map/all_gather | solution.py:156
  9.2 17.7 %all-to-all-start = ((bf16[8,16,128]{2,1,0:T(8,128)(2,1)}), bf16[8,16,128]{2,1,0:T(8,128)(2,1)S(1)}, u32[]{:S(2)}, u32[]{:S(2)}) async-start(bf16[8,16,128]{2,1,0:T(8,128)(2,1)} %tile.10), calls=%async_computation | async-start | bytes 65536 | tf_op jit(solution)/shard_map/all_to_all | solution.py:136
  20.9 6.1 %collective-permute-start = (bf16[2,16,1024]{2,1,0:T(8,128)(2,1)S(1)}, bf16[2,16,1024]{2,1,0:T(8,128)(2,1)S(1)}, u32[]{:S(2)}, u32[]{:S(2)}) collective-permute-start(bf16[2,16,1024]{2,1,0:T(8,128)(2,1)S(1)} %pad_maximum_fusion.3), channel_id=1, source_target_pairs={{0,0},{1,1},{2,2},{3,3},{4,4},{5,5},{6,6},{7,7},{8,64},{9,65},{10,... | collective-permute-start | bytes 196616 | tf_op jit(solution)/shard_map/ppermute | solution.py:159
  37.9 20.4 %collective-permute-start.2 = (bf16[4,3,16,1024]{3,2,1,0:T(8,128)(2,1)S(1)}, bf16[4,3,16,1024]{3,2,1,0:T(8,128)(2,1)S(1)}, u32[]{:S(2)}, u32[]{:S(2)}) collective-permute-start(bf16[4,3,16,1024]{3,2,1,0:T(8,128)(2,1)S(1)} %bitcast.37), channel_id=1, source_target_pairs={{0,56},{8,0},{16,8},{24,16},{32,24},{40,32},{48,40},{56,48},{1,57}... | collective-permute-start | bytes 1179656 | tf_op jit(solution)/shard_map/ppermute | solution.py:141
  45.2 13.1 %collective-permute-start.1 = (bf16[4,3,16,1024]{3,2,1,0:T(8,128)(2,1)S(1)}, bf16[4,3,16,1024]{3,2,1,0:T(8,128)(2,1)S(1)}, u32[]{:S(2)}, u32[]{:S(2)}) collective-permute-start(bf16[4,3,16,1024]{3,2,1,0:T(8,128)(2,1)S(1)} %bitcast.38), channel_id=1, source_target_pairs={{0,8},{8,16},{16,24},{24,32},{32,40},{40,48},{48,56},{56,0},{1,9},... | collective-permute-start | bytes 1179656 | tf_op jit(solution)/shard_map/ppermute | solution.py:141
  59.2 38.7 %all-to-all-start.3 = ((bf16[8,256,128]{2,1,0:T(8,128)(2,1)}), bf16[8,256,128]{2,1,0:T(8,128)(2,1)}, u32[]{:S(2)}, u32[]{:S(2)}) async-start(bf16[8,256,128]{2,1,0:T(8,128)(2,1)} %tile.26), calls=%async_computation.3 | async-start | bytes 1048576 | tf_op jit(solution)/shard_map/all_to_all | solution.py:136
  70.2 12.5 %collective-permute-start.3 = (bf16[4,3,16,1024]{3,2,1,0:T(8,128)(2,1)S(1)}, bf16[4,3,16,1024]{3,2,1,0:T(8,128)(2,1)S(1)}, u32[]{:S(2)}, u32[]{:S(2)}) collective-permute-start(bf16[4,3,16,1024]{3,2,1,0:T(8,128)(2,1)S(1)} %collective-permute-done.1.refs_1_), channel_id=1, source_target_pairs={{0,8},{8,16},{16,24},{24,32},{32,40},{40,48},{48,56},{56,0},{1,9},... | collective-permute-start | bytes 1179656 | tf_op jit(solution)/shard_map/ppermute | solution.py:141
  72.4 20.6 %collective-permute-start.6 = (bf16[4,3,16,1024]{3,2,1,0:T(8,128)(2,1)S(1)}, bf16[4,3,16,1024]{3,2,1,0:T(8,128)(2,1)S(1)}, u32[]{:S(2)}, u32[]{:S(2)}) collective-permute-start(bf16[4,3,16,1024]{3,2,1,0:T(8,128)(2,1)S(1)} %collective-permute-done.2.refs_7_), channel_id=1, source_target_pairs={{0,56},{8,0},{16,8},{24,16},{32,24},{40,32},{48,40},{56,48},{1,57}... | collective-permute-start | bytes 1179656 | tf_op jit(solution)/shard_map/ppermute | solution.py:141
  82.7 15.1 %collective-permute-start.4 = (bf16[4,3,16,1024]{3,2,1,0:T(8,128)(2,1)S(1)}, bf16[4,3,16,1024]{3,2,1,0:T(8,128)(2,1)S(1)}, u32[]{:S(2)}, u32[]{:S(2)}) collective-permute-start(bf16[4,3,16,1024]{3,2,1,0:T(8,128)(2,1)S(1)} %collective-permute-done.3.refs_2_), channel_id=1, source_target_pairs={{0,8},{8,16},{16,24},{24,32},{32,40},{40,48},{48,56},{56,0},{1,9},... | collective-permute-start | bytes 1179656 | tf_op jit(solution)/shard_map/ppermute | solution.py:141
  84.7 16.4 %collective-permute-start.8 = (bf16[4,3,16,1024]{3,2,1,0:T(8,128)(2,1)S(1)}, bf16[4,3,16,1024]{3,2,1,0:T(8,128)(2,1)S(1)}, u32[]{:S(2)}, u32[]{:S(2)}) collective-permute-start(bf16[4,3,16,1024]{3,2,1,0:T(8,128)(2,1)S(1)} %bitcast.39), channel_id=1, source_target_pairs={{0,4},{4,0},{1,5},{5,1},{2,6},{6,2},{3,7},{7,3},{8,12},{12,8},{9,1... | collective-permute-start | bytes 1179656 | tf_op jit(solution)/shard_map/ppermute | solution.py:181
  88.6 14.8 %collective-permute-start.15 = (bf16[4,3,16,1024]{3,2,1,0:T(8,128)(2,1)S(1)}, bf16[4,3,16,1024]{3,2,1,0:T(8,128)(2,1)S(1)}, u32[]{:S(2)}, u32[]{:S(2)}) collective-permute-start(bf16[4,3,16,1024]{3,2,1,0:T(8,128)(2,1)S(1)} %collective-permute-done.2.refs_7_), channel_id=1, source_target_pairs={{0,4},{4,0},{1,5},{5,1},{2,6},{6,2},{3,7},{7,3},{8,12},{12,8},{9,1... | collective-permute-start | bytes 1179656 | tf_op jit(solution)/shard_map/ppermute | solution.py:181
  90.6 15.0 %collective-permute-start.9 = (bf16[4,3,16,1024]{3,2,1,0:T(8,128)(2,1)S(1)}, bf16[4,3,16,1024]{3,2,1,0:T(8,128)(2,1)S(1)}, u32[]{:S(2)}, u32[]{:S(2)}) collective-permute-start(bf16[4,3,16,1024]{3,2,1,0:T(8,128)(2,1)S(1)} %collective-permute-done.1.refs_1_), channel_id=1, source_target_pairs={{0,4},{4,0},{1,5},{5,1},{2,6},{6,2},{3,7},{7,3},{8,12},{12,8},{9,1... | collective-permute-start | bytes 1179656 | tf_op jit(solution)/shard_map/ppermute | solution.py:181
  93.0 14.8 %collective-permute-start.7 = (bf16[4,3,16,1024]{3,2,1,0:T(8,128)(2,1)S(1)}, bf16[4,3,16,1024]{3,2,1,0:T(8,128)(2,1)}, u32[]{:S(2)}, u32[]{:S(2)}) collective-permute-start(bf16[4,3,16,1024]{3,2,1,0:T(8,128)(2,1)S(1)} %collective-permute-done.6.refs_6_), channel_id=1, source_target_pairs={{0,56},{8,0},{16,8},{24,16},{32,24},{40,32},{48,40},{56,48},{1,57}... | collective-permute-start | bytes 1179656 | tf_op jit(solution)/shard_map/ppermute | solution.py:141
  97.9 13.6 %collective-permute-start.5 = (bf16[4,3,16,1024]{3,2,1,0:T(8,128)(2,1)S(1)}, bf16[4,3,16,1024]{3,2,1,0:T(8,128)(2,1)}, u32[]{:S(2)}, u32[]{:S(2)}) collective-permute-start(bf16[4,3,16,1024]{3,2,1,0:T(8,128)(2,1)S(1)} %collective-permute-done.4.refs_3_), channel_id=1, source_target_pairs={{0,8},{8,16},{16,24},{24,32},{32,40},{40,48},{48,56},{56,0},{1,9},... | collective-permute-start | bytes 1179656 | tf_op jit(solution)/shard_map/ppermute | solution.py:141
  99.8 16.2 %copy-start = (bf16[2,1024,1024]{2,1,0:T(8,128)(2,1)S(1)}, bf16[2,1024,1024]{2,1,0:T(8,128)(2,1)}, u32[]{:S(2)}) copy-start(bf16[2,1024,1024]{2,1,0:T(8,128)(2,1)} %all-gather.2.cloned.1.call-done.whole) | copy-start | bytes 12582916
  101.1 14.7 %collective-permute-start.10 = (bf16[4,3,16,1024]{3,2,1,0:T(8,128)(2,1)S(1)}, bf16[4,3,16,1024]{3,2,1,0:T(8,128)(2,1)S(1)}, u32[]{:S(2)}, u32[]{:S(2)}) collective-permute-start(bf16[4,3,16,1024]{3,2,1,0:T(8,128)(2,1)S(1)} %collective-permute-done.3.refs_2_), channel_id=1, source_target_pairs={{0,4},{4,0},{1,5},{5,1},{2,6},{6,2},{3,7},{7,3},{8,12},{12,8},{9,1... | collective-permute-start | bytes 1179656 | tf_op jit(solution)/shard_map/ppermute | solution.py:181
  103.4 12.4 %collective-permute-start.14 = (bf16[4,3,16,1024]{3,2,1,0:T(8,128)(2,1)S(1)}, bf16[4,3,16,1024]{3,2,1,0:T(8,128)(2,1)S(1)}, u32[]{:S(2)}, u32[]{:S(2)}) collective-permute-start(bf16[4,3,16,1024]{3,2,1,0:T(8,128)(2,1)S(1)} %collective-permute-done.6.refs_6_), channel_id=1, source_target_pairs={{0,4},{4,0},{1,5},{5,1},{2,6},{6,2},{3,7},{7,3},{8,12},{12,8},{9,1... | collective-permute-start | bytes 1179656 | tf_op jit(solution)/shard_map/ppermute | solution.py:181
  105.6 10.3 %collective-permute-start.11 = (bf16[4,3,16,1024]{3,2,1,0:T(8,128)(2,1)S(1)}, bf16[4,3,16,1024]{3,2,1,0:T(8,128)(2,1)S(1)}, u32[]{:S(2)}, u32[]{:S(2)}) collective-permute-start(bf16[4,3,16,1024]{3,2,1,0:T(8,128)(2,1)S(1)} %collective-permute-done.4.refs_3_), channel_id=1, source_target_pairs={{0,4},{4,0},{1,5},{5,1},{2,6},{6,2},{3,7},{7,3},{8,12},{12,8},{9,1... | collective-permute-start | bytes 1179656 | tf_op jit(solution)/shard_map/ppermute | solution.py:181
  107.8 8.1 %collective-permute-start.13 = (bf16[4,3,16,1024]{3,2,1,0:T(8,128)(2,1)}, bf16[4,3,16,1024]{3,2,1,0:T(8,128)(2,1)S(1)}, u32[]{:S(2)}, u32[]{:S(2)}) collective-permute-start(bf16[4,3,16,1024]{3,2,1,0:T(8,128)(2,1)} %collective-permute-done.7.refs_5_), channel_id=1, source_target_pairs={{0,4},{4,0},{1,5},{5,1},{2,6},{6,2},{3,7},{7,3},{8,12},{12,8},{9,1... | collective-permute-start | bytes 1179656 | tf_op jit(solution)/shard_map/ppermute | solution.py:181
  111.5 4.6 %collective-permute-start.12 = (bf16[4,3,16,1024]{3,2,1,0:T(8,128)(2,1)}, bf16[4,3,16,1024]{3,2,1,0:T(8,128)(2,1)S(1)}, u32[]{:S(2)}, u32[]{:S(2)}) collective-permute-start(bf16[4,3,16,1024]{3,2,1,0:T(8,128)(2,1)} %collective-permute-done.5.refs_4_), channel_id=1, source_target_pairs={{0,4},{4,0},{1,5},{5,1},{2,6},{6,2},{3,7},{7,3},{8,12},{12,8},{9,1... | collective-permute-start | bytes 1179656 | tf_op jit(solution)/shard_map/ppermute | solution.py:181
  116.1 1.0 copy-start.1
  117.0 0.9 copy-start.2
Sparse Core Ops, SparseCore 0:
  10.1 63.7 all-gather.1

commit v4 on v1

v4 whole, which is shorter than its diff:
```python
import functools

import jax
import jax.numpy as jnp
import numpy as np
from jax import lax
from jax.experimental import pallas as pl
from jax.experimental.pallas import tpu as pltpu
from jax.sharding import Mesh
from jax.sharding import PartitionSpec as P

TILE = 256
F32, BF16 = jnp.float32, jnp.bfloat16


def lower(inv, load, store):
    for i in range(inv.shape[0] // TILE):
        n = (i + 1) * TILE
        left = inv[i * TILE : n, :n]
        store(i, jnp.dot(left, load(n), preferred_element_type=F32))


def piece(t):
    return slice(t * TILE, (t + 1) * TILE)


def start_copies(pairs, sems, base=0):
    copies = [
        pltpu.make_async_copy(src, dst, sems.at[base + i]) for i, (src, dst) in enumerate(pairs)
    ]
    for copy in copies:
        copy.start()
    return copies


def wait(copies):
    for copy in copies:
        copy.wait()


def ordered(pieces, p, y, panel):
    count = len(pieces)
    return [(pieces[k].at[p], panel.at[:, lax.rem(y + (count - k), count)]) for k in range(count)]


def flatten(panel):
    return panel.reshape(panel.shape[0], -1, panel.shape[-1])


def pack_kernel(low, following, sent):
    cores, voxes = sent.shape[:2]
    cols = sent.shape[-1]
    for p, ref in enumerate((low, following)):
        for core in range(cores):
            for vox in range(voxes):
                for j in range(voxes + 1):
                    at = (core * voxes + (vox if j == voxes else j)) * cols
                    sent[core, vox, j, p] = ref[:, at : at + cols]


def unpack_kernel(got, mine, single):
    group, slots = got.shape[:2]
    for src in range(group):
        single[src] = got[src, slots - 1]
        for p in range(2):
            for j in range(slots - 1):
                mine[p, j, src] = got[src, j, p]


def top_kernel(whole, blocks, top, inv, panel, result, sems):
    loads = [(whole.at[0], inv)]
    loads += [(blocks.at[:, y], panel.at[y]) for y in range(panel.shape[0])]
    wait(start_copies(loads, sems))
    flat = panel.reshape(-1, panel.shape[-1])
    stores = []
    for t in range(top.shape[0] // TILE):

        def store(i, x):
            result[piece(t), piece(i)] = x.astype(BF16).T

        lower(inv, lambda n: flat[:n, piece(t)], store)
        stores += start_copies([(result.at[piece(t)], top.at[piece(t)])], sems, t)
    wait(stores)


def first_kernel(ys, at_ref, whole, *refs):
    pieces, (first, inv, panel, result, sems) = refs[:ys], refs[ys:]
    loads = [(whole.at[0], inv)] + ordered(pieces, 0, at_ref[0], panel)
    wait(start_copies(loads, sems))
    flat = flatten(panel)
    for t in range(first.shape[1] // TILE):

        def load(n):
            return jnp.concatenate([flat[2 * t, :n], flat[2 * t + 1, :n]], axis=1)

        def store(i, x):
            result[piece(i), piece(t)] = x.astype(BF16)

        lower(inv, load, store)
    wait(start_copies([(result, first)], sems))


def second_kernel(ys, at_ref, whole, top_own, top_other, first, *refs):
    pieces, refs = refs[:ys], refs[ys:]
    second, inv, panel, top, left, updated, result, sems = refs
    core = at_ref[1]
    loads = [(top_own, top.at[0]), (first, left)] + ordered(pieces, 1, at_ref[0], panel)
    early = start_copies(loads, sems)
    late = start_copies([(top_other, top.at[1]), (whole.at[1], inv)], sems, len(loads))
    wait(early)
    flat = flatten(panel)
    half = top_own.shape[0]
    for part, side in ((0, core), (1, 1 - core)):
        if part == 1:
            wait(late)
        for t in range(first.shape[1] // TILE):
            for i in range(half // TILE):
                rows = pl.ds(pl.multiple_of(side * half + i * TILE, TILE), TILE)
                change = jnp.dot(
                    top[part, piece(i)], left[:, piece(t)], preferred_element_type=F32
                )
                old = jnp.concatenate([flat[2 * t, rows], flat[2 * t + 1, rows]], axis=1)
                updated[rows, piece(t)] = (old.astype(F32) - change).astype(BF16)
    for t in range(first.shape[1] // TILE):

        def store(i, x):
            result[piece(i), piece(t)] = x.astype(BF16)

        lower(inv, lambda n: updated[:n, piece(t)], store)
    wait(start_copies([(result, second)], sems))


def side_kernel(
    at_ref, whole, top_own, top_other, side_one, side_two, first, second, inv, top, updated, sems
):
    core = at_ref[1]
    half = top_own.shape[0]
    early = start_copies([(whole.at[0], inv.at[0])], sems)
    late = start_copies(
        [(top_own, top.at[0]), (top_other, top.at[1]), (whole.at[1], inv.at[1])], sems, 1
    )
    wait(early)

    def store_first(i, x):
        first[piece(i), :] = x.astype(BF16)

    lower(inv.at[0], lambda n: side_one[:n, :], store_first)
    wait(late)
    for part, side in ((0, core), (1, 1 - core)):
        for i in range(half // TILE):
            rows = pl.ds(pl.multiple_of(side * half + i * TILE, TILE), TILE)
            change = jnp.dot(top[part, piece(i)], first[...], preferred_element_type=F32)
            updated[rows, :] = (side_two[rows, :].astype(F32) - change).astype(BF16)

    def store_second(i, x):
        second[piece(i), :] = x.astype(BF16)

    lower(inv.at[1], lambda n: updated[:n, :], store_second)


def rest_kernel(
    at_ref, first_own, first_other, second_own, second_other, side_one, side_two, gram, right,
    factor, solved, trailing, residual, first, second, minuend, sems,
):
    core, own = at_ref[1], at_ref[2]
    half = first_own.shape[1]
    cols = gram.shape[1]
    loads = [
        start_copies([(first_own, first.at[0]), (second_own, second.at[0])], sems),
        start_copies([(first_other, first.at[1]), (second_other, second.at[1])], sems, 2),
    ]
    loads[0] += start_copies([(gram, minuend.at[0]), (right, minuend.at[1])], sems, 4)
    solved[0] = side_one[:, cols:]
    solved[1] = side_two[:, cols:]
    one, two = side_one[...].T, side_two[...].T
    mine = pl.ds(pl.multiple_of(own, 16), factor.shape[1])
    for part, side in ((0, core), (1, 1 - core)):
        wait(loads[part])
        base = pl.multiple_of(side * half, half)
        factor[0, :, pl.ds(base, half)] = first[part, mine, :]
        factor[1, :, pl.ds(base, half)] = second[part, mine, :]
        for t in range(half // TILE):
            change = jnp.dot(one, first[part, :, piece(t)], preferred_element_type=F32)
            change += jnp.dot(two, second[part, :, piece(t)], preferred_element_type=F32)
            change = change.T
            rows = pl.ds(pl.multiple_of(base + t * TILE, TILE), TILE)
            trailing[rows, :] = minuend[0, rows, :].astype(F32) - change[:, :cols]
            residual[rows, :] = minuend[1, rows, :].astype(F32) - change[:, cols:]


def exchange(blocks, axis):
    flat = blocks.reshape(blocks.shape[0], -1, blocks.shape[-1])
    return lax.all_to_all(flat, axis, 0, 0, tiled=True).reshape(blocks.shape)


def gather_small(block, axis, size):
    return exchange(jnp.broadcast_to(block[None], (size,) + block.shape), axis)


def shift(block, axis, size, by):
    return lax.ppermute(block, axis, [(i, (i + by) % size) for i in range(size)])


def call(body, name, outs, scratch, flops, *operands, small=False):
    local = pl.BlockSpec(memory_space=pltpu.VMEM)
    anywhere = pl.BlockSpec(memory_space=pl.ANY)
    specs = [
        pl.BlockSpec(memory_space=pltpu.SMEM) if x.dtype == jnp.int32
        else local if small or x.shape[-1] == TILE else anywhere
        for x in operands
    ]
    moved = sum(x.size * x.dtype.itemsize for x in operands)
    return pl.pallas_call(
        body,
        name=name,
        out_shape=tuple(jax.ShapeDtypeStruct(shape, dtype) for shape, dtype in outs),
        in_specs=specs,
        out_specs=(local if small or len(outs) > 1 else anywhere,) * len(outs),
        scratch_shapes=scratch,
        compiler_params=pltpu.CompilerParams(vmem_limit_bytes=(8 if small else 56) << 20),
        cost_estimate=pl.CostEstimate(flops=flops, bytes_accessed=moved, transcendentals=0),
    )(*operands)


def per_device(sizes, panel_top, panel_low, panel_next, gram_rest, inverses, right_top, right_low):
    rows, ys, cores, voxes = sizes
    axes = ("row", "y", "core", "vox")
    near = ("core", "vox")
    order = np.arange(rows * ys * cores * voxes).reshape(sizes)
    swap = list(zip(order.ravel().tolist(), order.transpose(1, 0, 2, 3).ravel().tolist()))
    y, core, vox = lax.axis_index("y"), lax.axis_index("core"), lax.axis_index("vox")
    size, (height, width) = inverses.shape[2], panel_low.shape
    cols = gram_rest.shape[1]
    half = height // cores
    group = cores * voxes
    other = [(0, 1), (1, 0)]

    whole = lax.all_gather(inverses, "row", axis=1, tiled=True)

    (sent,) = call(
        pack_kernel, "pack", [((cores, voxes, voxes + 1, 2, width, cols), BF16)], [], 0,
        panel_low.T, panel_next.T, small=True,
    )
    got = exchange(sent.reshape((group,) + sent.shape[2:]), near)
    mine, single = call(
        unpack_kernel, "unpack",
        [((2, voxes, group, width, cols), BF16), ((group, 2, width, cols), BF16)], [], 0,
        got, small=True,
    )
    mine = mine.reshape(2, voxes, group * width, cols)
    swapped = lax.ppermute(single, axes, swap)

    def ring(k):
        up = shift(pieces[k - 1], "y", ys, 1)
        down = shift(pieces[(ys - k + 1) % ys], "y", ys, -1) if k < ys - k else None
        return up, down

    pieces = {0: mine}
    top, pieces[0] = lax.optimization_barrier((panel_top.T, pieces[0]))
    pieces[1], pieces[ys - 1] = ring(1)
    top = gather_small(top, "row", rows).transpose(1, 0, 2).reshape(width, size)
    top, pieces[1], pieces[ys - 1] = lax.optimization_barrier((top, pieces[1], pieces[ys - 1]))
    pieces[2], pieces[ys - 2] = ring(2)
    tops = gather_small(top, "y", ys)
    tops, pieces[2], pieces[ys - 2] = lax.optimization_barrier((tops, pieces[2], pieces[ys - 2]))
    pieces[3], pieces[ys - 3] = ring(3)
    blocks = tops.reshape(ys, width, cores, size // cores).transpose(2, 0, 1, 3)
    blocks = jnp.broadcast_to(blocks[:, None], (cores, voxes) + blocks.shape[1:])
    blocks = exchange(blocks.reshape((group,) + blocks.shape[2:]), near)
    blocks, swapped, pieces[3], pieces[ys - 3] = lax.optimization_barrier(
        (blocks, swapped, pieces[3], pieces[ys - 3])
    )
    pieces[4], _ = ring(4)
    matching = gather_small(swapped, "row", rows)
    matching = jnp.moveaxis(matching, 2, 0).reshape(2, size, cols)
    pieces = [pieces[k] for k in range(ys)]

    own = ((y * cores + core) * voxes + vox) * width
    where = jnp.stack([y, core, own]).astype(jnp.int32)
    sems = pltpu.SemaphoreType.DMA((ys + 4,))
    panel = pltpu.VMEM((voxes, ys, group * width, cols), BF16)
    square = pltpu.VMEM((size, size), BF16)
    tall = pltpu.VMEM((size, half), BF16)
    work = 2 * size * size

    (top_own,) = call(
        top_kernel, "top", [((size // cores, size), BF16)],
        [square, pltpu.VMEM((ys, group, width, size // cores), BF16),
         pltpu.VMEM((size // cores, size), BF16), sems],
        work * size // cores, whole, blocks,
    )
    top_other = lax.ppermute(top_own, "core", other)
    (first_own,) = call(
        functools.partial(first_kernel, ys), "first", [((size, half), BF16)],
        [square, panel, tall, sems], work * half, where, whole, *pieces,
    )
    first_other = lax.ppermute(first_own, "core", other)
    (second_own,) = call(
        functools.partial(second_kernel, ys), "second", [((size, half), BF16)],
        [square, panel, pltpu.VMEM((cores, size // cores, size), BF16), tall, tall, tall, sems],
        2 * work * half, where, whole, top_own, top_other, first_own, *pieces,
    )
    second_other = lax.ppermute(second_own, "core", other)
    sides = [jnp.concatenate([matching[k], right_top[k]], axis=1) for k in range(2)]
    side_one, side_two = call(
        side_kernel, "side", [((size, 2 * cols), BF16)] * 2,
        [pltpu.VMEM((2, size, size), BF16), pltpu.VMEM((cores, size // cores, size), BF16),
         pltpu.VMEM((size, 2 * cols), BF16), sems],
        6 * work * cols, where, whole, top_own, top_other, *sides,
    )
    factor, solved, trailing, residual = call(
        rest_kernel, "rest",
        [((2, width, height), BF16), ((2, size, cols), BF16)] + [((height, cols), F32)] * 2,
        [pltpu.VMEM((cores, size, half), BF16)] * 2 + [pltpu.VMEM((2, height, cols), BF16), sems],
        4 * work * cols, where, first_own, first_other, second_own, second_other,
        side_one, side_two, gram_rest, right_low,
    )
    return (factor.transpose(0, 2, 1), solved, trailing, residual)


def solution(mesh):
    cores = 2
    sizes = (mesh.shape["row"], mesh.shape["col"] // cores, cores, mesh.shape["vox"])
    split = Mesh(mesh.devices.reshape(sizes), ("row", "y", "core", "vox"))
    cols = ("y", "core", "vox")
    in_specs = (
        P("row", cols),
        P("row", cols),
        P("row", cols),
        P("row", cols),
        P(None, "row", None),
        P(None, None, cols),
        P("row", cols),
    )
    out_specs = (
        P(None, "row", cols),
        P(None, None, cols),
        P("row", cols),
        P("row", cols),
    )
    return jax.shard_map(
        functools.partial(per_device, sizes),
        mesh=split,
        in_specs=in_specs,
        out_specs=out_specs,
        check_vma=False,
    )
```

time: 261 us -> 154 us (0.59)
  the two profiles are of different devices: /device:TPU:16 before, /device:TPU:1 now
where the time goes in v4:
time: 154 us; the launch traced here: 153 us
  starting transfers between devices  61.3 us (40%)
  Pallas kernels  27 us (18%)
  waiting for transfers between devices  21.8 us (14%)
  blocking collectives  16.8 us (11%)
  between operations  14.4 us (9%)
  local copies, waits for them, and re-layouts  10.1 us (7%)
  other arithmetic  1.68 us (1%)
    all_to_all x4, starting transfers between devices, exchange(): return lax.all_to_all(flat, axis, 0, 0, tiled=True).reshape(blocks.shape)  30.7 us
    pallas_call x7, Pallas kernels, call(): pl.pallas_call(body, name=name, out_shape=tuple((jax.ShapeDtypeStruct(sha...  27 us
    ppermute x7, starting transfers between devices, shift(): lax.ppermute(block, axis, [(i, (i + by) % size) for i in range(size)])  23.1 us
    ppermute x7, waiting for transfers between devices, shift(): lax.ppermute(block, axis, [(i, (i + by) % size) for i in range(size)])  18.5 us
    all_to_all x1, blocking collectives, exchange(): return lax.all_to_all(flat, axis, 0, 0, tiled=True).reshape(blocks.shape)  16.8 us
    unnamed x30, local copies, waits for them, and re-layouts  5.68 us
  transfers between devices with their start and end apart: 16, of which 8 were waited for; matrix products, arithmetic and copies ran while one was open for 4% of the time, Pallas kernels for 11%

profile of v4, /device:TPU:1, one launch (start us, length us, event | category | flops | bytes accessed | tf_op | source)
XLA Modules:
  0.0 153.1 jit_solution(14024949609829951594)
XLA Ops:
  7.2 0.0 all-gather.2.cloned.1.call-start
  7.2 0.7 all-gather.2.cloned.1.call-update
  7.9 0.7 copy-done.1
  8.7 0.8 copy-done.2
  9.5 16.8 %all_to_all.25 = bf16[8,160,128]{2,1,0:T(8,128)(2,1)S(1)} all-to-all(bf16[8,160,128]{2,1,0:T(8,128)(2,1)S(1)} %bitcast.30), channel_id=1, replica_groups=mesh['row'=8,'y'=8,'core'=2,'vox'=4] {'core','vox'}, dimensions={0} | all-to-all | bytes 655360 | tf_op jit(solution)/shard_map/all_to_all | solution.py:193
  26.3 0.0 copy-start
  26.3 1.3 broadcast_in_dim.10
  27.7 6.4 %all-to-all-start.1 = ((bf16[8,16,128]{2,1,0:T(8,128)(2,1)}), bf16[8,16,128]{2,1,0:T(8,128)(2,1)S(1)}, u32[]{:S(2)}, u32[]{:S(2)}) async-start(bf16[8,16,128]{2,1,0:T(8,128)(2,1)} %broadcast_in_dim.10), calls=%async_computation.1 | async-start | bytes 65536 | tf_op jit(solution)/shard_map/all_to_all | solution.py:193
  34.1 3.2 %collective-permute-start = (bf16[2,4,128,128]{3,2,1,0:T(8,128)(2,1)S(1)}, bf16[2,4,128,128]{3,2,1,0:T(8,128)(2,1)S(1)}, u32[]{:S(2)}, u32[]{:S(2)}) collective-permute-start(bf16[2,4,128,128]{3,2,1,0:T(8,128)(2,1)S(1)} %bitcast.31), channel_id=1, source_target_pairs={{0,8},{8,16},{16,24},{24,32},{32,40},{40,48},{48,56},{56,0},{1,9},... | collective-permute-start | bytes 786440 | tf_op jit(solution)/shard_map/ppermute | solution.py:201
  37.3 3.8 %collective-permute-start.1 = (bf16[2,4,128,128]{3,2,1,0:T(8,128)(2,1)S(1)}, bf16[2,4,128,128]{3,2,1,0:T(8,128)(2,1)S(1)}, u32[]{:S(2)}, u32[]{:S(2)}) collective-permute-start(bf16[2,4,128,128]{3,2,1,0:T(8,128)(2,1)S(1)} %bitcast.32), channel_id=1, source_target_pairs={{0,56},{8,0},{16,8},{24,16},{32,24},{40,32},{48,40},{56,48},{1,57}... | collective-permute-start | bytes 786440 | tf_op jit(solution)/shard_map/ppermute | solution.py:201
  41.1 0.2 all-to-all-done.1
  41.3 4.0 %collective-permute-done.refs_1_ = bf16[2,4,128,128]{3,2,1,0:T(8,128)(2,1)S(1)} collective-permute-done((bf16[2,4,128,128]{3,2,1,0:T(8,128)(2,1)S(1)}, bf16[2,4,128,128]{3,2,1,0:T(8,128)(2,1)S(1)}, u32[]{:S(2)}, u32[]{:S(2)}) %collective-permute-start) | collective-permute-done | bytes 262176 | tf_op jit(solution)/shard_map/ppermute | solution.py:201
  45.3 0.8 collective-permute-done.1.refs_7_
  46.1 0.8 broadcast_in_dim.11
  46.9 7.0 %all-to-all-start.2 = ((bf16[8,16,1024]{2,1,0:T(8,128)(2,1)}), bf16[8,16,1024]{2,1,0:T(8,128)(2,1)S(1)}, u32[]{:S(2)}, u32[]{:S(2)}) async-start(bf16[8,16,1024]{2,1,0:T(8,128)(2,1)} %broadcast_in_dim.11), calls=%async_computation.2 | async-start | bytes 524288 | tf_op jit(solution)/shard_map/all_to_all | solution.py:193
  53.9 3.4 %collective-permute-start.2 = (bf16[2,4,128,128]{3,2,1,0:T(8,128)(2,1)S(1)}, bf16[2,4,128,128]{3,2,1,0:T(8,128)(2,1)S(1)}, u32[]{:S(2)}, u32[]{:S(2)}) collective-permute-start(bf16[2,4,128,128]{3,2,1,0:T(8,128)(2,1)S(1)} %collective-permute-done.refs_1_), channel_id=1, source_target_pairs={{0,8},{8,16},{16,24},{24,32},{32,40},{40,48},{48,56},{56,0},{1,9},... | collective-permute-start | bytes 786440 | tf_op jit(solution)/shard_map/ppermute | solution.py:201
  57.3 3.1 %collective-permute-start.3 = (bf16[2,4,128,128]{3,2,1,0:T(8,128)(2,1)S(1)}, bf16[2,4,128,128]{3,2,1,0:T(8,128)(2,1)S(1)}, u32[]{:S(2)}, u32[]{:S(2)}) collective-permute-start(bf16[2,4,128,128]{3,2,1,0:T(8,128)(2,1)S(1)} %collective-permute-done.1.refs_7_), channel_id=1, source_target_pairs={{0,56},{8,0},{16,8},{24,16},{32,24},{40,32},{48,40},{56,48},{1,57}... | collective-permute-start | bytes 786440 | tf_op jit(solution)/shard_map/ppermute | solution.py:201
  60.4 7.4 %collective-permute-done.2.refs_2_ = bf16[2,4,128,128]{3,2,1,0:T(8,128)(2,1)S(1)} collective-permute-done((bf16[2,4,128,128]{3,2,1,0:T(8,128)(2,1)S(1)}, bf16[2,4,128,128]{3,2,1,0:T(8,128)(2,1)S(1)}, u32[]{:S(2)}, u32[]{:S(2)}) %collective-permute-start.2) | collective-permute-done | bytes 262176 | tf_op jit(solution)/shard_map/ppermute | solution.py:201
  67.8 0.0 collective-permute-done.3.refs_6_
  67.8 0.2 reshape.41
  68.0 1.1 broadcast_in_dim.12
  69.2 5.4 %all-to-all-start.3 = ((bf16[8,128,512]{2,1,0:T(8,128)(2,1)}), bf16[8,128,512]{2,1,0:T(8,128)(2,1)S(1)}, u32[]{:S(2)}, u32[]{:S(2)}) async-start(bf16[8,128,512]{2,1,0:T(8,128)(2,1)} %bitcast.11), calls=%async_computation.3 | async-start | bytes 2097152 | tf_op jit(solution)/shard_map/all_to_all | solution.py:193
  74.6 3.1 %collective-permute-start.5 = (bf16[2,4,128,128]{3,2,1,0:T(8,128)(2,1)S(1)}, bf16[2,4,128,128]{3,2,1,0:T(8,128)(2,1)S(1)}, u32[]{:S(2)}, u32[]{:S(2)}) collective-permute-start(bf16[2,4,128,128]{3,2,1,0:T(8,128)(2,1)S(1)} %collective-permute-done.2.refs_2_), channel_id=1, source_target_pairs={{0,8},{8,16},{16,24},{24,32},{32,40},{40,48},{48,56},{56,0},{1,9},... | collective-permute-start | bytes 786440 | tf_op jit(solution)/shard_map/ppermute | solution.py:201
  77.7 3.4 %collective-permute-start.6 = (bf16[2,4,128,128]{3,2,1,0:T(8,128)(2,1)S(1)}, bf16[2,4,128,128]{3,2,1,0:T(8,128)(2,1)S(1)}, u32[]{:S(2)}, u32[]{:S(2)}) collective-permute-start(bf16[2,4,128,128]{3,2,1,0:T(8,128)(2,1)S(1)} %collective-permute-done.3.refs_6_), channel_id=1, source_target_pairs={{0,56},{8,0},{16,8},{24,16},{32,24},{40,32},{48,40},{56,48},{1,57}... | collective-permute-start | bytes 786440 | tf_op jit(solution)/shard_map/ppermute | solution.py:201
  81.1 0.7 collective-permute-start.4
  81.7 3.8 %collective-permute-done.5.refs_3_ = bf16[2,4,128,128]{3,2,1,0:T(8,128)(2,1)S(1)} collective-permute-done((bf16[2,4,128,128]{3,2,1,0:T(8,128)(2,1)S(1)}, bf16[2,4,128,128]{3,2,1,0:T(8,128)(2,1)S(1)}, u32[]{:S(2)}, u32[]{:S(2)}) %collective-permute-start.5) | collective-permute-done | bytes 262176 | tf_op jit(solution)/shard_map/ppermute | solution.py:201
  85.5 1.6 %collective-permute-done.6.refs_5_ = bf16[2,4,128,128]{3,2,1,0:T(8,128)(2,1)S(1)} collective-permute-done((bf16[2,4,128,128]{3,2,1,0:T(8,128)(2,1)S(1)}, bf16[2,4,128,128]{3,2,1,0:T(8,128)(2,1)S(1)}, u32[]{:S(2)}, u32[]{:S(2)}) %collective-permute-start.6) | collective-permute-done | bytes 262176 | tf_op jit(solution)/shard_map/ppermute | solution.py:201
  87.1 2.4 %all-to-all-done.3 = bf16[8,128,512]{2,1,0:T(8,128)(2,1)S(1)} async-done(((bf16[8,128,512]{2,1,0:T(8,128)(2,1)}), bf16[8,128,512]{2,1,0:T(8,128)(2,1)S(1)}, u32[]{:S(2)}, u32[]{:S(2)}) %all-to-all-start.3) | async-done | bytes 1048608 | tf_op jit(solution)/shard_map/all_to_all | solution.py:193
  89.5 1.0 copy-done.3
  90.5 3.7 %top.1.top_own = bf16[512,1024]{1,0:T(8,128)(2,1)} custom-call(bf16[2,1024,1024]{2,1,0:T(8,128)(2,1)} %all-gather.2.cloned.1.call-done.whole, bf16[8,8,16,512]{3,2,1,0:T(8,128)(2,1)} %bitcast.37), custom_call_target="tpu_custom_call" | custom-call | flops 1073741824 | bytes 5242880 | tf_op jit(solution)/shard_map/top/pallas_call | solution.py:213
  94.3 2.3 %collective-permute-start.9 = (bf16[512,1024]{1,0:T(8,128)(2,1)}, bf16[512,1024]{1,0:T(8,128)(2,1)S(1)}, u32[]{:S(2)}, u32[]{:S(2)}) collective-permute-start(bf16[512,1024]{1,0:T(8,128)(2,1)} %top.1.top_own), channel_id=1, source_target_pairs={{0,4},{4,0},{1,5},{5,1},{2,6},{6,2},{3,7},{7,3},{8,12},{12,8},{9,1... | collective-permute-start | bytes 3145736 | tf_op jit(solution)/shard_map/ppermute | solution.py:292
  96.6 3.1 %collective-permute-start.7 = (bf16[2,4,128,128]{3,2,1,0:T(8,128)(2,1)S(1)}, bf16[2,4,128,128]{3,2,1,0:T(8,128)(2,1)S(1)}, u32[]{:S(2)}, u32[]{:S(2)}) collective-permute-start(bf16[2,4,128,128]{3,2,1,0:T(8,128)(2,1)S(1)} %collective-permute-done.5.refs_3_), channel_id=1, source_target_pairs={{0,8},{8,16},{16,24},{24,32},{32,40},{40,48},{48,56},{56,0},{1,9},... | collective-permute-start | bytes 786440 | tf_op jit(solution)/shard_map/ppermute | solution.py:201
  99.7 0.9 broadcast_in_dim.14
  100.6 11.9 %all-to-all-start.4 = ((bf16[8,256,128]{2,1,0:T(8,128)(2,1)}), bf16[8,256,128]{2,1,0:T(8,128)(2,1)S(1)}, u32[]{:S(2)}, u32[]{:S(2)}) async-start(bf16[8,256,128]{2,1,0:T(8,128)(2,1)} %broadcast_in_dim.14), calls=%async_computation.4 | async-start | bytes 1048576 | tf_op jit(solution)/shard_map/all_to_all | solution.py:193
  112.5 0.6 pad_add_fusion.at_ref
  113.1 0.9 collective-permute-done.7.refs_4_
  114.0 0.7 copy-done.13
  114.7 4.4 %first.1.first_own = bf16[1024,512]{1,0:T(8,128)(2,1)} custom-call(s32[3]{0:T(128)} %pad_add_fusion.at_ref, bf16[2,1024,1024]{2,1,0:T(8,128)(2,1)} %all-gather.2.cloned.1.call-done.whole, bf16[2,4,128,128]{3,2,1,0:T(8,128)(2,1)} %bitcast.33, bf16[2,4,128,128]{3,2,1,0:T(8,128)(2,1)} %copy-done.7, bf16[2,4,128,128]{3,2,1,0:T(8,128)(2,1)} %copy-done.9, ...), custom_call_target="tpu_custom_call" | custom-call | flops 1073741824 | bytes 6291468 | tf_op jit(solution)/shard_map/first/pallas_call | solution.py:213
  119.1 0.0 copy-start.14
  119.1 2.6 %collective-permute-start.8 = (bf16[1024,512]{1,0:T(8,128)(2,1)}, bf16[1024,512]{1,0:T(8,128)(2,1)S(1)}, u32[]{:S(2)}, u32[]{:S(2)}) collective-permute-start(bf16[1024,512]{1,0:T(8,128)(2,1)} %first.1.first_own), channel_id=1, source_target_pairs={{0,4},{4,0},{1,5},{5,1},{2,6},{6,2},{3,7},{7,3},{8,12},{12,8},{9,1... | collective-permute-start | bytes 3145736 | tf_op jit(solution)/shard_map/ppermute | solution.py:297
  121.8 1.1 copy-done.4
  122.9 6.3 %second.1.second_own = bf16[1024,512]{1,0:T(8,128)(2,1)} custom-call(s32[3]{0:T(128)} %pad_add_fusion.at_ref, bf16[2,1024,1024]{2,1,0:T(8,128)(2,1)} %all-gather.2.cloned.1.call-done.whole, bf16[512,1024]{1,0:T(8,128)(2,1)} %top.1.top_own, bf16[512,1024]{1,0:T(8,128)(2,1)} %copy-done.4, bf16[1024,512]{1,0:T(8,128)(2,1)} %first.1.first_own, ...), custom_call_target="tpu_custom_call" | custom-call | flops 2147483648 | bytes 9437196 | tf_op jit(solution)/shard_map/second/pallas_call | solution.py:213
  129.1 1.9 %collective-permute-start.10 = (bf16[1024,512]{1,0:T(8,128)(2,1)}, bf16[1024,512]{1,0:T(8,128)(2,1)S(1)}, u32[]{:S(2)}, u32[]{:S(2)}) collective-permute-start(bf16[1024,512]{1,0:T(8,128)(2,1)} %second.1.second_own), channel_id=1, source_target_pairs={{0,4},{4,0},{1,5},{5,1},{2,6},{6,2},{3,7},{7,3},{8,12},{12,8},{9,1... | collective-permute-start | bytes 3145736 | tf_op jit(solution)/shard_map/ppermute | solution.py:303
  131.2 1.1 pad_maximum_fusion
  132.3 6.3 %side.1 = (bf16[1024,256]{1,0:T(8,128)(2,1)}, bf16[1024,256]{1,0:T(8,128)(2,1)}) custom-call(s32[3]{0:T(128)} %pad_add_fusion.at_ref, bf16[2,1024,1024]{2,1,0:T(8,128)(2,1)} %all-gather.2.cloned.1.call-done.whole, bf16[512,1024]{1,0:T(8,128)(2,1)} %top.1.top_own, bf16[512,1024]{1,0:T(8,128)(2,1)} %copy-done.4, bf16[1024,256]{1,0:T(8,128)(2,1)} %get-tuple-element.48.side_one, ...), custom_call_target="tpu_custom_call" | custom-call | flops 1610612736 | bytes 7340044 | tf_op jit(solution)/shard_map/side/pallas_call | solution.py:213
  138.7 1.0 copy-done.5
  139.6 0.4 copy-done.6
  140.0 6.2 %rest.1 = (bf16[2,16,1024]{2,1,0:T(8,128)(2,1)}, bf16[2,1024,128]{2,1,0:T(8,128)(2,1)}, f32[1024,128]{1,0:T(8,128)}, f32[1024,128]{1,0:T(8,128)}) custom-call(s32[3]{0:T(128)} %pad_add_fusion.at_ref, bf16[1024,512]{1,0:T(8,128)(2,1)} %first.1.first_own, bf16[1024,512]{1,0:T(8,128)(2,1)} %copy-done.5, bf16[1024,512]{1,0:T(8,128)(2,1)} %second.1.second_own, ...), custom_call_target="tpu_custom_call" | custom-call | flops 1073741824 | bytes 5767180 | tf_op jit(solution)/shard_map/rest/pallas_call | solution.py:213
  (34 shorter events, 0.2 us)
Async XLA Ops:
  7.2 82.4 %all-gather.2.cloned.1.call-start = ((), (), s32[]{:S(2)}) async-start(), calls=%async_computation.5 | async-start | bytes 4718592 | tf_op jit(solution)/shard_map/all_gather | solution.py:238
  7.9 0.8 copy-start.1
  8.7 0.8 copy-start.2
  26.3 67.9 %copy-start = (bf16[2,4,8,16,128]{4,3,2,1,0:T(8,128)(2,1)}, bf16[2,4,8,16,128]{4,3,2,1,0:T(8,128)(2,1)S(1)}, u32[]{:S(2)}) copy-start(bf16[2,4,8,16,128]{4,3,2,1,0:T(8,128)(2,1)S(1)} %get-tuple-element.24) | copy-start | bytes 786436
  27.7 13.6 %all-to-all-start.1 = ((bf16[8,16,128]{2,1,0:T(8,128)(2,1)}), bf16[8,16,128]{2,1,0:T(8,128)(2,1)S(1)}, u32[]{:S(2)}, u32[]{:S(2)}) async-start(bf16[8,16,128]{2,1,0:T(8,128)(2,1)} %broadcast_in_dim.10), calls=%async_computation.1 | async-start | bytes 65536 | tf_op jit(solution)/shard_map/all_to_all | solution.py:193
  34.1 11.2 %collective-permute-start = (bf16[2,4,128,128]{3,2,1,0:T(8,128)(2,1)S(1)}, bf16[2,4,128,128]{3,2,1,0:T(8,128)(2,1)S(1)}, u32[]{:S(2)}, u32[]{:S(2)}) collective-permute-start(bf16[2,4,128,128]{3,2,1,0:T(8,128)(2,1)S(1)} %bitcast.31), channel_id=1, source_target_pairs={{0,8},{8,16},{16,24},{24,32},{32,40},{40,48},{48,56},{56,0},{1,9},... | collective-permute-start | bytes 786440 | tf_op jit(solution)/shard_map/ppermute | solution.py:201
  37.3 8.9 %collective-permute-start.1 = (bf16[2,4,128,128]{3,2,1,0:T(8,128)(2,1)S(1)}, bf16[2,4,128,128]{3,2,1,0:T(8,128)(2,1)S(1)}, u32[]{:S(2)}, u32[]{:S(2)}) collective-permute-start(bf16[2,4,128,128]{3,2,1,0:T(8,128)(2,1)S(1)} %bitcast.32), channel_id=1, source_target_pairs={{0,56},{8,0},{16,8},{24,16},{32,24},{40,32},{48,40},{56,48},{1,57}... | collective-permute-start | bytes 786440 | tf_op jit(solution)/shard_map/ppermute | solution.py:201
  45.3 49.0 %copy-start.7 = (bf16[2,4,128,128]{3,2,1,0:T(8,128)(2,1)}, bf16[2,4,128,128]{3,2,1,0:T(8,128)(2,1)S(1)}, u32[]{:S(2)}) copy-start(bf16[2,4,128,128]{3,2,1,0:T(8,128)(2,1)S(1)} %collective-permute-done.refs_1_) | copy-start | bytes 786436
  46.1 48.1 %copy-start.8 = (bf16[2,4,128,128]{3,2,1,0:T(8,128)(2,1)}, bf16[2,4,128,128]{3,2,1,0:T(8,128)(2,1)S(1)}, u32[]{:S(2)}) copy-start(bf16[2,4,128,128]{3,2,1,0:T(8,128)(2,1)S(1)} %collective-permute-done.1.refs_7_) | copy-start | bytes 786436
  46.9 20.9 %all-to-all-start.2 = ((bf16[8,16,1024]{2,1,0:T(8,128)(2,1)}), bf16[8,16,1024]{2,1,0:T(8,128)(2,1)S(1)}, u32[]{:S(2)}, u32[]{:S(2)}) async-start(bf16[8,16,1024]{2,1,0:T(8,128)(2,1)} %broadcast_in_dim.11), calls=%async_computation.2 | async-start | bytes 524288 | tf_op jit(solution)/shard_map/all_to_all | solution.py:193
  53.9 13.9 %collective-permute-start.2 = (bf16[2,4,128,128]{3,2,1,0:T(8,128)(2,1)S(1)}, bf16[2,4,128,128]{3,2,1,0:T(8,128)(2,1)S(1)}, u32[]{:S(2)}, u32[]{:S(2)}) collective-permute-start(bf16[2,4,128,128]{3,2,1,0:T(8,128)(2,1)S(1)} %collective-permute-done.refs_1_), channel_id=1, source_target_pairs={{0,8},{8,16},{16,24},{24,32},{32,40},{40,48},{48,56},{56,0},{1,9},... | collective-permute-start | bytes 786440 | tf_op jit(solution)/shard_map/ppermute | solution.py:201
  57.3 10.5 %collective-permute-start.3 = (bf16[2,4,128,128]{3,2,1,0:T(8,128)(2,1)S(1)}, bf16[2,4,128,128]{3,2,1,0:T(8,128)(2,1)S(1)}, u32[]{:S(2)}, u32[]{:S(2)}) collective-permute-start(bf16[2,4,128,128]{3,2,1,0:T(8,128)(2,1)S(1)} %collective-permute-done.1.refs_7_), channel_id=1, source_target_pairs={{0,56},{8,0},{16,8},{24,16},{32,24},{40,32},{48,40},{56,48},{1,57}... | collective-permute-start | bytes 786440 | tf_op jit(solution)/shard_map/ppermute | solution.py:201
  67.8 26.5 %copy-start.9 = (bf16[2,4,128,128]{3,2,1,0:T(8,128)(2,1)}, bf16[2,4,128,128]{3,2,1,0:T(8,128)(2,1)S(1)}, u32[]{:S(2)}) copy-start(bf16[2,4,128,128]{3,2,1,0:T(8,128)(2,1)S(1)} %collective-permute-done.2.refs_2_) | copy-start | bytes 786436
  67.8 26.5 %copy-start.10 = (bf16[2,4,128,128]{3,2,1,0:T(8,128)(2,1)}, bf16[2,4,128,128]{3,2,1,0:T(8,128)(2,1)S(1)}, u32[]{:S(2)}) copy-start(bf16[2,4,128,128]{3,2,1,0:T(8,128)(2,1)S(1)} %collective-permute-done.3.refs_6_) | copy-start | bytes 786436
  69.2 20.4 %all-to-all-start.3 = ((bf16[8,128,512]{2,1,0:T(8,128)(2,1)}), bf16[8,128,512]{2,1,0:T(8,128)(2,1)S(1)}, u32[]{:S(2)}, u32[]{:S(2)}) async-start(bf16[8,128,512]{2,1,0:T(8,128)(2,1)} %bitcast.11), calls=%async_computation.3 | async-start | bytes 2097152 | tf_op jit(solution)/shard_map/all_to_all | solution.py:193
  74.6 11.0 %collective-permute-start.5 = (bf16[2,4,128,128]{3,2,1,0:T(8,128)(2,1)S(1)}, bf16[2,4,128,128]{3,2,1,0:T(8,128)(2,1)S(1)}, u32[]{:S(2)}, u32[]{:S(2)}) collective-permute-start(bf16[2,4,128,128]{3,2,1,0:T(8,128)(2,1)S(1)} %collective-permute-done.2.refs_2_), channel_id=1, source_target_pairs={{0,8},{8,16},{16,24},{24,32},{32,40},{40,48},{48,56},{56,0},{1,9},... | collective-permute-start | bytes 786440 | tf_op jit(solution)/shard_map/ppermute | solution.py:201
  77.7 9.4 %collective-permute-start.6 = (bf16[2,4,128,128]{3,2,1,0:T(8,128)(2,1)S(1)}, bf16[2,4,128,128]{3,2,1,0:T(8,128)(2,1)S(1)}, u32[]{:S(2)}, u32[]{:S(2)}) collective-permute-start(bf16[2,4,128,128]{3,2,1,0:T(8,128)(2,1)S(1)} %collective-permute-done.3.refs_6_), channel_id=1, source_target_pairs={{0,56},{8,0},{16,8},{24,16},{32,24},{40,32},{48,40},{56,48},{1,57}... | collective-permute-start | bytes 786440 | tf_op jit(solution)/shard_map/ppermute | solution.py:201
  81.1 0.7 collective-permute-start.4
  85.5 28.5 %copy-start.11 = (bf16[2,4,128,128]{3,2,1,0:T(8,128)(2,1)}, bf16[2,4,128,128]{3,2,1,0:T(8,128)(2,1)S(1)}, u32[]{:S(2)}) copy-start(bf16[2,4,128,128]{3,2,1,0:T(8,128)(2,1)S(1)} %collective-permute-done.5.refs_3_) | copy-start | bytes 786436
  87.1 26.8 %copy-start.12 = (bf16[2,4,128,128]{3,2,1,0:T(8,128)(2,1)}, bf16[2,4,128,128]{3,2,1,0:T(8,128)(2,1)S(1)}, u32[]{:S(2)}) copy-start(bf16[2,4,128,128]{3,2,1,0:T(8,128)(2,1)S(1)} %collective-permute-done.6.refs_5_) | copy-start | bytes 786436
  89.5 1.0 copy-start.3
  94.3 27.5 %collective-permute-start.9 = (bf16[512,1024]{1,0:T(8,128)(2,1)}, bf16[512,1024]{1,0:T(8,128)(2,1)S(1)}, u32[]{:S(2)}, u32[]{:S(2)}) collective-permute-start(bf16[512,1024]{1,0:T(8,128)(2,1)} %top.1.top_own), channel_id=1, source_target_pairs={{0,4},{4,0},{1,5},{5,1},{2,6},{6,2},{3,7},{7,3},{8,12},{12,8},{9,1... | collective-permute-start | bytes 3145736 | tf_op jit(solution)/shard_map/ppermute | solution.py:292
  96.6 17.4 %collective-permute-start.7 = (bf16[2,4,128,128]{3,2,1,0:T(8,128)(2,1)S(1)}, bf16[2,4,128,128]{3,2,1,0:T(8,128)(2,1)S(1)}, u32[]{:S(2)}, u32[]{:S(2)}) collective-permute-start(bf16[2,4,128,128]{3,2,1,0:T(8,128)(2,1)S(1)} %collective-permute-done.5.refs_3_), channel_id=1, source_target_pairs={{0,8},{8,16},{16,24},{24,32},{32,40},{40,48},{48,56},{56,0},{1,9},... | collective-permute-start | bytes 786440 | tf_op jit(solution)/shard_map/ppermute | solution.py:201
  100.6 30.5 %all-to-all-start.4 = ((bf16[8,256,128]{2,1,0:T(8,128)(2,1)}), bf16[8,256,128]{2,1,0:T(8,128)(2,1)S(1)}, u32[]{:S(2)}, u32[]{:S(2)}) async-start(bf16[8,256,128]{2,1,0:T(8,128)(2,1)} %broadcast_in_dim.14), calls=%async_computation.4 | async-start | bytes 1048576 | tf_op jit(solution)/shard_map/all_to_all | solution.py:193
  114.0 0.7 copy-start.13
  119.1 11.9 %copy-start.14 = (bf16[2,1024,128]{2,1,0:T(8,128)(2,1)S(1)}, bf16[2,1024,128]{2,1,0:T(8,128)(2,1)}, u32[]{:S(2)}) copy-start(bf16[2,1024,128]{2,1,0:T(8,128)(2,1)} %param.12) | copy-start | bytes 1572868
  119.1 19.5 %collective-permute-start.8 = (bf16[1024,512]{1,0:T(8,128)(2,1)}, bf16[1024,512]{1,0:T(8,128)(2,1)S(1)}, u32[]{:S(2)}, u32[]{:S(2)}) collective-permute-start(bf16[1024,512]{1,0:T(8,128)(2,1)} %first.1.first_own), channel_id=1, source_target_pairs={{0,4},{4,0},{1,5},{5,1},{2,6},{6,2},{3,7},{7,3},{8,12},{12,8},{9,1... | collective-permute-start | bytes 3145736 | tf_op jit(solution)/shard_map/ppermute | solution.py:297
  121.8 1.1 copy-start.4
  129.1 9.5 %collective-permute-start.10 = (bf16[1024,512]{1,0:T(8,128)(2,1)}, bf16[1024,512]{1,0:T(8,128)(2,1)S(1)}, u32[]{:S(2)}, u32[]{:S(2)}) collective-permute-start(bf16[1024,512]{1,0:T(8,128)(2,1)} %second.1.second_own), channel_id=1, source_target_pairs={{0,4},{4,0},{1,5},{5,1},{2,6},{6,2},{3,7},{7,3},{8,12},{12,8},{9,1... | collective-permute-start | bytes 3145736 | tf_op jit(solution)/shard_map/ppermute | solution.py:303
  138.6 1.0 copy-start.5
  138.7 1.3 copy-start.6
Sparse Core Ops, SparseCore 0:
  10.1 64.4 all-gather.1

commit v5 on v3

--- a/solution.py
+++ b/solution.py
@@ -12,27 +12,87 @@
 TILE = 256
 
 
-def factor_kernel(ys, at_ref, whole, *refs):
-    pieces, others, refs = refs[:ys], refs[ys : 2 * ys], refs[2 * ys :]
+def start_copies(pairs, sems):
+    copies = [pltpu.make_async_copy(src, dst, sems.at[i]) for i, (src, dst) in enumerate(pairs)]
+    for copy in copies:
+        copy.start()
+    return copies
+
+
+def wait(copies):
+    for copy in copies:
+        copy.wait()
+
+
+def pack_kernel(top, low, following, sent):
+    cores, voxes = sent.shape[:2]
+    cols = sent.shape[-1]
+    for core in range(cores):
+        for vox in range(voxes):
+            for j in range(voxes):
+                chunk = core * voxes + j
+                at = slice(chunk * cols, (chunk + 1) * cols)
+                sent[core, vox, j] = top[chunk]
+                sent[core, vox, voxes + j] = low[:, at]
+                sent[core, vox, 2 * voxes + j] = following[:, at]
+            chunk = core * voxes + vox
+            at = slice(chunk * cols, (chunk + 1) * cols)
+            sent[core, vox, 3 * voxes] = low[:, at]
+            sent[core, vox, 3 * voxes + 1] = following[:, at]
+
+
+def unpack_kernel(got, mine, single):
+    group, slots = got.shape[:2]
+    for src in range(group):
+        for j in range(slots - 2):
+            mine[j, src] = got[src, j]
+        single[src, 0] = got[src, slots - 2]
+        single[src, 1] = got[src, slots - 1]
+
+
+def stack_kernel(*refs):
+    pieces, stacked, sems = refs[:-2], refs[-2], refs[-1]
+    wait(start_copies([(ref, stacked.at[i]) for i, ref in enumerate(pieces)], sems))
+
+
+def order_kernel(at_ref, *refs):
+    pieces, stacked, sems = refs[:-2], refs[-2], refs[-1]
+    n = len(pieces)
+    wait(
+        start_copies(
+            [(ref, stacked.at[lax.rem(at_ref[3] + (n - k), n)]) for k, ref in enumerate(pieces)],
+            sems,
+        )
+    )
+
+
+def factor_kernel(near, ys, at_ref, inv_own, inv_other, *refs):
+    pieces, refs = refs[:ys], refs[ys:]
+    far_near, far_rest, refs = refs[0], refs[1], refs[2:]
+    others = {k: (far_near, i) for i, k in enumerate(near)}
+    others |= {k: (far_rest, i) for i, k in enumerate(k for k in range(ys) if k not in near)}
     side_one, side_two, gram, right, factor, solved, trailing, residual = refs[:8]
     inv, panels, side, minuend, top, first, updated, second, sems = refs[8:]
     y, core, own = at_ref[0], at_ref[1], at_ref[2]
     size = first.shape[0]
+    voxes = panels.shape[1] // 2
     f32, bf16 = jnp.float32, jnp.bfloat16
 
     inv_copies = [
-        pltpu.make_async_copy(whole.at[0], inv.at[0], sems.at[0]),
-        pltpu.make_async_copy(whole.at[1], inv.at[1], sems.at[1]),
+        pltpu.make_async_copy(inv_own, inv.at[core], sems.at[0]),
+        pltpu.make_async_copy(inv_other, inv.at[1 - core], sems.at[1]),
     ]
     panel_copies = [[], [], []]
     for p in range(3):
+        part = slice(p * voxes, (p + 1) * voxes)
         for k in range(ys):
             spot = lax.rem(y + (ys - k), ys)
-            for ref, half in ((pieces[k], core), (others[k], 1 - core)):
+            far, i = others[k]
+            for ref, half in ((pieces[k].at[part], core), (far.at[i, part], 1 - core)):
                 panel_copies[p].append(
                     pltpu.make_async_copy(
-                        ref.at[:, p],
-                        panels.at[p, spot, half],
+                        ref,
+                        panels.at[p, pl.ds(half * voxes, voxes), spot],
                         sems.at[2 + 2 * ys * p + len(panel_copies[p])],
                     )
                 )
@@ -50,7 +110,8 @@
         copy.wait()
 
     def inverse(k, i):
-        return inv[k, i * TILE : (i + 1) * TILE, : (i + 1) * TILE]
+        rows = inv[k, 2 * i : 2 * i + 2].reshape(TILE, size)
+        return rows[:, : (i + 1) * TILE]
 
     def lower(k, load, store):
         for i in range(size // TILE):
@@ -59,7 +120,10 @@
     def at(t):
         return pl.ds(pl.multiple_of(t * TILE, TILE), TILE)
 
-    flat = panels.reshape(3, size, size)
+    flat = panels.reshape(panels.shape[:2] + (size, panels.shape[-1]))
+
+    def tile(p, rows, t):
+        return jnp.concatenate([flat[p, 2 * t, rows], flat[p, 2 * t + 1, rows]], axis=1)
 
     for copy in panel_copies[0]:
         copy.wait()
@@ -69,7 +133,7 @@
         def store(i, x):
             top[at(t), i * TILE : (i + 1) * TILE] = x.astype(bf16).T
 
-        lower(0, lambda n: flat[0, :n, at(t)], store)
+        lower(0, lambda n: tile(0, slice(n), t), store)
 
     for copy in panel_copies[1] + side_copies:
         copy.wait()
@@ -79,7 +143,7 @@
         def store(i, x):
             first[i * TILE : (i + 1) * TILE, at(t)] = x.astype(bf16)
 
-        lower(0, lambda n: flat[1, :n, at(t)], store)
+        lower(0, lambda n: tile(1, slice(n), t), store)
 
     def store_side_one(i, x):
         first[i * TILE : (i + 1) * TILE, size:] = x.astype(bf16)
@@ -98,7 +162,7 @@
 
     @pl.loop(0, size // TILE)
     def _(t):
-        subtract(lambda rows: flat[2, rows, at(t)], at(t))
+        subtract(lambda rows: tile(2, rows, t), at(t))
 
         def store(i, x):
             second[i * TILE : (i + 1) * TILE, at(t)] = x.astype(bf16)
@@ -131,14 +195,43 @@
         residual[at(t), :] = minuend[1, at(t), :].astype(f32) - change[:, TILE // 2 :]
 
 
+def exchange(blocks, axis):
+    flat = blocks.reshape(blocks.shape[0], -1, blocks.shape[-1])
+    return lax.all_to_all(flat, axis, 0, 0, tiled=True).reshape(blocks.shape)
+
+
 def gather_small(block, axis, size):
-    flat = block.reshape(1, -1, block.shape[-1])
-    out = lax.all_to_all(jnp.tile(flat, (size, 1, 1)), axis, 0, 0, tiled=True)
-    return out.reshape((size,) + block.shape)
+    return exchange(jnp.broadcast_to(block[None], (size,) + block.shape), axis)
 
 
 def shift(block, axis, size, by):
     return lax.ppermute(block, axis, [(i, (i + by) % size) for i in range(size)])
+
+
+def call(body, name, outs, *operands):
+    local = pl.BlockSpec(memory_space=pltpu.VMEM)
+    return pl.pallas_call(
+        body,
+        name=name,
+        out_shape=tuple(jax.ShapeDtypeStruct(shape, dtype) for shape, dtype in outs),
+        in_specs=[local] * len(operands),
+        out_specs=(local,) * len(outs),
+        compiler_params=pltpu.CompilerParams(vmem_limit_bytes=2 << 20),
+    )(*operands)
+
+
+def stack(pieces, where=None):
+    anywhere = pl.BlockSpec(memory_space=pl.ANY)
+    extra = [] if where is None else [where]
+    return pl.pallas_call(
+        stack_kernel if where is None else order_kernel,
+        name="stack" if where is None else "order",
+        out_shape=jax.ShapeDtypeStruct((len(pieces),) + pieces[0].shape, pieces[0].dtype),
+        in_specs=[pl.BlockSpec(memory_space=pltpu.SMEM)] * len(extra) + [anywhere] * len(pieces),
+        out_specs=anywhere,
+        scratch_shapes=[pltpu.SemaphoreType.DMA((len(pieces),))],
+        compiler_params=pltpu.CompilerParams(vmem_limit_bytes=1 << 20),
+    )(*extra, *pieces)
 
 
 def per_device(sizes, panel_top, panel_low, panel_next, gram_rest, inverses, right_top, right_low):
@@ -153,58 +246,81 @@
     bf16 = jnp.bfloat16
     other = [(0, 1), (1, 0)]
 
-    whole = lax.all_gather(inverses, "row", axis=1, tiled=True)
-    low, following = panel_low.T, panel_next.T
-    pair = jnp.stack([low, following])
-    swapped = lax.ppermute(pair, axes, swap)
-
-    top = gather_small(panel_top.T, "row", rows).transpose(1, 0, 2).reshape(width, -1)
-    top, swapped = lax.optimization_barrier((top, swapped))
-    panels = gather_small(jnp.stack([top, low, following]), "vox", voxes)
-    blocks = swapped.reshape(2, width, cores * voxes, cols).transpose(2, 0, 1, 3)
-
-    up = down = panels
-    pieces, others = {0: panels}, {}
-    for k in range(1, ys // 2 + 1):
-        if k == 2:
-            up, down, blocks = lax.optimization_barrier((up, down, blocks))
-        if k == 4:
-            up, matching, whole = lax.optimization_barrier((up, matching, whole))
-        if k == 1:
-            blocks = lax.all_to_all(blocks, ("core", "vox"), 0, 0, tiled=True)
-        if k == 2:
-            matching = gather_small(blocks, "row", rows)
-        pieces[k] = up = shift(up, "y", ys, 1)
-        if k < ys - k:
-            pieces[ys - k] = down = shift(down, "y", ys, -1)
-    for k in range(ys):
-        others[k] = lax.ppermute(pieces[k], "core", other)
-    matching = jnp.moveaxis(matching, 2, 0)
-    matching = matching.reshape(2, size, cols)
+    own = ((y * cores + core) * voxes + vox) * width
+    where = jnp.stack([y, core, own, z]).astype(jnp.int32)
+    barrier = lax.optimization_barrier
+    group = cores * voxes
+    flats = [panel_low.T, panel_next.T]
+
+    def ring(pieces, k, axis, n):
+        up = pieces[k] = shift(pieces[k - 1], axis, n, 1)
+        if k == n - k:
+            return [up]
+        down = pieces[n - k] = shift(pieces[(n - k + 1) % n], axis, n, -1)
+        return [up, down]
+
+    def ordered(values, pieces, k, n):
+        keys = sorted({k, n - k})
+        values, held = barrier((values, [pieces[i] for i in keys]))
+        for i, piece in zip(keys, held):
+            pieces[i] = piece
+        return values
+
+    invs = {0: lax.dynamic_index_in_dim(inverses, core, 0, False)}
+    ring(invs, 1, "row", rows)
+    top = gather_small(panel_top.T, "row", rows)
+    top = ordered(top, invs, 1, rows)
+    ring(invs, 2, "row", rows)
+    (sent,) = call(
+        pack_kernel, "pack", [((cores, voxes, 3 * voxes + 2, width, cols), bf16)], top, *flats
+    )
+    got = exchange(sent.reshape((group,) + sent.shape[2:]), ("core", "vox"))
+    mine, single = call(
+        unpack_kernel, "unpack",
+        [((3 * voxes, group, width, cols), bf16), ((group, 2, width, cols), bf16)], got,
+    )
+    pieces = {0: mine.reshape(3 * voxes, group * width, cols)}
+    pieces[0], single = ordered((pieces[0], single), invs, 2, rows)
+    ring(pieces, 1, "y", ys)
+    swapped = lax.ppermute(single, axes, swap)
+    ring(invs, 3, "row", rows)
+    swapped = ordered(ordered(swapped, invs, 3, rows), pieces, 1, ys)
+    ring(pieces, 2, "y", ys)
+    ring(invs, 4, "row", rows)
+    matching = gather_small(swapped, "row", rows)
+    invs[4] = ordered(invs[4], pieces, 2, ys)
+    ring(pieces, 3, "y", ys)
+    near = sorted(k % ys for k in range(-2, 3))
+    far_near = lax.ppermute(stack([pieces[k] for k in near]), "core", other)
+    inv_own = stack([invs[k] for k in range(rows)], where)
+    inv_own, matching = ordered((inv_own, matching), pieces, 3, ys)
+    inv_other = lax.ppermute(inv_own, "core", other)
+    ring(pieces, 4, "y", ys)
+    rest = [pieces[k] for k in range(ys) if k not in near]
+    far_rest = lax.ppermute(stack(rest), "core", other)
+
+    matching = jnp.moveaxis(matching, 2, 0).reshape(2, size, cols)
     sides = [jnp.concatenate([matching[k], right_top[k]], axis=1) for k in range(2)]
     pieces = [pieces[k] for k in range(ys)]
-    others = [others[k] for k in range(ys)]
-
-    own = ((y * cores + core) * voxes + vox) * width
-    where = jnp.stack([y, core, own]).astype(jnp.int32)
+
     height = panel_low.shape[0]
     any_space = pl.BlockSpec(memory_space=pl.ANY)
     local = pl.BlockSpec(memory_space=pltpu.VMEM)
     vmem = pltpu.VMEM
     flops = 2 * size * size * (2 * size + TILE + 2 * (size + TILE) + 2 * TILE)
     factor, solved, trailing, residual = pl.pallas_call(
-        functools.partial(factor_kernel, ys),
+        functools.partial(factor_kernel, near, ys),
         out_shape=(
             jax.ShapeDtypeStruct((2, width, height), bf16),
             jax.ShapeDtypeStruct((2, size, cols), bf16),
             jax.ShapeDtypeStruct((height, cols), jnp.float32),
             jax.ShapeDtypeStruct((height, cols), jnp.float32),
         ),
-        in_specs=[pl.BlockSpec(memory_space=pltpu.SMEM)] + [any_space] * (5 + 2 * ys),
+        in_specs=[pl.BlockSpec(memory_space=pltpu.SMEM)] + [any_space] * (8 + ys),
         out_specs=(local,) * 4,
         scratch_shapes=[
-            vmem((2, size, size), bf16),
-            vmem((3, ys, cores, voxes, width, height), bf16),
+            vmem((2, rows, size // rows, size), bf16),
+            vmem((3, cores * voxes, ys, group * width, cols), bf16),
             vmem((2, size, TILE), bf16),
             vmem((2, height, cols), bf16),
             vmem((size, size), bf16),
@@ -216,7 +332,7 @@
         compiler_params=pltpu.CompilerParams(vmem_limit_bytes=40 * 1024 * 1024),
         cost_estimate=pl.CostEstimate(flops=flops, bytes_accessed=14 << 20, transcendentals=0),
         name="factor_and_update",
-    )(where, whole, *pieces, *others, *sides, gram_rest, right_low)
+    )(where, inv_own, inv_other, *pieces, far_near, far_rest, *sides, gram_rest, right_low)
     return (factor.transpose(0, 2, 1), solved, trailing, residual)
 
 

time: 143 us -> 166 us (1.16); the launches traced: 142 us -> 163 us
  starting transfers between devices: 67.1 us -> 84.4 us
  waiting for transfers between devices: 14 us -> 28.6 us
  between operations: 14.3 us -> 1.09 us
  blocking collectives: 21.2 us -> 10.6 us
  local copies, waits for them, and re-layouts: 6.43 us -> 16.9 us
  Pallas kernels: 17.4 us -> 21.7 us
    ppermute x7 -> x14, starting transfers between devices: 24.4 us -> 54.3 us  [shift(): lax.ppermute(block, axis, [(i, (i + by) % size) for i in range(size)])]
    ppermute x7 -> x14, waiting for transfers between devices: 7.66 us -> 24.9 us  [shift(): lax.ppermute(block, axis, [(i, (i + by) % size) for i in range(size)])]
    unnamed x7 -> x54, local copies, waits for them, and re-layouts: 1.92 us -> 14.1 us
    all_to_all x2 -> x1, blocking collectives: 21.2 us -> 10.6 us  [exchange(): return lax.all_to_all(flat, axis, 0, 0, tiled=True).reshape(blocks.shape)]
    ppermute x9 -> x4, starting transfers between devices: 20.8 us -> 10.9 us  [the longest x1 5.13 us: per_device(): inv_other = lax.ppermute(inv_own, 'core', other)]
    pallas_call x1 -> x6, Pallas kernels: 17.4 us -> 21.7 us  [the longest x1 17.1 us: per_device(): pl.pallas_call(functools.partial(factor_kernel, near, ys), out_shape=(jax...]
    all_to_all x2, waiting for transfers between devices: 5.44 us -> 2.47 us  [exchange(): return lax.all_to_all(flat, axis, 0, 0, tiled=True).reshape(blocks.shape)]
    all_to_all x2, starting transfers between devices: 21.9 us -> 19.2 us  [exchange(): return lax.all_to_all(flat, axis, 0, 0, tiled=True).reshape(blocks.shape)]
  transfers between devices with their start and end apart: 19 -> 20, of which waited for: 4 -> 8; matrix products, arithmetic and copies ran while one was open for 4% -> 1% of each run, Pallas kernels for 0% -> 2%
where the time goes in v5:
time: 166 us; the launch traced here: 163 us
  starting transfers between devices  84.4 us (51%)
  waiting for transfers between devices  28.6 us (17%)
  Pallas kernels  21.7 us (13%)
  local copies, waits for them, and re-layouts  16.9 us (10%)
  blocking collectives  10.6 us (6%)
    ppermute x14, starting transfers between devices, shift(): lax.ppermute(block, axis, [(i, (i + by) % size) for i in range(size)])  54.3 us
    ppermute x14, waiting for transfers between devices, shift(): lax.ppermute(block, axis, [(i, (i + by) % size) for i in range(size)])  24.9 us
    all_to_all x2, starting transfers between devices, exchange(): return lax.all_to_all(flat, axis, 0, 0, tiled=True).reshape(blocks.shape)  19.2 us
    pallas_call x1, Pallas kernels, per_device(): pl.pallas_call(functools.partial(factor_kernel, near, ys), out_shape=(jax...  17.1 us
    unnamed x54, local copies, waits for them, and re-layouts  14.1 us
    all_to_all x1, blocking collectives, exchange(): return lax.all_to_all(flat, axis, 0, 0, tiled=True).reshape(blocks.shape)  10.6 us
    ppermute x1, starting transfers between devices, per_device(): inv_other = lax.ppermute(inv_own, 'core', other)  5.13 us
    pallas_call x3, Pallas kernels, stack(): pl.pallas_call(stack_kernel if where is None else order_kernel, name='sta...  3.71 us
  transfers between devices with their start and end apart: 20, of which 8 were waited for; matrix products, arithmetic and copies ran while one was open for 1% of the time, Pallas kernels for 2%

profile of v5, /device:TPU:1, one launch (start us, length us, event | category | flops | bytes accessed | tf_op | source)
XLA Modules:
  0.0 163.5 jit_solution(15470296216202682440)
XLA Ops:
  0.7 1.0 copy-done
  1.7 11.5 %collective-permute-start.1 = (bf16[128,1024]{1,0:T(8,128)(2,1)S(1)}, bf16[128,1024]{1,0:T(8,128)(2,1)S(1)}, u32[]{:S(2)}, u32[]{:S(2)}) collective-permute-start(bf16[128,1024]{1,0:T(8,128)(2,1)S(1)} %dynamic-slice_bitcast_fusion.refs_0_), channel_id=1, source_target_pairs={{0,448},{64,0},{128,64},{192,128},{256,192},{320,256},{384,320},{4... | collective-permute-start | bytes 786440 | tf_op jit(solution)/shard_map/ppermute | solution.py:208
  13.2 1.9 %collective-permute-start = (bf16[128,1024]{1,0:T(8,128)(2,1)S(1)}, bf16[128,1024]{1,0:T(8,128)(2,1)S(1)}, u32[]{:S(2)}, u32[]{:S(2)}) collective-permute-start(bf16[128,1024]{1,0:T(8,128)(2,1)S(1)} %dynamic-slice_bitcast_fusion.refs_0_), channel_id=1, source_target_pairs={{0,64},{64,128},{128,192},{192,256},{256,320},{320,384},{384,448},... | collective-permute-start | bytes 786440 | tf_op jit(solution)/shard_map/ppermute | solution.py:208
  15.8 10.6 %all_to_all.15.top = bf16[8,16,128]{2,1,0:T(8,128)(2,1)S(1)} all-to-all(bf16[8,16,128]{2,1,0:T(8,128)(2,1)S(1)} %broadcast_in_dim.6), channel_id=1, replica_groups=mesh['row'=8,'y'=8,'core'=2,'vox'=4] {'row'}, dimensions={0} | all-to-all | bytes 65536 | tf_op jit(solution)/shard_map/all_to_all | solution.py:200
  26.5 0.7 copy-done.22
  27.2 0.8 copy-done.23
  28.0 0.8 pack.1
  28.8 6.9 %all-to-all-start.1 = ((bf16[8,224,128]{2,1,0:T(8,128)(2,1)}), bf16[8,224,128]{2,1,0:T(8,128)(2,1)S(1)}, u32[]{:S(2)}, u32[]{:S(2)}) async-start(bf16[8,224,128]{2,1,0:T(8,128)(2,1)} %bitcast.8), calls=%async_computation.1 | async-start | bytes 917504 | tf_op jit(solution)/shard_map/all_to_all | solution.py:200
  35.8 2.2 %collective-permute-start.2 = (bf16[128,1024]{1,0:T(8,128)(2,1)S(1)}, bf16[128,1024]{1,0:T(8,128)(2,1)S(1)}, u32[]{:S(2)}, u32[]{:S(2)}) collective-permute-start(bf16[128,1024]{1,0:T(8,128)(2,1)S(1)} %collective-permute-done.refs_1_), channel_id=1, source_target_pairs={{0,64},{64,128},{128,192},{192,256},{256,320},{320,384},{384,448},... | collective-permute-start | bytes 786440 | tf_op jit(solution)/shard_map/ppermute | solution.py:208
  37.9 4.3 %collective-permute-start.3 = (bf16[128,1024]{1,0:T(8,128)(2,1)S(1)}, bf16[128,1024]{1,0:T(8,128)(2,1)S(1)}, u32[]{:S(2)}, u32[]{:S(2)}) collective-permute-start(bf16[128,1024]{1,0:T(8,128)(2,1)S(1)} %collective-permute-done.1.refs_7_), channel_id=1, source_target_pairs={{0,448},{64,0},{128,64},{192,128},{256,192},{320,256},{384,320},{4... | collective-permute-start | bytes 786440 | tf_op jit(solution)/shard_map/ppermute | solution.py:208
  42.2 2.5 %all-to-all-done.1 = bf16[8,224,128]{2,1,0:T(8,128)(2,1)S(1)} async-done(((bf16[8,224,128]{2,1,0:T(8,128)(2,1)}), bf16[8,224,128]{2,1,0:T(8,128)(2,1)S(1)}, u32[]{:S(2)}, u32[]{:S(2)}) %all-to-all-start.1) | async-done | bytes 458784 | tf_op jit(solution)/shard_map/all_to_all | solution.py:200
  44.8 2.0 %collective-permute-done.2.refs_2_ = bf16[128,1024]{1,0:T(8,128)(2,1)S(1)} collective-permute-done((bf16[128,1024]{1,0:T(8,128)(2,1)S(1)}, bf16[128,1024]{1,0:T(8,128)(2,1)S(1)}, u32[]{:S(2)}, u32[]{:S(2)}) %collective-permute-start.2) | collective-permute-done | bytes 262176 | tf_op jit(solution)/shard_map/ppermute | solution.py:208
  46.8 0.9 collective-permute-done.3.refs_6_
  47.6 5.1 %collective-permute-start.9 = (bf16[12,128,128]{2,1,0:T(8,128)(2,1)S(1)}, bf16[12,128,128]{2,1,0:T(8,128)(2,1)S(1)}, u32[]{:S(2)}, u32[]{:S(2)}) collective-permute-start(bf16[12,128,128]{2,1,0:T(8,128)(2,1)S(1)} %bitcast.23), channel_id=1, source_target_pairs={{0,56},{8,0},{16,8},{24,16},{32,24},{40,32},{48,40},{56,48},{1,57}... | collective-permute-start | bytes 1179656 | tf_op jit(solution)/shard_map/ppermute | solution.py:208
  52.7 1.9 %collective-permute-start.8 = (bf16[12,128,128]{2,1,0:T(8,128)(2,1)S(1)}, bf16[12,128,128]{2,1,0:T(8,128)(2,1)S(1)}, u32[]{:S(2)}, u32[]{:S(2)}) collective-permute-start(bf16[12,128,128]{2,1,0:T(8,128)(2,1)S(1)} %bitcast.24), channel_id=1, source_target_pairs={{0,8},{8,16},{16,24},{24,32},{32,40},{40,48},{48,56},{56,0},{1,9},... | collective-permute-start | bytes 1179656 | tf_op jit(solution)/shard_map/ppermute | solution.py:208
  54.7 0.7 copy-done.1
  55.4 1.9 %collective-permute-start.5 = (bf16[128,1024]{1,0:T(8,128)(2,1)S(1)}, bf16[128,1024]{1,0:T(8,128)(2,1)S(1)}, u32[]{:S(2)}, u32[]{:S(2)}) collective-permute-start(bf16[128,1024]{1,0:T(8,128)(2,1)S(1)} %collective-permute-done.2.refs_2_), channel_id=1, source_target_pairs={{0,64},{64,128},{128,192},{192,256},{256,320},{320,384},{384,448},... | collective-permute-start | bytes 786440 | tf_op jit(solution)/shard_map/ppermute | solution.py:208
  58.0 5.3 %collective-permute-start.6 = (bf16[128,1024]{1,0:T(8,128)(2,1)S(1)}, bf16[128,1024]{1,0:T(8,128)(2,1)S(1)}, u32[]{:S(2)}, u32[]{:S(2)}) collective-permute-start(bf16[128,1024]{1,0:T(8,128)(2,1)S(1)} %collective-permute-done.3.refs_6_), channel_id=1, source_target_pairs={{0,448},{64,0},{128,64},{192,128},{256,192},{320,256},{384,320},{4... | collective-permute-start | bytes 786440 | tf_op jit(solution)/shard_map/ppermute | solution.py:208
  64.7 1.2 collective-permute-done.5.refs_3_
  66.0 1.6 collective-permute-done.6.refs_5_
  67.6 1.0 broadcast_in_dim.16
  68.5 12.3 %all-to-all-start.2 = ((bf16[8,256,128]{2,1,0:T(8,128)(2,1)}), bf16[8,256,128]{2,1,0:T(8,128)(2,1)}, u32[]{:S(2)}, u32[]{:S(2)}) async-start(bf16[8,256,128]{2,1,0:T(8,128)(2,1)} %broadcast_in_dim.16), calls=%async_computation.2 | async-start | bytes 1048576 | tf_op jit(solution)/shard_map/all_to_all | solution.py:200
  80.8 1.9 %collective-permute-start.10 = (bf16[12,128,128]{2,1,0:T(8,128)(2,1)S(1)}, bf16[12,128,128]{2,1,0:T(8,128)(2,1)}, u32[]{:S(2)}, u32[]{:S(2)}) collective-permute-start(bf16[12,128,128]{2,1,0:T(8,128)(2,1)S(1)} %collective-permute-done.8.refs_1_), channel_id=1, source_target_pairs={{0,8},{8,16},{16,24},{24,32},{32,40},{40,48},{48,56},{56,0},{1,9},... | collective-permute-start | bytes 1179656 | tf_op jit(solution)/shard_map/ppermute | solution.py:208
  82.7 4.6 %collective-permute-start.11 = (bf16[12,128,128]{2,1,0:T(8,128)(2,1)S(1)}, bf16[12,128,128]{2,1,0:T(8,128)(2,1)}, u32[]{:S(2)}, u32[]{:S(2)}) collective-permute-start(bf16[12,128,128]{2,1,0:T(8,128)(2,1)S(1)} %collective-permute-done.9.refs_4_.refs_7_), channel_id=1, source_target_pairs={{0,56},{8,0},{16,8},{24,16},{32,24},{40,32},{48,40},{56,48},{1,57}... | collective-permute-start | bytes 1179656 | tf_op jit(solution)/shard_map/ppermute | solution.py:208
  87.3 3.4 %collective-permute-start.7 = (bf16[128,1024]{1,0:T(8,128)(2,1)S(1)}, bf16[128,1024]{1,0:T(8,128)(2,1)S(1)}, u32[]{:S(2)}, u32[]{:S(2)}) collective-permute-start(bf16[128,1024]{1,0:T(8,128)(2,1)S(1)} %collective-permute-done.5.refs_3_), channel_id=1, source_target_pairs={{0,64},{64,128},{128,192},{192,256},{256,320},{320,384},{384,448},... | collective-permute-start | bytes 786440 | tf_op jit(solution)/shard_map/ppermute | solution.py:208
  90.7 8.9 %collective-permute-done.7.refs_4_ = bf16[128,1024]{1,0:T(8,128)(2,1)S(1)} collective-permute-done((bf16[128,1024]{1,0:T(8,128)(2,1)S(1)}, bf16[128,1024]{1,0:T(8,128)(2,1)S(1)}, u32[]{:S(2)}, u32[]{:S(2)}) %collective-permute-start.7) | collective-permute-done | bytes 262176 | tf_op jit(solution)/shard_map/ppermute | solution.py:208
  100.3 1.9 %collective-permute-start.12 = (bf16[12,128,128]{2,1,0:T(8,128)(2,1)}, bf16[12,128,128]{2,1,0:T(8,128)(2,1)S(1)}, u32[]{:S(2)}, u32[]{:S(2)}) collective-permute-start(bf16[12,128,128]{2,1,0:T(8,128)(2,1)} %collective-permute-done.10.refs_2_), channel_id=1, source_target_pairs={{0,8},{8,16},{16,24},{24,32},{32,40},{40,48},{48,56},{56,0},{1,9},... | collective-permute-start | bytes 1179656 | tf_op jit(solution)/shard_map/ppermute | solution.py:208
  102.2 4.6 %collective-permute-start.13 = (bf16[12,128,128]{2,1,0:T(8,128)(2,1)}, bf16[12,128,128]{2,1,0:T(8,128)(2,1)}, u32[]{:S(2)}, u32[]{:S(2)}) collective-permute-start(bf16[12,128,128]{2,1,0:T(8,128)(2,1)} %collective-permute-done.11.refs_3_.refs_6_), channel_id=1, source_target_pairs={{0,56},{8,0},{16,8},{24,16},{32,24},{40,32},{48,40},{56,48},{1,57}... | collective-permute-start | bytes 1179656 | tf_op jit(solution)/shard_map/ppermute | solution.py:208
  106.9 0.9 copy-done.11
  107.9 0.9 copy-done.13
  108.8 0.9 copy-done.15
  109.8 0.9 copy-done.17
  110.7 0.9 copy-done.19
  111.7 0.9 copy-done.21
  112.6 0.8 order.1.inv_own
  113.5 5.1 %collective-permute-start.14 = (bf16[8,128,1024]{2,1,0:T(8,128)(2,1)S(1)}, bf16[8,128,1024]{2,1,0:T(8,128)(2,1)S(1)}, u32[]{:S(2)}, u32[]{:S(2)}) collective-permute-start(bf16[8,128,1024]{2,1,0:T(8,128)(2,1)S(1)} %order.1.inv_own), channel_id=1, source_target_pairs={{0,4},{4,0},{1,5},{5,1},{2,6},{6,2},{3,7},{7,3},{8,12},{12,8},{9,1... | collective-permute-start | bytes 6291464 | tf_op jit(solution)/shard_map/ppermute | solution.py:297
  118.6 1.0 copy-done.2
  119.6 1.0 copy-done.5
  120.6 1.0 copy-done.8
  121.6 1.5 stack.22
  123.1 2.1 %collective-permute-start.16 = (bf16[5,12,128,128]{3,2,1,0:T(8,128)(2,1)S(1)}, bf16[5,12,128,128]{3,2,1,0:T(8,128)(2,1)S(1)}, u32[]{:S(2)}, u32[]{:S(2)}) collective-permute-start(bf16[5,12,128,128]{3,2,1,0:T(8,128)(2,1)S(1)} %stack.22), channel_id=1, source_target_pairs={{0,4},{4,0},{1,5},{5,1},{2,6},{6,2},{3,7},{7,3},{8,12},{12,8},{9,1... | collective-permute-start | bytes 5898248 | tf_op jit(solution)/shard_map/ppermute | solution.py:294
  125.2 3.8 %collective-permute-start.15 = (bf16[12,128,128]{2,1,0:T(8,128)(2,1)S(1)}, bf16[12,128,128]{2,1,0:T(8,128)(2,1)S(1)}, u32[]{:S(2)}, u32[]{:S(2)}) collective-permute-start(bf16[12,128,128]{2,1,0:T(8,128)(2,1)S(1)} %collective-permute-done.12.refs_0_.refs_3_), channel_id=1, source_target_pairs={{0,8},{8,16},{16,24},{24,32},{32,40},{40,48},{48,56},{56,0},{1,9},... | collective-permute-start | bytes 1179656 | tf_op jit(solution)/shard_map/ppermute | solution.py:208
  129.0 10.3 %collective-permute-done.15.refs_1_.refs_4_ = bf16[12,128,128]{2,1,0:T(8,128)(2,1)S(1)} collective-permute-done((bf16[12,128,128]{2,1,0:T(8,128)(2,1)S(1)}, bf16[12,128,128]{2,1,0:T(8,128)(2,1)S(1)}, u32[]{:S(2)}, u32[]{:S(2)}) %collective-permute-start.15) | collective-permute-done | bytes 393248 | tf_op jit(solution)/shard_map/ppermute | solution.py:208
  139.3 1.4 stack.23
  140.7 3.1 %collective-permute-start.17 = (bf16[3,12,128,128]{3,2,1,0:T(8,128)(2,1)S(1)}, bf16[3,12,128,128]{3,2,1,0:T(8,128)(2,1)S(1)}, u32[]{:S(2)}, u32[]{:S(2)}) collective-permute-start(bf16[3,12,128,128]{3,2,1,0:T(8,128)(2,1)S(1)} %stack.23), channel_id=1, source_target_pairs={{0,4},{4,0},{1,5},{5,1},{2,6},{6,2},{3,7},{7,3},{8,12},{12,8},{9,1... | collective-permute-start | bytes 3538952 | tf_op jit(solution)/shard_map/ppermute | solution.py:300
  143.9 1.1 fusion
  145.1 1.2 collective-permute-done.17.refs_9_
  146.3 17.1 %factor_and_update.1 = (bf16[2,16,1024]{2,1,0:T(8,128)(2,1)}, bf16[2,1024,128]{2,1,0:T(8,128)(2,1)}, f32[1024,128]{1,0:T(8,128)}, f32[1024,128]{1,0:T(8,128)}) custom-call(s32[4]{0:T(128)S(1)} %pad_add_fusion.at_ref, bf16[8,128,1024]{2,1,0:T(8,128)(2,1)S(1)} %order.1.inv_own, bf16[8,128,1024]{2,1,0:T(8,128)(2,1)S(1)} %collective-permute-done.14.inv_other, ...), custom_call_target="tpu_custom_call" | custom-call | flops 11274289152 | bytes 14680064 | tf_op jit(solution)/shard_map/factor_and_update/pallas_call | solution.py:311
  (60 shorter events, 3.8 us)
Async XLA Ops:
  0.6 1.0 copy-start
  1.7 24.8 %collective-permute-start.1 = (bf16[128,1024]{1,0:T(8,128)(2,1)S(1)}, bf16[128,1024]{1,0:T(8,128)(2,1)S(1)}, u32[]{:S(2)}, u32[]{:S(2)}) collective-permute-start(bf16[128,1024]{1,0:T(8,128)(2,1)S(1)} %dynamic-slice_bitcast_fusion.refs_0_), channel_id=1, source_target_pairs={{0,448},{64,0},{128,64},{192,128},{256,192},{320,256},{384,320},{4... | collective-permute-start | bytes 786440 | tf_op jit(solution)/shard_map/ppermute | solution.py:208
  13.2 13.3 %collective-permute-start = (bf16[128,1024]{1,0:T(8,128)(2,1)S(1)}, bf16[128,1024]{1,0:T(8,128)(2,1)S(1)}, u32[]{:S(2)}, u32[]{:S(2)}) collective-permute-start(bf16[128,1024]{1,0:T(8,128)(2,1)S(1)} %dynamic-slice_bitcast_fusion.refs_0_), channel_id=1, source_target_pairs={{0,64},{64,128},{128,192},{192,256},{256,320},{320,384},{384,448},... | collective-permute-start | bytes 786440 | tf_op jit(solution)/shard_map/ppermute | solution.py:208
  26.5 73.8 %copy-start.10 = (bf16[128,1024]{1,0:T(8,128)(2,1)}, bf16[128,1024]{1,0:T(8,128)(2,1)S(1)}, u32[]{:S(2)}) copy-start(bf16[128,1024]{1,0:T(8,128)(2,1)S(1)} %collective-permute-done.refs_1_) | copy-start | bytes 786436
  26.5 0.8 copy-start.22
  27.2 0.8 copy-start.23
  28.8 15.9 %all-to-all-start.1 = ((bf16[8,224,128]{2,1,0:T(8,128)(2,1)}), bf16[8,224,128]{2,1,0:T(8,128)(2,1)S(1)}, u32[]{:S(2)}, u32[]{:S(2)}) async-start(bf16[8,224,128]{2,1,0:T(8,128)(2,1)} %bitcast.8), calls=%async_computation.1 | async-start | bytes 917504 | tf_op jit(solution)/shard_map/all_to_all | solution.py:200
  35.8 11.0 %collective-permute-start.2 = (bf16[128,1024]{1,0:T(8,128)(2,1)S(1)}, bf16[128,1024]{1,0:T(8,128)(2,1)S(1)}, u32[]{:S(2)}, u32[]{:S(2)}) collective-permute-start(bf16[128,1024]{1,0:T(8,128)(2,1)S(1)} %collective-permute-done.refs_1_), channel_id=1, source_target_pairs={{0,64},{64,128},{128,192},{192,256},{256,320},{320,384},{384,448},... | collective-permute-start | bytes 786440 | tf_op jit(solution)/shard_map/ppermute | solution.py:208
  37.9 9.7 %collective-permute-start.3 = (bf16[128,1024]{1,0:T(8,128)(2,1)S(1)}, bf16[128,1024]{1,0:T(8,128)(2,1)S(1)}, u32[]{:S(2)}, u32[]{:S(2)}) collective-permute-start(bf16[128,1024]{1,0:T(8,128)(2,1)S(1)} %collective-permute-done.1.refs_7_), channel_id=1, source_target_pairs={{0,448},{64,0},{128,64},{192,128},{256,192},{320,256},{384,320},{4... | collective-permute-start | bytes 786440 | tf_op jit(solution)/shard_map/ppermute | solution.py:208
  47.6 19.9 %collective-permute-start.9 = (bf16[12,128,128]{2,1,0:T(8,128)(2,1)S(1)}, bf16[12,128,128]{2,1,0:T(8,128)(2,1)S(1)}, u32[]{:S(2)}, u32[]{:S(2)}) collective-permute-start(bf16[12,128,128]{2,1,0:T(8,128)(2,1)S(1)} %bitcast.23), channel_id=1, source_target_pairs={{0,56},{8,0},{16,8},{24,16},{32,24},{40,32},{48,40},{56,48},{1,57}... | collective-permute-start | bytes 1179656 | tf_op jit(solution)/shard_map/ppermute | solution.py:208
  52.7 14.8 %collective-permute-start.8 = (bf16[12,128,128]{2,1,0:T(8,128)(2,1)S(1)}, bf16[12,128,128]{2,1,0:T(8,128)(2,1)S(1)}, u32[]{:S(2)}, u32[]{:S(2)}) collective-permute-start(bf16[12,128,128]{2,1,0:T(8,128)(2,1)S(1)} %bitcast.24), channel_id=1, source_target_pairs={{0,8},{8,16},{16,24},{24,32},{32,40},{40,48},{48,56},{56,0},{1,9},... | collective-permute-start | bytes 1179656 | tf_op jit(solution)/shard_map/ppermute | solution.py:208
  54.7 0.7 copy-start.1
  55.4 10.5 %collective-permute-start.5 = (bf16[128,1024]{1,0:T(8,128)(2,1)S(1)}, bf16[128,1024]{1,0:T(8,128)(2,1)S(1)}, u32[]{:S(2)}, u32[]{:S(2)}) collective-permute-start(bf16[128,1024]{1,0:T(8,128)(2,1)S(1)} %collective-permute-done.2.refs_2_), channel_id=1, source_target_pairs={{0,64},{64,128},{128,192},{192,256},{256,320},{320,384},{384,448},... | collective-permute-start | bytes 786440 | tf_op jit(solution)/shard_map/ppermute | solution.py:208
  57.3 0.7 copy-start.12
  58.0 9.5 %collective-permute-start.6 = (bf16[128,1024]{1,0:T(8,128)(2,1)S(1)}, bf16[128,1024]{1,0:T(8,128)(2,1)S(1)}, u32[]{:S(2)}, u32[]{:S(2)}) collective-permute-start(bf16[128,1024]{1,0:T(8,128)(2,1)S(1)} %collective-permute-done.3.refs_6_), channel_id=1, source_target_pairs={{0,448},{64,0},{128,64},{192,128},{256,192},{320,256},{384,320},{4... | collective-permute-start | bytes 786440 | tf_op jit(solution)/shard_map/ppermute | solution.py:208
  63.3 0.7 copy-start.14
  64.0 0.7 collective-permute-start.4
  66.0 40.9 %copy-start.16 = (bf16[128,1024]{1,0:T(8,128)(2,1)}, bf16[128,1024]{1,0:T(8,128)(2,1)S(1)}, u32[]{:S(2)}) copy-start(bf16[128,1024]{1,0:T(8,128)(2,1)S(1)} %collective-permute-done.5.refs_3_) | copy-start | bytes 786436
  67.5 39.3 %copy-start.18 = (bf16[128,1024]{1,0:T(8,128)(2,1)}, bf16[128,1024]{1,0:T(8,128)(2,1)S(1)}, u32[]{:S(2)}) copy-start(bf16[128,1024]{1,0:T(8,128)(2,1)S(1)} %collective-permute-done.6.refs_5_) | copy-start | bytes 786436
  67.5 39.3 %copy-start.4 = (bf16[12,128,128]{2,1,0:T(8,128)(2,1)}, bf16[12,128,128]{2,1,0:T(8,128)(2,1)S(1)}, u32[]{:S(2)}) copy-start(bf16[12,128,128]{2,1,0:T(8,128)(2,1)S(1)} %collective-permute-done.9.refs_4_.refs_7_) | copy-start | bytes 1179652
  67.6 39.3 %copy-start.7 = (bf16[12,128,128]{2,1,0:T(8,128)(2,1)}, bf16[12,128,128]{2,1,0:T(8,128)(2,1)S(1)}, u32[]{:S(2)}) copy-start(bf16[12,128,128]{2,1,0:T(8,128)(2,1)S(1)} %collective-permute-done.8.refs_1_) | copy-start | bytes 1179652
  68.5 44.9 %all-to-all-start.2 = ((bf16[8,256,128]{2,1,0:T(8,128)(2,1)}), bf16[8,256,128]{2,1,0:T(8,128)(2,1)}, u32[]{:S(2)}, u32[]{:S(2)}) async-start(bf16[8,256,128]{2,1,0:T(8,128)(2,1)} %broadcast_in_dim.16), calls=%async_computation.2 | async-start | bytes 1048576 | tf_op jit(solution)/shard_map/all_to_all | solution.py:200
  80.8 19.5 %collective-permute-start.10 = (bf16[12,128,128]{2,1,0:T(8,128)(2,1)S(1)}, bf16[12,128,128]{2,1,0:T(8,128)(2,1)}, u32[]{:S(2)}, u32[]{:S(2)}) collective-permute-start(bf16[12,128,128]{2,1,0:T(8,128)(2,1)S(1)} %collective-permute-done.8.refs_1_), channel_id=1, source_target_pairs={{0,8},{8,16},{16,24},{24,32},{32,40},{40,48},{48,56},{56,0},{1,9},... | collective-permute-start | bytes 1179656 | tf_op jit(solution)/shard_map/ppermute | solution.py:208
  82.7 17.6 %collective-permute-start.11 = (bf16[12,128,128]{2,1,0:T(8,128)(2,1)S(1)}, bf16[12,128,128]{2,1,0:T(8,128)(2,1)}, u32[]{:S(2)}, u32[]{:S(2)}) collective-permute-start(bf16[12,128,128]{2,1,0:T(8,128)(2,1)S(1)} %collective-permute-done.9.refs_4_.refs_7_), channel_id=1, source_target_pairs={{0,56},{8,0},{16,8},{24,16},{32,24},{40,32},{48,40},{56,48},{1,57}... | collective-permute-start | bytes 1179656 | tf_op jit(solution)/shard_map/ppermute | solution.py:208
  87.3 12.3 %collective-permute-start.7 = (bf16[128,1024]{1,0:T(8,128)(2,1)S(1)}, bf16[128,1024]{1,0:T(8,128)(2,1)S(1)}, u32[]{:S(2)}, u32[]{:S(2)}) collective-permute-start(bf16[128,1024]{1,0:T(8,128)(2,1)S(1)} %collective-permute-done.5.refs_3_), channel_id=1, source_target_pairs={{0,64},{64,128},{128,192},{192,256},{256,320},{320,384},{384,448},... | collective-permute-start | bytes 786440 | tf_op jit(solution)/shard_map/ppermute | solution.py:208
  99.6 0.7 copy-start.20
  100.3 13.1 %collective-permute-start.12 = (bf16[12,128,128]{2,1,0:T(8,128)(2,1)}, bf16[12,128,128]{2,1,0:T(8,128)(2,1)S(1)}, u32[]{:S(2)}, u32[]{:S(2)}) collective-permute-start(bf16[12,128,128]{2,1,0:T(8,128)(2,1)} %collective-permute-done.10.refs_2_), channel_id=1, source_target_pairs={{0,8},{8,16},{16,24},{24,32},{32,40},{40,48},{48,56},{56,0},{1,9},... | collective-permute-start | bytes 1179656 | tf_op jit(solution)/shard_map/ppermute | solution.py:208
  102.2 11.2 %collective-permute-start.13 = (bf16[12,128,128]{2,1,0:T(8,128)(2,1)}, bf16[12,128,128]{2,1,0:T(8,128)(2,1)}, u32[]{:S(2)}, u32[]{:S(2)}) collective-permute-start(bf16[12,128,128]{2,1,0:T(8,128)(2,1)} %collective-permute-done.11.refs_3_.refs_6_), channel_id=1, source_target_pairs={{0,56},{8,0},{16,8},{24,16},{32,24},{40,32},{48,40},{56,48},{1,57}... | collective-permute-start | bytes 1179656 | tf_op jit(solution)/shard_map/ppermute | solution.py:208
  106.9 1.0 copy-start.11
  107.9 0.9 copy-start.13
  108.8 0.9 copy-start.15
  109.8 0.9 copy-start.17
  110.7 0.9 copy-start.19
  111.7 0.9 copy-start.21
  113.5 32.8 %collective-permute-start.14 = (bf16[8,128,1024]{2,1,0:T(8,128)(2,1)S(1)}, bf16[8,128,1024]{2,1,0:T(8,128)(2,1)S(1)}, u32[]{:S(2)}, u32[]{:S(2)}) collective-permute-start(bf16[8,128,1024]{2,1,0:T(8,128)(2,1)S(1)} %order.1.inv_own), channel_id=1, source_target_pairs={{0,4},{4,0},{1,5},{5,1},{2,6},{6,2},{3,7},{7,3},{8,12},{12,8},{9,1... | collective-permute-start | bytes 6291464 | tf_op jit(solution)/shard_map/ppermute | solution.py:297
  118.6 1.0 copy-start.2
  119.6 1.0 copy-start.5
  120.6 1.0 copy-start.8
  123.1 20.7 %copy-start.26 = (bf16[2,1024,128]{2,1,0:T(8,128)(2,1)S(1)}, bf16[2,1024,128]{2,1,0:T(8,128)(2,1)}, u32[]{:S(2)}) copy-start(bf16[2,1024,128]{2,1,0:T(8,128)(2,1)} %param.12) | copy-start | bytes 1572868
  123.1 21.9 %collective-permute-start.16 = (bf16[5,12,128,128]{3,2,1,0:T(8,128)(2,1)S(1)}, bf16[5,12,128,128]{3,2,1,0:T(8,128)(2,1)S(1)}, u32[]{:S(2)}, u32[]{:S(2)}) collective-permute-start(bf16[5,12,128,128]{3,2,1,0:T(8,128)(2,1)S(1)} %stack.22), channel_id=1, source_target_pairs={{0,4},{4,0},{1,5},{5,1},{2,6},{6,2},{3,7},{7,3},{8,12},{12,8},{9,1... | collective-permute-start | bytes 5898248 | tf_op jit(solution)/shard_map/ppermute | solution.py:294
  125.2 14.1 %collective-permute-start.15 = (bf16[12,128,128]{2,1,0:T(8,128)(2,1)S(1)}, bf16[12,128,128]{2,1,0:T(8,128)(2,1)S(1)}, u32[]{:S(2)}, u32[]{:S(2)}) collective-permute-start(bf16[12,128,128]{2,1,0:T(8,128)(2,1)S(1)} %collective-permute-done.12.refs_0_.refs_3_), channel_id=1, source_target_pairs={{0,8},{8,16},{16,24},{24,32},{32,40},{40,48},{48,56},{56,0},{1,9},... | collective-permute-start | bytes 1179656 | tf_op jit(solution)/shard_map/ppermute | solution.py:208
  140.7 5.6 %copy-start.3 = (bf16[12,8,16,128]{3,2,1,0:T(8,128)(2,1)S(1)}, bf16[12,8,16,128]{3,2,1,0:T(8,128)(2,1)}, u32[]{:S(2)}) copy-start(bf16[12,8,16,128]{3,2,1,0:T(8,128)(2,1)} %copy-done.1) | copy-start | bytes 1179652
  140.7 5.6 %copy-start.6 = (bf16[12,128,128]{2,1,0:T(8,128)(2,1)S(1)}, bf16[12,128,128]{2,1,0:T(8,128)(2,1)}, u32[]{:S(2)}) copy-start(bf16[12,128,128]{2,1,0:T(8,128)(2,1)} %copy-done.4) | copy-start | bytes 1179652
  140.7 5.6 %copy-start.9 = (bf16[12,128,128]{2,1,0:T(8,128)(2,1)S(1)}, bf16[12,128,128]{2,1,0:T(8,128)(2,1)}, u32[]{:S(2)}) copy-start(bf16[12,128,128]{2,1,0:T(8,128)(2,1)} %copy-done.7) | copy-start | bytes 1179652
  140.7 5.6 %copy-start.24 = (bf16[1024,128]{1,0:T(8,128)(2,1)S(1)}, bf16[1024,128]{1,0:T(8,128)(2,1)}, u32[]{:S(2)}) copy-start(bf16[1024,128]{1,0:T(8,128)(2,1)} %refs_12_.1) | copy-start | bytes 786436
  140.7 5.6 %copy-start.25 = (bf16[1024,128]{1,0:T(8,128)(2,1)S(1)}, bf16[1024,128]{1,0:T(8,128)(2,1)}, u32[]{:S(2)}) copy-start(bf16[1024,128]{1,0:T(8,128)(2,1)} %refs_13_.1) | copy-start | bytes 786436
  140.7 5.5 %collective-permute-start.17 = (bf16[3,12,128,128]{3,2,1,0:T(8,128)(2,1)S(1)}, bf16[3,12,128,128]{3,2,1,0:T(8,128)(2,1)S(1)}, u32[]{:S(2)}, u32[]{:S(2)}) collective-permute-start(bf16[3,12,128,128]{3,2,1,0:T(8,128)(2,1)S(1)} %stack.23), channel_id=1, source_target_pairs={{0,4},{4,0},{1,5},{5,1},{2,6},{6,2},{3,7},{7,3},{8,12},{12,8},{9,1... | collective-permute-start | bytes 3538952 | tf_op jit(solution)/shard_map/ppermute | solution.py:300

commit v6 on v5

--- a/solution.py
+++ b/solution.py
@@ -55,18 +55,7 @@
     wait(start_copies([(ref, stacked.at[i]) for i, ref in enumerate(pieces)], sems))
 
 
-def order_kernel(at_ref, *refs):
-    pieces, stacked, sems = refs[:-2], refs[-2], refs[-1]
-    n = len(pieces)
-    wait(
-        start_copies(
-            [(ref, stacked.at[lax.rem(at_ref[3] + (n - k), n)]) for k, ref in enumerate(pieces)],
-            sems,
-        )
-    )
-
-
-def factor_kernel(near, ys, at_ref, inv_own, inv_other, *refs):
+def factor_kernel(near, ys, at_ref, whole, *refs):
     pieces, refs = refs[:ys], refs[ys:]
     far_near, far_rest, refs = refs[0], refs[1], refs[2:]
     others = {k: (far_near, i) for i, k in enumerate(near)}
@@ -79,8 +68,8 @@
     f32, bf16 = jnp.float32, jnp.bfloat16
 
     inv_copies = [
-        pltpu.make_async_copy(inv_own, inv.at[core], sems.at[0]),
-        pltpu.make_async_copy(inv_other, inv.at[1 - core], sems.at[1]),
+        pltpu.make_async_copy(whole.at[0], inv.at[0], sems.at[0]),
+        pltpu.make_async_copy(whole.at[1], inv.at[1], sems.at[1]),
     ]
     panel_copies = [[], [], []]
     for p in range(3):
@@ -110,8 +99,7 @@
         copy.wait()
 
     def inverse(k, i):
-        rows = inv[k, 2 * i : 2 * i + 2].reshape(TILE, size)
-        return rows[:, : (i + 1) * TILE]
+        return inv[k, i * TILE : (i + 1) * TILE, : (i + 1) * TILE]
 
     def lower(k, load, store):
         for i in range(size // TILE):
@@ -220,18 +208,17 @@
     )(*operands)
 
 
-def stack(pieces, where=None):
+def stack(pieces):
     anywhere = pl.BlockSpec(memory_space=pl.ANY)
-    extra = [] if where is None else [where]
     return pl.pallas_call(
-        stack_kernel if where is None else order_kernel,
-        name="stack" if where is None else "order",
+        stack_kernel,
+        name="stack",
         out_shape=jax.ShapeDtypeStruct((len(pieces),) + pieces[0].shape, pieces[0].dtype),
-        in_specs=[pl.BlockSpec(memory_space=pltpu.SMEM)] * len(extra) + [anywhere] * len(pieces),
+        in_specs=[anywhere] * len(pieces),
         out_specs=anywhere,
         scratch_shapes=[pltpu.SemaphoreType.DMA((len(pieces),))],
         compiler_params=pltpu.CompilerParams(vmem_limit_bytes=1 << 20),
-    )(*extra, *pieces)
+    )(*pieces)
 
 
 def per_device(sizes, panel_top, panel_low, panel_next, gram_rest, inverses, right_top, right_low):
@@ -239,7 +226,7 @@
     axes = ("row", "y", "core", "vox")
     order = np.arange(rows * ys * cores * voxes).reshape(sizes)
     swap = list(zip(order.ravel().tolist(), order.transpose(1, 0, 2, 3).ravel().tolist()))
-    z, y = lax.axis_index("row"), lax.axis_index("y")
+    y = lax.axis_index("y")
     core, vox = lax.axis_index("core"), lax.axis_index("vox")
     size, width = inverses.shape[2], panel_low.shape[1]
     cols = gram_rest.shape[1]
@@ -247,7 +234,7 @@
     other = [(0, 1), (1, 0)]
 
     own = ((y * cores + core) * voxes + vox) * width
-    where = jnp.stack([y, core, own, z]).astype(jnp.int32)
+    where = jnp.stack([y, core, own]).astype(jnp.int32)
     barrier = lax.optimization_barrier
     group = cores * voxes
     flats = [panel_low.T, panel_next.T]
@@ -266,11 +253,8 @@
             pieces[i] = piece
         return values
 
-    invs = {0: lax.dynamic_index_in_dim(inverses, core, 0, False)}
-    ring(invs, 1, "row", rows)
+    whole = lax.all_gather(inverses, "row", axis=1, tiled=True)
     top = gather_small(panel_top.T, "row", rows)
-    top = ordered(top, invs, 1, rows)
-    ring(invs, 2, "row", rows)
     (sent,) = call(
         pack_kernel, "pack", [((cores, voxes, 3 * voxes + 2, width, cols), bf16)], top, *flats
     )
@@ -280,21 +264,15 @@
         [((3 * voxes, group, width, cols), bf16), ((group, 2, width, cols), bf16)], got,
     )
     pieces = {0: mine.reshape(3 * voxes, group * width, cols)}
-    pieces[0], single = ordered((pieces[0], single), invs, 2, rows)
     ring(pieces, 1, "y", ys)
     swapped = lax.ppermute(single, axes, swap)
-    ring(invs, 3, "row", rows)
-    swapped = ordered(ordered(swapped, invs, 3, rows), pieces, 1, ys)
     ring(pieces, 2, "y", ys)
-    ring(invs, 4, "row", rows)
-    matching = gather_small(swapped, "row", rows)
-    invs[4] = ordered(invs[4], pieces, 2, ys)
+    swapped = ordered(swapped, pieces, 2, ys)
     ring(pieces, 3, "y", ys)
     near = sorted(k % ys for k in range(-2, 3))
     far_near = lax.ppermute(stack([pieces[k] for k in near]), "core", other)
-    inv_own = stack([invs[k] for k in range(rows)], where)
-    inv_own, matching = ordered((inv_own, matching), pieces, 3, ys)
-    inv_other = lax.ppermute(inv_own, "core", other)
+    matching = gather_small(swapped, "row", rows)
+    far_near, whole = ordered((far_near, whole), pieces, 3, ys)
     ring(pieces, 4, "y", ys)
     rest = [pieces[k] for k in range(ys) if k not in near]
     far_rest = lax.ppermute(stack(rest), "core", other)
@@ -316,10 +294,10 @@
             jax.ShapeDtypeStruct((height, cols), jnp.float32),
             jax.ShapeDtypeStruct((height, cols), jnp.float32),
         ),
-        in_specs=[pl.BlockSpec(memory_space=pltpu.SMEM)] + [any_space] * (8 + ys),
+        in_specs=[pl.BlockSpec(memory_space=pltpu.SMEM)] + [any_space] * (7 + ys),
         out_specs=(local,) * 4,
         scratch_shapes=[
-            vmem((2, rows, size // rows, size), bf16),
+            vmem((2, size, size), bf16),
             vmem((3, cores * voxes, ys, group * width, cols), bf16),
             vmem((2, size, TILE), bf16),
             vmem((2, height, cols), bf16),
@@ -329,10 +307,10 @@
             vmem((size, height + TILE), bf16),
             pltpu.SemaphoreType.DMA((6 * ys + 6,)),
         ],
-        compiler_params=pltpu.CompilerParams(vmem_limit_bytes=40 * 1024 * 1024),
+        compiler_params=pltpu.CompilerParams(vmem_limit_bytes=56 * 1024 * 1024),
         cost_estimate=pl.CostEstimate(flops=flops, bytes_accessed=14 << 20, transcendentals=0),
         name="factor_and_update",
-    )(where, inv_own, inv_other, *pieces, far_near, far_rest, *sides, gram_rest, right_low)
+    )(where, whole, *pieces, far_near, far_rest, *sides, gram_rest, right_low)
     return (factor.transpose(0, 2, 1), solved, trailing, residual)
 
 

time: 166 us -> 151 us (0.910)
  starting transfers between devices: 84.4 us -> 38.1 us
  blocking collectives: 10.6 us -> 32.8 us
  local copies, waits for them, and re-layouts: 16.9 us -> 3.18 us
  between operations: 1.09 us -> 14.3 us
  waiting for transfers between devices: 28.6 us -> 39.3 us
  Pallas kernels: 21.7 us -> 19.4 us
  other arithmetic: 0.19 us -> 1.85 us
    ppermute x14 -> x7, starting transfers between devices: 54.3 us -> 22.8 us  [shift(): lax.ppermute(block, axis, [(i, (i + by) % size) for i in range(size)])]
    all_to_all x1 -> x2, blocking collectives: 10.6 us -> 32.8 us  [exchange(): return lax.all_to_all(flat, axis, 0, 0, tiled=True).reshape(blocks.shape)]
    all_to_all x2 -> x1, starting transfers between devices: 19.2 us -> 4.4 us  [exchange(): return lax.all_to_all(flat, axis, 0, 0, tiled=True).reshape(blocks.shape)]
    unnamed x54 -> x22, local copies, waits for them, and re-layouts: 14.1 us -> 1.55 us
    ppermute x14 -> x7, waiting for transfers between devices: 24.9 us -> 33.5 us  [shift(): lax.ppermute(block, axis, [(i, (i + by) % size) for i in range(size)])]
    ppermute x1 -> x0, starting transfers between devices: 5.13 us -> none  [per_device(): inv_other = lax.ppermute(inv_own, 'core', other)]
    ppermute x1, starting transfers between devices: 2.05 us -> 6.61 us  [per_device(): far_near = lax.ppermute(stack([pieces[k] for k in near]), 'core', other)]
    all_to_all x2 -> x1, waiting for transfers between devices: 2.47 us -> 5.18 us  [exchange(): return lax.all_to_all(flat, axis, 0, 0, tiled=True).reshape(blocks.shape)]
  transfers between devices with their start and end apart: 20 -> 12, of which waited for: 8 -> 7; matrix products, arithmetic and copies ran while one was open for 1% -> 2% of each run, Pallas kernels for 2% -> 1%
where the time goes in v6:
time: 151 us; the launch traced here: 149 us
  waiting for transfers between devices  39.3 us (26%)
  starting transfers between devices  38.1 us (25%)
  blocking collectives  32.8 us (22%)
  Pallas kernels  19.4 us (13%)
  between operations  14.3 us (9%)
  local copies, waits for them, and re-layouts  3.18 us (2%)
  other arithmetic  1.85 us (1%)
    ppermute x7, waiting for transfers between devices, shift(): lax.ppermute(block, axis, [(i, (i + by) % size) for i in range(size)])  33.5 us
    all_to_all x2, blocking collectives, exchange(): return lax.all_to_all(flat, axis, 0, 0, tiled=True).reshape(blocks.shape)  32.8 us
    ppermute x7, starting transfers between devices, shift(): lax.ppermute(block, axis, [(i, (i + by) % size) for i in range(size)])  22.8 us
    pallas_call x1, Pallas kernels, per_device(): pl.pallas_call(functools.partial(factor_kernel, near, ys), out_shape=(jax...  17.7 us
    ppermute x1, starting transfers between devices, per_device(): far_near = lax.ppermute(stack([pieces[k] for k in near]), 'core', other)  6.61 us
    all_to_all x1, waiting for transfers between devices, exchange(): return lax.all_to_all(flat, axis, 0, 0, tiled=True).reshape(blocks.shape)  5.18 us
    all_to_all x1, starting transfers between devices, exchange(): return lax.all_to_all(flat, axis, 0, 0, tiled=True).reshape(blocks.shape)  4.4 us
    ppermute x1, starting transfers between devices, per_device(): far_rest = lax.ppermute(stack(rest), 'core', other)  3.64 us
  transfers between devices with their start and end apart: 12, of which 7 were waited for; matrix products, arithmetic and copies ran while one was open for 2% of the time, Pallas kernels for 1%

profile of v6, /device:TPU:1, one launch (start us, length us, event | category | flops | bytes accessed | tf_op | source)
XLA Modules:
  0.0 148.9 jit_solution(14992587649300834096)
XLA Ops:
  7.2 0.0 all-gather.2.cloned.1.call-start
  7.2 0.7 all-gather.2.cloned.1.call-update
  7.9 0.7 broadcast_in_dim.6
  8.6 17.5 %all_to_all.15.top = bf16[8,16,128]{2,1,0:T(8,128)(2,1)S(1)} all-to-all(bf16[8,16,128]{2,1,0:T(8,128)(2,1)S(1)} %broadcast_in_dim.6), channel_id=1, replica_groups=mesh['row'=8,'y'=8,'core'=2,'vox'=4] {'row'}, dimensions={0} | all-to-all | bytes 65536 | tf_op jit(solution)/shard_map/all_to_all | solution.py:188
  26.1 0.8 copy-done.8
  26.9 0.8 copy-done.9
  27.6 0.1 pack.1
  27.7 15.3 %all_to_all.16 = bf16[8,224,128]{2,1,0:T(8,128)(2,1)S(1)} all-to-all(bf16[8,224,128]{2,1,0:T(8,128)(2,1)S(1)} %bitcast.21), channel_id=1, replica_groups=mesh['row'=8,'y'=8,'core'=2,'vox'=4] {'core','vox'}, dimensions={0} | all-to-all | bytes 917504 | tf_op jit(solution)/shard_map/all_to_all | solution.py:188
  43.0 0.0 copy-start.3
  43.0 5.1 %collective-permute-start.3 = (bf16[12,128,128]{2,1,0:T(8,128)(2,1)S(1)}, bf16[12,128,128]{2,1,0:T(8,128)(2,1)S(1)}, u32[]{:S(2)}, u32[]{:S(2)}) collective-permute-start(bf16[12,128,128]{2,1,0:T(8,128)(2,1)S(1)} %bitcast.22), channel_id=1, source_target_pairs={{0,56},{8,0},{16,8},{24,16},{32,24},{40,32},{48,40},{56,48},{1,57}... | collective-permute-start | bytes 1179656 | tf_op jit(solution)/shard_map/ppermute | solution.py:196
  48.1 1.9 %collective-permute-start = (bf16[12,128,128]{2,1,0:T(8,128)(2,1)S(1)}, bf16[12,128,128]{2,1,0:T(8,128)(2,1)S(1)}, u32[]{:S(2)}, u32[]{:S(2)}) collective-permute-start(bf16[12,128,128]{2,1,0:T(8,128)(2,1)S(1)} %bitcast.23), channel_id=1, source_target_pairs={{0,8},{8,16},{16,24},{24,32},{32,40},{40,48},{48,56},{56,0},{1,9},... | collective-permute-start | bytes 1179656 | tf_op jit(solution)/shard_map/ppermute | solution.py:196
  50.1 6.6 %collective-permute-done.3.refs_4_.refs_7_ = bf16[12,128,128]{2,1,0:T(8,128)(2,1)S(1)} collective-permute-done((bf16[12,128,128]{2,1,0:T(8,128)(2,1)S(1)}, bf16[12,128,128]{2,1,0:T(8,128)(2,1)S(1)}, u32[]{:S(2)}, u32[]{:S(2)}) %collective-permute-start.3) | collective-permute-done | bytes 393248 | tf_op jit(solution)/shard_map/ppermute | solution.py:196
  56.6 5.4 %collective-permute-start.4 = (bf16[12,128,128]{2,1,0:T(8,128)(2,1)S(1)}, bf16[12,128,128]{2,1,0:T(8,128)(2,1)S(1)}, u32[]{:S(2)}, u32[]{:S(2)}) collective-permute-start(bf16[12,128,128]{2,1,0:T(8,128)(2,1)S(1)} %collective-permute-done.3.refs_4_.refs_7_), channel_id=1, source_target_pairs={{0,56},{8,0},{16,8},{24,16},{32,24},{40,32},{48,40},{56,48},{1,57}... | collective-permute-start | bytes 1179656 | tf_op jit(solution)/shard_map/ppermute | solution.py:196
  62.1 0.0 collective-permute-done.refs_1_
  62.1 0.0 copy-start.5
  62.1 1.9 %collective-permute-start.2 = (bf16[12,128,128]{2,1,0:T(8,128)(2,1)S(1)}, bf16[12,128,128]{2,1,0:T(8,128)(2,1)S(1)}, u32[]{:S(2)}, u32[]{:S(2)}) collective-permute-start(bf16[12,128,128]{2,1,0:T(8,128)(2,1)S(1)} %collective-permute-done.refs_1_), channel_id=1, source_target_pairs={{0,8},{8,16},{16,24},{24,32},{32,40},{40,48},{48,56},{56,0},{1,9},... | collective-permute-start | bytes 1179656 | tf_op jit(solution)/shard_map/ppermute | solution.py:196
  64.0 0.7 collective-permute-start.1
  64.7 0.0 collective-permute-done.1
  64.7 5.1 %collective-permute-done.4.refs_3_.refs_6_ = bf16[12,128,128]{2,1,0:T(8,128)(2,1)S(1)} collective-permute-done((bf16[12,128,128]{2,1,0:T(8,128)(2,1)S(1)}, bf16[12,128,128]{2,1,0:T(8,128)(2,1)S(1)}, u32[]{:S(2)}, u32[]{:S(2)}) %collective-permute-start.4) | collective-permute-done | bytes 393248 | tf_op jit(solution)/shard_map/ppermute | solution.py:196
  69.8 7.1 %collective-permute-done.2.refs_2_ = bf16[12,128,128]{2,1,0:T(8,128)(2,1)S(1)} collective-permute-done((bf16[12,128,128]{2,1,0:T(8,128)(2,1)S(1)}, bf16[12,128,128]{2,1,0:T(8,128)(2,1)S(1)}, u32[]{:S(2)}, u32[]{:S(2)}) %collective-permute-start.2) | collective-permute-done | bytes 393248 | tf_op jit(solution)/shard_map/ppermute | solution.py:196
  76.9 1.0 stack.18
  77.9 0.0 copy-done.3
  77.9 0.0 copy-done.4
  77.9 0.0 copy-done.5
  77.9 6.6 %collective-permute-start.5 = (bf16[5,12,128,128]{3,2,1,0:T(8,128)(2,1)S(1)}, bf16[5,12,128,128]{3,2,1,0:T(8,128)(2,1)}, u32[]{:S(2)}, u32[]{:S(2)}) collective-permute-start(bf16[5,12,128,128]{3,2,1,0:T(8,128)(2,1)S(1)} %stack.18), channel_id=1, source_target_pairs={{0,4},{4,0},{1,5},{5,1},{2,6},{6,2},{3,7},{7,3},{8,12},{12,8},{9,1... | collective-permute-start | bytes 5898248 | tf_op jit(solution)/shard_map/ppermute | solution.py:273
  84.6 0.0 copy-done.7
  84.6 1.9 %collective-permute-start.6 = (bf16[12,128,128]{2,1,0:T(8,128)(2,1)S(1)}, bf16[12,128,128]{2,1,0:T(8,128)(2,1)S(1)}, u32[]{:S(2)}, u32[]{:S(2)}) collective-permute-start(bf16[12,128,128]{2,1,0:T(8,128)(2,1)S(1)} %collective-permute-done.2.refs_2_), channel_id=1, source_target_pairs={{0,8},{8,16},{16,24},{24,32},{32,40},{40,48},{48,56},{56,0},{1,9},... | collective-permute-start | bytes 1179656 | tf_op jit(solution)/shard_map/ppermute | solution.py:196
  86.5 0.0 copy-done.6
  86.5 4.6 %collective-permute-start.7 = (bf16[12,128,128]{2,1,0:T(8,128)(2,1)S(1)}, bf16[12,128,128]{2,1,0:T(8,128)(2,1)S(1)}, u32[]{:S(2)}, u32[]{:S(2)}) collective-permute-start(bf16[12,128,128]{2,1,0:T(8,128)(2,1)S(1)} %collective-permute-done.4.refs_3_.refs_6_), channel_id=1, source_target_pairs={{0,56},{8,0},{16,8},{24,16},{32,24},{40,32},{48,40},{56,48},{1,57}... | collective-permute-start | bytes 1179656 | tf_op jit(solution)/shard_map/ppermute | solution.py:196
  91.1 7.3 %collective-permute-done.6.refs_0_.refs_3_ = bf16[12,128,128]{2,1,0:T(8,128)(2,1)S(1)} collective-permute-done((bf16[12,128,128]{2,1,0:T(8,128)(2,1)S(1)}, bf16[12,128,128]{2,1,0:T(8,128)(2,1)S(1)}, u32[]{:S(2)}, u32[]{:S(2)}) %collective-permute-start.6) | collective-permute-done | bytes 393248 | tf_op jit(solution)/shard_map/ppermute | solution.py:196
  98.4 0.9 collective-permute-done.7.refs_2_.refs_5_
  99.3 0.0 collective-permute-done.5.refs_8_
  99.3 1.9 %collective-permute-start.8 = (bf16[12,128,128]{2,1,0:T(8,128)(2,1)S(1)}, bf16[12,128,128]{2,1,0:T(8,128)(2,1)S(1)}, u32[]{:S(2)}, u32[]{:S(2)}) collective-permute-start(bf16[12,128,128]{2,1,0:T(8,128)(2,1)S(1)} %collective-permute-done.6.refs_0_.refs_3_), channel_id=1, source_target_pairs={{0,8},{8,16},{16,24},{24,32},{32,40},{40,48},{48,56},{56,0},{1,9},... | collective-permute-start | bytes 1179656 | tf_op jit(solution)/shard_map/ppermute | solution.py:196
  101.2 0.0 copy-start.10
  101.2 0.9 broadcast_in_dim.16
  102.1 4.4 %all-to-all-start.2 = ((bf16[8,256,128]{2,1,0:T(8,128)(2,1)}), bf16[8,256,128]{2,1,0:T(8,128)(2,1)S(1)}, u32[]{:S(2)}, u32[]{:S(2)}) async-start(bf16[8,256,128]{2,1,0:T(8,128)(2,1)} %broadcast_in_dim.16), calls=%async_computation.2 | async-start | bytes 1048576 | tf_op jit(solution)/shard_map/all_to_all | solution.py:188
  106.5 6.5 %collective-permute-done.8.refs_1_.refs_4_ = bf16[12,128,128]{2,1,0:T(8,128)(2,1)S(1)} collective-permute-done((bf16[12,128,128]{2,1,0:T(8,128)(2,1)S(1)}, bf16[12,128,128]{2,1,0:T(8,128)(2,1)S(1)}, u32[]{:S(2)}, u32[]{:S(2)}) %collective-permute-start.8) | collective-permute-done | bytes 393248 | tf_op jit(solution)/shard_map/ppermute | solution.py:196
  112.9 0.6 stack.19
  113.5 0.0 copy-done
  113.5 0.0 copy-done.1
  113.6 3.6 %collective-permute-start.9 = (bf16[3,12,128,128]{3,2,1,0:T(8,128)(2,1)S(1)}, bf16[3,12,128,128]{3,2,1,0:T(8,128)(2,1)}, u32[]{:S(2)}, u32[]{:S(2)}) collective-permute-start(bf16[3,12,128,128]{3,2,1,0:T(8,128)(2,1)S(1)} %stack.19), channel_id=1, source_target_pairs={{0,4},{4,0},{1,5},{5,1},{2,6},{6,2},{3,7},{7,3},{8,12},{12,8},{9,1... | collective-permute-start | bytes 3538952 | tf_op jit(solution)/shard_map/ppermute | solution.py:278
  117.2 0.7 pad_add_fusion.at_ref
  117.9 0.0 copy-done.10
  117.9 5.2 %all-to-all-done.2 = bf16[8,256,128]{2,1,0:T(8,128)(2,1)S(1)} async-done(((bf16[8,256,128]{2,1,0:T(8,128)(2,1)}), bf16[8,256,128]{2,1,0:T(8,128)(2,1)S(1)}, u32[]{:S(2)}, u32[]{:S(2)}) %all-to-all-start.2) | async-done | bytes 524320 | tf_op jit(solution)/shard_map/all_to_all | solution.py:188
  123.1 0.0 copy-done.2
  123.1 1.2 pad_maximum_fusion
  124.3 0.0 collective-permute-done.9.refs_9_
  124.3 17.7 %factor_and_update.1 = (bf16[2,16,1024]{2,1,0:T(8,128)(2,1)}, bf16[2,1024,128]{2,1,0:T(8,128)(2,1)}, f32[1024,128]{1,0:T(8,128)}, f32[1024,128]{1,0:T(8,128)}) custom-call(s32[3]{0:T(128)} %pad_add_fusion.at_ref, bf16[2,1024,1024]{2,1,0:T(8,128)(2,1)} %all-gather.2.cloned.1.call-done.whole, bf16[12,128,128]{2,1,0:T(8,128)(2,1)} %bitcast.25, ...), custom_call_target="tpu_custom_call" | custom-call | flops 11274289152 | bytes 14680064 | tf_op jit(solution)/shard_map/factor_and_update/pallas_call | solution.py:289
  (12 shorter events, 0.1 us)
Async XLA Ops:
  7.2 92.1 %all-gather.2.cloned.1.call-start = ((), (), s32[]{:S(2)}) async-start(), calls=%async_computation.3 | async-start | bytes 4718592 | tf_op jit(solution)/shard_map/all_gather | solution.py:256
  26.1 0.8 copy-start.8
  26.9 0.8 copy-start.9
  43.0 34.9 %copy-start.3 = (bf16[12,8,16,128]{3,2,1,0:T(8,128)(2,1)}, bf16[12,8,16,128]{3,2,1,0:T(8,128)(2,1)S(1)}, u32[]{:S(2)}) copy-start(bf16[12,8,16,128]{3,2,1,0:T(8,128)(2,1)S(1)} %get-tuple-element.17) | copy-start | bytes 1179652
  43.0 13.6 %collective-permute-start.3 = (bf16[12,128,128]{2,1,0:T(8,128)(2,1)S(1)}, bf16[12,128,128]{2,1,0:T(8,128)(2,1)S(1)}, u32[]{:S(2)}, u32[]{:S(2)}) collective-permute-start(bf16[12,128,128]{2,1,0:T(8,128)(2,1)S(1)} %bitcast.22), channel_id=1, source_target_pairs={{0,56},{8,0},{16,8},{24,16},{32,24},{40,32},{48,40},{56,48},{1,57}... | collective-permute-start | bytes 1179656 | tf_op jit(solution)/shard_map/ppermute | solution.py:196
  48.1 13.9 %collective-permute-start = (bf16[12,128,128]{2,1,0:T(8,128)(2,1)S(1)}, bf16[12,128,128]{2,1,0:T(8,128)(2,1)S(1)}, u32[]{:S(2)}, u32[]{:S(2)}) collective-permute-start(bf16[12,128,128]{2,1,0:T(8,128)(2,1)S(1)} %bitcast.23), channel_id=1, source_target_pairs={{0,8},{8,16},{16,24},{24,32},{32,40},{40,48},{48,56},{56,0},{1,9},... | collective-permute-start | bytes 1179656 | tf_op jit(solution)/shard_map/ppermute | solution.py:196
  56.6 21.3 %copy-start.4 = (bf16[12,128,128]{2,1,0:T(8,128)(2,1)}, bf16[12,128,128]{2,1,0:T(8,128)(2,1)S(1)}, u32[]{:S(2)}) copy-start(bf16[12,128,128]{2,1,0:T(8,128)(2,1)S(1)} %collective-permute-done.3.refs_4_.refs_7_) | copy-start | bytes 1179652
  56.6 13.1 %collective-permute-start.4 = (bf16[12,128,128]{2,1,0:T(8,128)(2,1)S(1)}, bf16[12,128,128]{2,1,0:T(8,128)(2,1)S(1)}, u32[]{:S(2)}, u32[]{:S(2)}) collective-permute-start(bf16[12,128,128]{2,1,0:T(8,128)(2,1)S(1)} %collective-permute-done.3.refs_4_.refs_7_), channel_id=1, source_target_pairs={{0,56},{8,0},{16,8},{24,16},{32,24},{40,32},{48,40},{56,48},{1,57}... | collective-permute-start | bytes 1179656 | tf_op jit(solution)/shard_map/ppermute | solution.py:196
  62.1 15.9 %copy-start.5 = (bf16[12,128,128]{2,1,0:T(8,128)(2,1)}, bf16[12,128,128]{2,1,0:T(8,128)(2,1)S(1)}, u32[]{:S(2)}) copy-start(bf16[12,128,128]{2,1,0:T(8,128)(2,1)S(1)} %collective-permute-done.refs_1_) | copy-start | bytes 1179652
  62.1 14.9 %collective-permute-start.2 = (bf16[12,128,128]{2,1,0:T(8,128)(2,1)S(1)}, bf16[12,128,128]{2,1,0:T(8,128)(2,1)S(1)}, u32[]{:S(2)}, u32[]{:S(2)}) collective-permute-start(bf16[12,128,128]{2,1,0:T(8,128)(2,1)S(1)} %collective-permute-done.refs_1_), channel_id=1, source_target_pairs={{0,8},{8,16},{16,24},{24,32},{32,40},{40,48},{48,56},{56,0},{1,9},... | collective-permute-start | bytes 1179656 | tf_op jit(solution)/shard_map/ppermute | solution.py:196
  64.0 0.7 collective-permute-start.1
  69.8 16.7 %copy-start.6 = (bf16[12,128,128]{2,1,0:T(8,128)(2,1)}, bf16[12,128,128]{2,1,0:T(8,128)(2,1)S(1)}, u32[]{:S(2)}) copy-start(bf16[12,128,128]{2,1,0:T(8,128)(2,1)S(1)} %collective-permute-done.4.refs_3_.refs_6_) | copy-start | bytes 1179652
  76.9 7.6 %copy-start.7 = (bf16[12,128,128]{2,1,0:T(8,128)(2,1)}, bf16[12,128,128]{2,1,0:T(8,128)(2,1)S(1)}, u32[]{:S(2)}) copy-start(bf16[12,128,128]{2,1,0:T(8,128)(2,1)S(1)} %collective-permute-done.2.refs_2_) | copy-start | bytes 1179652
  77.9 21.3 %collective-permute-start.5 = (bf16[5,12,128,128]{3,2,1,0:T(8,128)(2,1)S(1)}, bf16[5,12,128,128]{3,2,1,0:T(8,128)(2,1)}, u32[]{:S(2)}, u32[]{:S(2)}) collective-permute-start(bf16[5,12,128,128]{3,2,1,0:T(8,128)(2,1)S(1)} %stack.18), channel_id=1, source_target_pairs={{0,4},{4,0},{1,5},{5,1},{2,6},{6,2},{3,7},{7,3},{8,12},{12,8},{9,1... | collective-permute-start | bytes 5898248 | tf_op jit(solution)/shard_map/ppermute | solution.py:273
  84.6 13.8 %collective-permute-start.6 = (bf16[12,128,128]{2,1,0:T(8,128)(2,1)S(1)}, bf16[12,128,128]{2,1,0:T(8,128)(2,1)S(1)}, u32[]{:S(2)}, u32[]{:S(2)}) collective-permute-start(bf16[12,128,128]{2,1,0:T(8,128)(2,1)S(1)} %collective-permute-done.2.refs_2_), channel_id=1, source_target_pairs={{0,8},{8,16},{16,24},{24,32},{32,40},{40,48},{48,56},{56,0},{1,9},... | collective-permute-start | bytes 1179656 | tf_op jit(solution)/shard_map/ppermute | solution.py:196
  86.5 12.8 %collective-permute-start.7 = (bf16[12,128,128]{2,1,0:T(8,128)(2,1)S(1)}, bf16[12,128,128]{2,1,0:T(8,128)(2,1)S(1)}, u32[]{:S(2)}, u32[]{:S(2)}) collective-permute-start(bf16[12,128,128]{2,1,0:T(8,128)(2,1)S(1)} %collective-permute-done.4.refs_3_.refs_6_), channel_id=1, source_target_pairs={{0,56},{8,0},{16,8},{24,16},{32,24},{40,32},{48,40},{56,48},{1,57}... | collective-permute-start | bytes 1179656 | tf_op jit(solution)/shard_map/ppermute | solution.py:196
  98.4 15.1 %copy-start = (bf16[12,128,128]{2,1,0:T(8,128)(2,1)}, bf16[12,128,128]{2,1,0:T(8,128)(2,1)S(1)}, u32[]{:S(2)}) copy-start(bf16[12,128,128]{2,1,0:T(8,128)(2,1)S(1)} %collective-permute-done.6.refs_0_.refs_3_) | copy-start | bytes 1179652
  99.3 14.3 %copy-start.1 = (bf16[12,128,128]{2,1,0:T(8,128)(2,1)}, bf16[12,128,128]{2,1,0:T(8,128)(2,1)S(1)}, u32[]{:S(2)}) copy-start(bf16[12,128,128]{2,1,0:T(8,128)(2,1)S(1)} %collective-permute-done.7.refs_2_.refs_5_) | copy-start | bytes 1179652
  99.3 13.6 %collective-permute-start.8 = (bf16[12,128,128]{2,1,0:T(8,128)(2,1)S(1)}, bf16[12,128,128]{2,1,0:T(8,128)(2,1)S(1)}, u32[]{:S(2)}, u32[]{:S(2)}) collective-permute-start(bf16[12,128,128]{2,1,0:T(8,128)(2,1)S(1)} %collective-permute-done.6.refs_0_.refs_3_), channel_id=1, source_target_pairs={{0,8},{8,16},{16,24},{24,32},{32,40},{40,48},{48,56},{56,0},{1,9},... | collective-permute-start | bytes 1179656 | tf_op jit(solution)/shard_map/ppermute | solution.py:196
  101.2 16.7 %copy-start.10 = (bf16[2,1024,128]{2,1,0:T(8,128)(2,1)S(1)}, bf16[2,1024,128]{2,1,0:T(8,128)(2,1)}, u32[]{:S(2)}) copy-start(bf16[2,1024,128]{2,1,0:T(8,128)(2,1)} %param.12) | copy-start | bytes 1572868
  102.1 21.0 %all-to-all-start.2 = ((bf16[8,256,128]{2,1,0:T(8,128)(2,1)}), bf16[8,256,128]{2,1,0:T(8,128)(2,1)S(1)}, u32[]{:S(2)}, u32[]{:S(2)}) async-start(bf16[8,256,128]{2,1,0:T(8,128)(2,1)} %broadcast_in_dim.16), calls=%async_computation.2 | async-start | bytes 1048576 | tf_op jit(solution)/shard_map/all_to_all | solution.py:188
  112.9 10.2 %copy-start.2 = (bf16[12,128,128]{2,1,0:T(8,128)(2,1)}, bf16[12,128,128]{2,1,0:T(8,128)(2,1)S(1)}, u32[]{:S(2)}) copy-start(bf16[12,128,128]{2,1,0:T(8,128)(2,1)S(1)} %collective-permute-done.8.refs_1_.refs_4_) | copy-start | bytes 1179652
  113.6 10.8 %collective-permute-start.9 = (bf16[3,12,128,128]{3,2,1,0:T(8,128)(2,1)S(1)}, bf16[3,12,128,128]{3,2,1,0:T(8,128)(2,1)}, u32[]{:S(2)}, u32[]{:S(2)}) collective-permute-start(bf16[3,12,128,128]{3,2,1,0:T(8,128)(2,1)S(1)} %stack.19), channel_id=1, source_target_pairs={{0,4},{4,0},{1,5},{5,1},{2,6},{6,2},{3,7},{7,3},{8,12},{12,8},{9,1... | collective-permute-start | bytes 3538952 | tf_op jit(solution)/shard_map/ppermute | solution.py:278
Sparse Core Ops, SparseCore 0:
  10.1 63.9 all-gather.1

commit v7 on v3

v7 whole, which is shorter than its diff:
```python
import functools

import jax
import jax.numpy as jnp
import numpy as np
from jax import lax
from jax.experimental import pallas as pl
from jax.experimental.pallas import tpu as pltpu
from jax.sharding import Mesh
from jax.sharding import PartitionSpec as P

BLOCK = 128


def factor_kernel(ys, at_ref, whole, *refs):
    pieces, others, refs = refs[:ys], refs[ys : 2 * ys], refs[2 * ys :]
    side_one, side_two, gram, right, factor, solved, trailing, residual = refs[:8]
    inv, head, panels, minuend, top, first, updated, second, sems = refs[8:]
    y, core, own = at_ref[0], at_ref[1], at_ref[2]
    size, wide = first.shape
    height = head.shape[-1]
    cols = gram.shape[1]
    f32, bf16 = jnp.float32, jnp.bfloat16

    panel_copies = [[], [], []]
    for p in range(3):
        target = head if p == 0 else panels.at[p - 1]
        for k in range(ys):
            spot = lax.rem(y + (ys - k), ys)
            for ref, half in ((pieces[k], core), (others[k], 1 - core)):
                panel_copies[p].append(
                    pltpu.make_async_copy(
                        ref.at[:, p],
                        target.at[spot, half, :, :, :height],
                        sems.at[2 * ys * p + len(panel_copies[p])],
                    )
                )
    rest_copies = [
        pltpu.make_async_copy(src, dst, sems.at[6 * ys + i])
        for i, (src, dst) in enumerate(
            (
                (whole.at[0], inv.at[0]),
                (whole.at[1], inv.at[1]),
                (side_one, panels.at[0, :, :, :, :, height:]),
                (side_two, panels.at[1, :, :, :, :, height:]),
                (gram, minuend.at[0]),
                (right, minuend.at[1]),
            )
        )
    ]
    groups = [
        rest_copies[:1] + panel_copies[0],
        panel_copies[1] + rest_copies[2:3],
        panel_copies[2] + rest_copies[3:4] + rest_copies[1:2],
        rest_copies[4:],
    ]
    for group in groups:
        for copy in group:
            copy.start()

    def wait(group):
        for copy in group:
            copy.wait()

    blocks = [slice(i * BLOCK, (i + 1) * BLOCK) for i in range(size // BLOCK)]

    def lower(k, right_of, i):
        n = (i + 1) * BLOCK
        return jnp.dot(inv[k, blocks[i], :n], right_of[:n, :], preferred_element_type=f32)

    flat_head = head.reshape(size, height)
    flat = panels.reshape(2, size, wide)

    wait(groups[0])
    for i, rows in enumerate(blocks):
        top[:, rows] = lower(0, flat_head, i).astype(bf16).T

    wait(groups[1])
    for i, rows in enumerate(blocks):
        first[rows, :] = lower(0, flat.at[0], i).astype(bf16)

    wait(groups[2])
    for rows in blocks:
        change = jnp.dot(top[rows, :], first[...], preferred_element_type=f32)
        updated[rows, :] = (flat[1, rows, :].astype(f32) - change).astype(bf16)
    for i, rows in enumerate(blocks):
        second[rows, :] = lower(1, updated, i).astype(bf16)

    solved[0] = first[:, height + cols :]
    solved[1] = second[:, height + cols :]
    mine = pl.ds(pl.multiple_of(own, 16), factor.shape[1])
    factor[0] = first[mine, :height]
    factor[1] = second[mine, :height]

    wait(groups[3])
    for j, out in enumerate((trailing, residual)):
        at = slice(height + j * cols, height + (j + 1) * cols)
        change = jnp.dot(first[:, at].T, first[:, :height], preferred_element_type=f32)
        change += jnp.dot(second[:, at].T, second[:, :height], preferred_element_type=f32)
        out[...] = minuend[j].astype(f32) - change.T


def gather_small(block, axis, size):
    flat = block.reshape(1, -1, block.shape[-1])
    out = lax.all_to_all(jnp.tile(flat, (size, 1, 1)), axis, 0, 0, tiled=True)
    return out.reshape((size,) + block.shape)


def shift(block, axis, size, by):
    return lax.ppermute(block, axis, [(i, (i + by) % size) for i in range(size)])


def per_device(sizes, panel_top, panel_low, panel_next, gram_rest, inverses, right_top, right_low):
    rows, ys, cores, voxes = sizes
    axes = ("row", "y", "core", "vox")
    order = np.arange(rows * ys * cores * voxes).reshape(sizes)
    swap = list(zip(order.ravel().tolist(), order.transpose(1, 0, 2, 3).ravel().tolist()))
    z, y = lax.axis_index("row"), lax.axis_index("y")
    core, vox = lax.axis_index("core"), lax.axis_index("vox")
    size, width = inverses.shape[2], panel_low.shape[1]
    cols = gram_rest.shape[1]
    bf16 = jnp.bfloat16
    other = [(0, 1), (1, 0)]

    whole = lax.all_gather(inverses, "row", axis=1, tiled=True)
    low, following = panel_low.T, panel_next.T
    pair = jnp.stack([low, following])
    swapped = lax.ppermute(pair, axes, swap)

    top = gather_small(panel_top.T, "row", rows).transpose(1, 0, 2).reshape(width, -1)
    top, swapped = lax.optimization_barrier((top, swapped))
    panels = gather_small(jnp.stack([top, low, following]), "vox", voxes)
    blocks = swapped.reshape(2, width, cores * voxes, cols).transpose(2, 0, 1, 3)

    up = down = panels
    pieces, others = {0: panels}, {}
    for k in range(1, ys // 2 + 1):
        if k == 2:
            up, down, blocks = lax.optimization_barrier((up, down, blocks))
        if k == 4:
            up, matching, whole = lax.optimization_barrier((up, matching, whole))
        if k == 1:
            blocks = lax.all_to_all(blocks, ("core", "vox"), 0, 0, tiled=True)
        if k == 2:
            matching = gather_small(blocks, "row", rows)
        pieces[k] = up = shift(up, "y", ys, 1)
        if k < ys - k:
            pieces[ys - k] = down = shift(down, "y", ys, -1)
    for k in range(ys):
        others[k] = lax.ppermute(pieces[k], "core", other)
    matching = jnp.moveaxis(matching, 2, 0)
    matching = matching.reshape(2, size, cols)
    sides = [jnp.concatenate([matching[k], right_top[k]], axis=1) for k in range(2)]
    sides = [side.reshape(ys, 2, voxes, width, 2 * cols) for side in sides]
    pieces = [pieces[k] for k in range(ys)]
    others = [others[k] for k in range(ys)]

    own = ((y * cores + core) * voxes + vox) * width
    where = jnp.stack([y, core, own]).astype(jnp.int32)
    height = panel_low.shape[0]
    any_space = pl.BlockSpec(memory_space=pl.ANY)
    local = pl.BlockSpec(memory_space=pltpu.VMEM)
    vmem = pltpu.VMEM
    flops = 2 * size * size * (4 * size + 10 * cols)
    factor, solved, trailing, residual = pl.pallas_call(
        functools.partial(factor_kernel, ys),
        out_shape=(
            jax.ShapeDtypeStruct((2, width, height), bf16),
            jax.ShapeDtypeStruct((2, size, cols), bf16),
            jax.ShapeDtypeStruct((height, cols), jnp.float32),
            jax.ShapeDtypeStruct((height, cols), jnp.float32),
        ),
        in_specs=[pl.BlockSpec(memory_space=pltpu.SMEM)] + [any_space] * (5 + 2 * ys),
        out_specs=(local,) * 4,
        scratch_shapes=[
            vmem((2, size, size), bf16),
            vmem((ys, cores, voxes, width, height), bf16),
            vmem((2, ys, cores, voxes, width, height + 2 * cols), bf16),
            vmem((2, height, cols), bf16),
            vmem((size, size), bf16),
            vmem((size, height + 2 * cols), bf16),
            vmem((size, height + 2 * cols), bf16),
            vmem((size, height + 2 * cols), bf16),
            pltpu.SemaphoreType.DMA((6 * ys + 6,)),
        ],
        compiler_params=pltpu.CompilerParams(vmem_limit_bytes=40 * 1024 * 1024),
        cost_estimate=pl.CostEstimate(flops=flops, bytes_accessed=14 << 20, transcendentals=0),
        name="factor_and_update",
    )(where, whole, *pieces, *others, *sides, gram_rest, right_low)
    return (factor.transpose(0, 2, 1), solved, trailing, residual)


def solution(mesh):
    cores = 2
    sizes = (mesh.shape["row"], mesh.shape["col"] // cores, cores, mesh.shape["vox"])
    split = Mesh(mesh.devices.reshape(sizes), ("row", "y", "core", "vox"))
    cols = ("y", "core", "vox")
    in_specs = (
        P("row", cols),
        P("row", cols),
        P("row", cols),
        P("row", cols),
        P(None, "row", None),
        P(None, None, cols),
        P("row", cols),
    )
    out_specs = (
        P(None, "row", cols),
        P(None, None, cols),
        P("row", cols),
        P("row", cols),
    )
    return jax.shard_map(
        functools.partial(per_device, sizes),
        mesh=split,
        in_specs=in_specs,
        out_specs=out_specs,
        check_vma=False,
    )
```

time: 143 us -> 139 us (0.972)
  Pallas kernels: 17.4 us -> 13.4 us
    pallas_call x1, Pallas kernels: 17.4 us -> 13.4 us  [per_device(): pl.pallas_call(functools.partial(factor_kernel, ys), out_shape=(jax.Shape...]
  transfers between devices with their start and end apart: 19 -> 19, of which waited for: 4 -> 3; matrix products, arithmetic and copies ran while one was open for 4% -> 5% of each run, Pallas kernels for 0% -> 0%
where the time goes in v7:
time: 139 us; the launch traced here: 138 us
  starting transfers between devices  67.3 us (48%)
  blocking collectives  21.2 us (15%)
  between operations  14.4 us (10%)
  waiting for transfers between devices  13.8 us (10%)
  Pallas kernels  13.4 us (10%)
  local copies, waits for them, and re-layouts  6.42 us (5%)
  other arithmetic  1.83 us (1%)
    ppermute x7, starting transfers between devices, shift(): lax.ppermute(block, axis, [(i, (i + by) % size) for i in range(size)])  24.4 us
    all_to_all x2, starting transfers between devices, gather_small(): out = lax.all_to_all(jnp.tile(flat, (size, 1, 1)), axis, 0, 0, tiled=True)  21.9 us
    ppermute x8, starting transfers between devices, per_device(): others[k] = lax.ppermute(pieces[k], 'core', other)  20.3 us
    pallas_call x1, Pallas kernels, per_device(): pl.pallas_call(functools.partial(factor_kernel, ys), out_shape=(jax.Shape...  13.4 us
    all_to_all x1, blocking collectives, per_device(): blocks = lax.all_to_all(blocks, ('core', 'vox'), 0, 0, tiled=True)  11.1 us
    all_to_all x1, blocking collectives, gather_small(): out = lax.all_to_all(jnp.tile(flat, (size, 1, 1)), axis, 0, 0, tiled=True)  10.1 us
    ppermute x7, waiting for transfers between devices, shift(): lax.ppermute(block, axis, [(i, (i + by) % size) for i in range(size)])  7.66 us
    all_to_all x2, waiting for transfers between devices, gather_small(): out = lax.all_to_all(jnp.tile(flat, (size, 1, 1)), axis, 0, 0, tiled=True)  5.44 us
  transfers between devices with their start and end apart: 19, of which 3 were waited for; matrix products, arithmetic and copies ran while one was open for 5% of the time, Pallas kernels for 0%

profile of v7, /device:TPU:1, one launch (start us, length us, event | category | flops | bytes accessed | tf_op | source)
XLA Modules:
  0.0 138.3 jit_solution(10627923554319257187)
XLA Ops:
  7.2 0.0 all-gather.2.cloned.1.call-start
  7.2 0.7 all-gather.2.cloned.1.call-update
  7.9 1.3 tile.10
  9.2 10.9 %all-to-all-start = ((bf16[8,16,128]{2,1,0:T(8,128)(2,1)}), bf16[8,16,128]{2,1,0:T(8,128)(2,1)S(1)}, u32[]{:S(2)}, u32[]{:S(2)}) async-start(bf16[8,16,128]{2,1,0:T(8,128)(2,1)} %tile.10), calls=%async_computation | async-start | bytes 65536 | tf_op jit(solution)/shard_map/all_to_all | solution.py:105
  20.1 0.8 pad_maximum_fusion.3
  20.9 0.7 collective-permute-start
  21.5 5.4 %all-to-all-done = bf16[8,16,128]{2,1,0:T(8,128)(2,1)S(1)} async-done(((bf16[8,16,128]{2,1,0:T(8,128)(2,1)}), bf16[8,16,128]{2,1,0:T(8,128)(2,1)S(1)}, u32[]{:S(2)}, u32[]{:S(2)}) %all-to-all-start) | async-done | bytes 32800 | tf_op jit(solution)/shard_map/all_to_all | solution.py:105
  27.0 0.0 collective-permute-done
  27.0 0.8 pad_maximum_fusion.2
  27.8 10.1 %all_to_all.20 = bf16[4,48,1024]{2,1,0:T(8,128)(2,1)S(1)} all-to-all(bf16[4,48,1024]{2,1,0:T(8,128)(2,1)S(1)} %tile.24), channel_id=1, replica_groups=mesh['row'=8,'y'=8,'core'=2,'vox'=4] {'vox'}, dimensions={0} | all-to-all | bytes 786432 | tf_op jit(solution)/shard_map/all_to_all | solution.py:105
  37.9 7.3 %collective-permute-start.2 = (bf16[4,3,16,1024]{3,2,1,0:T(8,128)(2,1)S(1)}, bf16[4,3,16,1024]{3,2,1,0:T(8,128)(2,1)S(1)}, u32[]{:S(2)}, u32[]{:S(2)}) collective-permute-start(bf16[4,3,16,1024]{3,2,1,0:T(8,128)(2,1)S(1)} %bitcast.35), channel_id=1, source_target_pairs={{0,56},{8,0},{16,8},{24,16},{32,24},{40,32},{48,40},{56,48},{1,57}... | collective-permute-start | bytes 1179656 | tf_op jit(solution)/shard_map/ppermute | solution.py:110
  45.2 1.9 %collective-permute-start.1 = (bf16[4,3,16,1024]{3,2,1,0:T(8,128)(2,1)S(1)}, bf16[4,3,16,1024]{3,2,1,0:T(8,128)(2,1)S(1)}, u32[]{:S(2)}, u32[]{:S(2)}) collective-permute-start(bf16[4,3,16,1024]{3,2,1,0:T(8,128)(2,1)S(1)} %bitcast.36), channel_id=1, source_target_pairs={{0,8},{8,16},{16,24},{24,32},{32,40},{40,48},{48,56},{56,0},{1,9},... | collective-permute-start | bytes 1179656 | tf_op jit(solution)/shard_map/ppermute | solution.py:110
  47.2 11.1 %all_to_all.21 = bf16[8,2,16,128]{3,2,1,0:T(8,128)(2,1)S(1)} all-to-all(bf16[8,2,16,128]{3,2,1,0:T(8,128)(2,1)S(1)} %copy.14), channel_id=1, replica_groups=mesh['row'=8,'y'=8,'core'=2,'vox'=4] {'core','vox'}, dimensions={0} | all-to-all | bytes 131072 | tf_op jit(solution)/shard_map/all_to_all | solution.py:143
  58.3 0.0 collective-permute-done.2.refs_7_
  58.3 0.0 collective-permute-done.1.refs_1_
  58.3 0.9 tile.26
  59.2 11.0 %all-to-all-start.3 = ((bf16[8,256,128]{2,1,0:T(8,128)(2,1)}), bf16[8,256,128]{2,1,0:T(8,128)(2,1)}, u32[]{:S(2)}, u32[]{:S(2)}) async-start(bf16[8,256,128]{2,1,0:T(8,128)(2,1)} %tile.26), calls=%async_computation.3 | async-start | bytes 1048576 | tf_op jit(solution)/shard_map/all_to_all | solution.py:105
  70.2 2.2 %collective-permute-start.3 = (bf16[4,3,16,1024]{3,2,1,0:T(8,128)(2,1)S(1)}, bf16[4,3,16,1024]{3,2,1,0:T(8,128)(2,1)S(1)}, u32[]{:S(2)}, u32[]{:S(2)}) collective-permute-start(bf16[4,3,16,1024]{3,2,1,0:T(8,128)(2,1)S(1)} %collective-permute-done.1.refs_1_), channel_id=1, source_target_pairs={{0,8},{8,16},{16,24},{24,32},{32,40},{40,48},{48,56},{56,0},{1,9},... | collective-permute-start | bytes 1179656 | tf_op jit(solution)/shard_map/ppermute | solution.py:110
  72.4 4.3 %collective-permute-start.6 = (bf16[4,3,16,1024]{3,2,1,0:T(8,128)(2,1)S(1)}, bf16[4,3,16,1024]{3,2,1,0:T(8,128)(2,1)S(1)}, u32[]{:S(2)}, u32[]{:S(2)}) collective-permute-start(bf16[4,3,16,1024]{3,2,1,0:T(8,128)(2,1)S(1)} %collective-permute-done.2.refs_7_), channel_id=1, source_target_pairs={{0,56},{8,0},{16,8},{24,16},{32,24},{40,32},{48,40},{56,48},{1,57}... | collective-permute-start | bytes 1179656 | tf_op jit(solution)/shard_map/ppermute | solution.py:110
  76.7 6.1 %collective-permute-done.3.refs_2_ = bf16[4,3,16,1024]{3,2,1,0:T(8,128)(2,1)S(1)} collective-permute-done((bf16[4,3,16,1024]{3,2,1,0:T(8,128)(2,1)S(1)}, bf16[4,3,16,1024]{3,2,1,0:T(8,128)(2,1)S(1)}, u32[]{:S(2)}, u32[]{:S(2)}) %collective-permute-start.3) | collective-permute-done | bytes 393248 | tf_op jit(solution)/shard_map/ppermute | solution.py:110
  82.7 1.9 %collective-permute-start.4 = (bf16[4,3,16,1024]{3,2,1,0:T(8,128)(2,1)S(1)}, bf16[4,3,16,1024]{3,2,1,0:T(8,128)(2,1)S(1)}, u32[]{:S(2)}, u32[]{:S(2)}) collective-permute-start(bf16[4,3,16,1024]{3,2,1,0:T(8,128)(2,1)S(1)} %collective-permute-done.3.refs_2_), channel_id=1, source_target_pairs={{0,8},{8,16},{16,24},{24,32},{32,40},{40,48},{48,56},{56,0},{1,9},... | collective-permute-start | bytes 1179656 | tf_op jit(solution)/shard_map/ppermute | solution.py:110
  84.7 4.0 %collective-permute-start.8 = (bf16[4,3,16,1024]{3,2,1,0:T(8,128)(2,1)S(1)}, bf16[4,3,16,1024]{3,2,1,0:T(8,128)(2,1)S(1)}, u32[]{:S(2)}, u32[]{:S(2)}) collective-permute-start(bf16[4,3,16,1024]{3,2,1,0:T(8,128)(2,1)S(1)} %bitcast.37), channel_id=1, source_target_pairs={{0,4},{4,0},{1,5},{5,1},{2,6},{6,2},{3,7},{7,3},{8,12},{12,8},{9,1... | collective-permute-start | bytes 1179656 | tf_op jit(solution)/shard_map/ppermute | solution.py:150
  88.6 1.9 %collective-permute-start.15 = (bf16[4,3,16,1024]{3,2,1,0:T(8,128)(2,1)S(1)}, bf16[4,3,16,1024]{3,2,1,0:T(8,128)(2,1)S(1)}, u32[]{:S(2)}, u32[]{:S(2)}) collective-permute-start(bf16[4,3,16,1024]{3,2,1,0:T(8,128)(2,1)S(1)} %collective-permute-done.2.refs_7_), channel_id=1, source_target_pairs={{0,4},{4,0},{1,5},{5,1},{2,6},{6,2},{3,7},{7,3},{8,12},{12,8},{9,1... | collective-permute-start | bytes 1179656 | tf_op jit(solution)/shard_map/ppermute | solution.py:150
  90.6 2.4 %collective-permute-start.9 = (bf16[4,3,16,1024]{3,2,1,0:T(8,128)(2,1)S(1)}, bf16[4,3,16,1024]{3,2,1,0:T(8,128)(2,1)S(1)}, u32[]{:S(2)}, u32[]{:S(2)}) collective-permute-start(bf16[4,3,16,1024]{3,2,1,0:T(8,128)(2,1)S(1)} %collective-permute-done.1.refs_1_), channel_id=1, source_target_pairs={{0,4},{4,0},{1,5},{5,1},{2,6},{6,2},{3,7},{7,3},{8,12},{12,8},{9,1... | collective-permute-start | bytes 1179656 | tf_op jit(solution)/shard_map/ppermute | solution.py:150
  93.0 0.0 collective-permute-done.6.refs_6_
  93.0 4.9 %collective-permute-start.7 = (bf16[4,3,16,1024]{3,2,1,0:T(8,128)(2,1)S(1)}, bf16[4,3,16,1024]{3,2,1,0:T(8,128)(2,1)}, u32[]{:S(2)}, u32[]{:S(2)}) collective-permute-start(bf16[4,3,16,1024]{3,2,1,0:T(8,128)(2,1)S(1)} %collective-permute-done.6.refs_6_), channel_id=1, source_target_pairs={{0,56},{8,0},{16,8},{24,16},{32,24},{40,32},{48,40},{56,48},{1,57}... | collective-permute-start | bytes 1179656 | tf_op jit(solution)/shard_map/ppermute | solution.py:110
  97.9 0.0 collective-permute-done.4.refs_3_
  97.9 0.0 all-to-all-done.3
  97.9 0.0 all-gather.2.cloned.1.call-done.whole
  97.9 1.9 %collective-permute-start.5 = (bf16[4,3,16,1024]{3,2,1,0:T(8,128)(2,1)S(1)}, bf16[4,3,16,1024]{3,2,1,0:T(8,128)(2,1)}, u32[]{:S(2)}, u32[]{:S(2)}) collective-permute-start(bf16[4,3,16,1024]{3,2,1,0:T(8,128)(2,1)S(1)} %collective-permute-done.4.refs_3_), channel_id=1, source_target_pairs={{0,8},{8,16},{16,24},{24,32},{32,40},{40,48},{48,56},{56,0},{1,9},... | collective-permute-start | bytes 1179656 | tf_op jit(solution)/shard_map/ppermute | solution.py:110
  99.9 1.2 fusion.1
  101.1 2.3 %collective-permute-start.10 = (bf16[4,3,16,1024]{3,2,1,0:T(8,128)(2,1)S(1)}, bf16[4,3,16,1024]{3,2,1,0:T(8,128)(2,1)S(1)}, u32[]{:S(2)}, u32[]{:S(2)}) collective-permute-start(bf16[4,3,16,1024]{3,2,1,0:T(8,128)(2,1)S(1)} %collective-permute-done.3.refs_2_), channel_id=1, source_target_pairs={{0,4},{4,0},{1,5},{5,1},{2,6},{6,2},{3,7},{7,3},{8,12},{12,8},{9,1... | collective-permute-start | bytes 1179656 | tf_op jit(solution)/shard_map/ppermute | solution.py:150
  103.4 0.0 collective-permute-done.15.refs_15_
  103.4 2.1 %collective-permute-start.14 = (bf16[4,3,16,1024]{3,2,1,0:T(8,128)(2,1)S(1)}, bf16[4,3,16,1024]{3,2,1,0:T(8,128)(2,1)S(1)}, u32[]{:S(2)}, u32[]{:S(2)}) collective-permute-start(bf16[4,3,16,1024]{3,2,1,0:T(8,128)(2,1)S(1)} %collective-permute-done.6.refs_6_), channel_id=1, source_target_pairs={{0,4},{4,0},{1,5},{5,1},{2,6},{6,2},{3,7},{7,3},{8,12},{12,8},{9,1... | collective-permute-start | bytes 1179656 | tf_op jit(solution)/shard_map/ppermute | solution.py:150
  105.6 2.2 %collective-permute-start.11 = (bf16[4,3,16,1024]{3,2,1,0:T(8,128)(2,1)S(1)}, bf16[4,3,16,1024]{3,2,1,0:T(8,128)(2,1)S(1)}, u32[]{:S(2)}, u32[]{:S(2)}) collective-permute-start(bf16[4,3,16,1024]{3,2,1,0:T(8,128)(2,1)S(1)} %collective-permute-done.4.refs_3_), channel_id=1, source_target_pairs={{0,4},{4,0},{1,5},{5,1},{2,6},{6,2},{3,7},{7,3},{8,12},{12,8},{9,1... | collective-permute-start | bytes 1179656 | tf_op jit(solution)/shard_map/ppermute | solution.py:150
  107.8 0.0 collective-permute-done.7.refs_5_
  107.8 2.1 %collective-permute-start.13 = (bf16[4,3,16,1024]{3,2,1,0:T(8,128)(2,1)}, bf16[4,3,16,1024]{3,2,1,0:T(8,128)(2,1)S(1)}, u32[]{:S(2)}, u32[]{:S(2)}) collective-permute-start(bf16[4,3,16,1024]{3,2,1,0:T(8,128)(2,1)} %collective-permute-done.7.refs_5_), channel_id=1, source_target_pairs={{0,4},{4,0},{1,5},{5,1},{2,6},{6,2},{3,7},{7,3},{8,12},{12,8},{9,1... | collective-permute-start | bytes 1179656 | tf_op jit(solution)/shard_map/ppermute | solution.py:150
  109.9 1.6 %collective-permute-done.5.refs_4_ = bf16[4,3,16,1024]{3,2,1,0:T(8,128)(2,1)} collective-permute-done((bf16[4,3,16,1024]{3,2,1,0:T(8,128)(2,1)S(1)}, bf16[4,3,16,1024]{3,2,1,0:T(8,128)(2,1)}, u32[]{:S(2)}, u32[]{:S(2)}) %collective-permute-start.5) | collective-permute-done | bytes 393248 | tf_op jit(solution)/shard_map/ppermute | solution.py:110
  111.5 3.2 %collective-permute-start.12 = (bf16[4,3,16,1024]{3,2,1,0:T(8,128)(2,1)}, bf16[4,3,16,1024]{3,2,1,0:T(8,128)(2,1)S(1)}, u32[]{:S(2)}, u32[]{:S(2)}) collective-permute-start(bf16[4,3,16,1024]{3,2,1,0:T(8,128)(2,1)} %collective-permute-done.5.refs_4_), channel_id=1, source_target_pairs={{0,4},{4,0},{1,5},{5,1},{2,6},{6,2},{3,7},{7,3},{8,12},{12,8},{9,1... | collective-permute-start | bytes 1179656 | tf_op jit(solution)/shard_map/ppermute | solution.py:150
  114.7 0.1 pad_add_fusion.at_ref
  114.8 1.1 fusion
  115.9 0.2 pad_maximum_fusion
  116.1 0.0 collective-permute-done.10.refs_10_
  116.1 0.0 collective-permute-done.13.refs_13_
  116.1 0.0 copy-start.1
  116.2 0.9 copy-done.1
  117.1 0.9 copy-done.2
  118.0 13.4 %factor_and_update.1 = (bf16[2,16,1024]{2,1,0:T(8,128)(2,1)}, bf16[2,1024,128]{2,1,0:T(8,128)(2,1)}, f32[1024,128]{1,0:T(8,128)}, f32[1024,128]{1,0:T(8,128)}) custom-call(s32[3]{0:T(128)S(1)} %pad_add_fusion.at_ref, bf16[2,1024,1024]{2,1,0:T(8,128)(2,1)S(1)} %copy-done, bf16[4,3,16,1024]{3,2,1,0:T(8,128)(2,1)S(1)} %bitcast.38, ...), custom_call_target="tpu_custom_call" | custom-call | flops 11274289152 | bytes 14680064 | tf_op jit(solution)/shard_map/factor_and_update/pallas_call | solution.py:165
  (13 shorter events, 0.1 us)
Async XLA Ops:
  7.2 90.7 %all-gather.2.cloned.1.call-start = ((), (), s32[]{:S(2)}) async-start(), calls=%async_computation.4 | async-start | bytes 4718592 | tf_op jit(solution)/shard_map/all_gather | solution.py:125
  9.2 17.7 %all-to-all-start = ((bf16[8,16,128]{2,1,0:T(8,128)(2,1)}), bf16[8,16,128]{2,1,0:T(8,128)(2,1)S(1)}, u32[]{:S(2)}, u32[]{:S(2)}) async-start(bf16[8,16,128]{2,1,0:T(8,128)(2,1)} %tile.10), calls=%async_computation | async-start | bytes 65536 | tf_op jit(solution)/shard_map/all_to_all | solution.py:105
  20.9 6.1 %collective-permute-start = (bf16[2,16,1024]{2,1,0:T(8,128)(2,1)S(1)}, bf16[2,16,1024]{2,1,0:T(8,128)(2,1)S(1)}, u32[]{:S(2)}, u32[]{:S(2)}) collective-permute-start(bf16[2,16,1024]{2,1,0:T(8,128)(2,1)S(1)} %pad_maximum_fusion.3), channel_id=1, source_target_pairs={{0,0},{1,1},{2,2},{3,3},{4,4},{5,5},{6,6},{7,7},{8,64},{9,65},{10,... | collective-permute-start | bytes 196616 | tf_op jit(solution)/shard_map/ppermute | solution.py:128
  37.9 20.4 %collective-permute-start.2 = (bf16[4,3,16,1024]{3,2,1,0:T(8,128)(2,1)S(1)}, bf16[4,3,16,1024]{3,2,1,0:T(8,128)(2,1)S(1)}, u32[]{:S(2)}, u32[]{:S(2)}) collective-permute-start(bf16[4,3,16,1024]{3,2,1,0:T(8,128)(2,1)S(1)} %bitcast.35), channel_id=1, source_target_pairs={{0,56},{8,0},{16,8},{24,16},{32,24},{40,32},{48,40},{56,48},{1,57}... | collective-permute-start | bytes 1179656 | tf_op jit(solution)/shard_map/ppermute | solution.py:110
  45.2 13.1 %collective-permute-start.1 = (bf16[4,3,16,1024]{3,2,1,0:T(8,128)(2,1)S(1)}, bf16[4,3,16,1024]{3,2,1,0:T(8,128)(2,1)S(1)}, u32[]{:S(2)}, u32[]{:S(2)}) collective-permute-start(bf16[4,3,16,1024]{3,2,1,0:T(8,128)(2,1)S(1)} %bitcast.36), channel_id=1, source_target_pairs={{0,8},{8,16},{16,24},{24,32},{32,40},{40,48},{48,56},{56,0},{1,9},... | collective-permute-start | bytes 1179656 | tf_op jit(solution)/shard_map/ppermute | solution.py:110
  59.2 38.7 %all-to-all-start.3 = ((bf16[8,256,128]{2,1,0:T(8,128)(2,1)}), bf16[8,256,128]{2,1,0:T(8,128)(2,1)}, u32[]{:S(2)}, u32[]{:S(2)}) async-start(bf16[8,256,128]{2,1,0:T(8,128)(2,1)} %tile.26), calls=%async_computation.3 | async-start | bytes 1048576 | tf_op jit(solution)/shard_map/all_to_all | solution.py:105
  70.2 12.5 %collective-permute-start.3 = (bf16[4,3,16,1024]{3,2,1,0:T(8,128)(2,1)S(1)}, bf16[4,3,16,1024]{3,2,1,0:T(8,128)(2,1)S(1)}, u32[]{:S(2)}, u32[]{:S(2)}) collective-permute-start(bf16[4,3,16,1024]{3,2,1,0:T(8,128)(2,1)S(1)} %collective-permute-done.1.refs_1_), channel_id=1, source_target_pairs={{0,8},{8,16},{16,24},{24,32},{32,40},{40,48},{48,56},{56,0},{1,9},... | collective-permute-start | bytes 1179656 | tf_op jit(solution)/shard_map/ppermute | solution.py:110
  72.4 20.6 %collective-permute-start.6 = (bf16[4,3,16,1024]{3,2,1,0:T(8,128)(2,1)S(1)}, bf16[4,3,16,1024]{3,2,1,0:T(8,128)(2,1)S(1)}, u32[]{:S(2)}, u32[]{:S(2)}) collective-permute-start(bf16[4,3,16,1024]{3,2,1,0:T(8,128)(2,1)S(1)} %collective-permute-done.2.refs_7_), channel_id=1, source_target_pairs={{0,56},{8,0},{16,8},{24,16},{32,24},{40,32},{48,40},{56,48},{1,57}... | collective-permute-start | bytes 1179656 | tf_op jit(solution)/shard_map/ppermute | solution.py:110
  82.7 15.1 %collective-permute-start.4 = (bf16[4,3,16,1024]{3,2,1,0:T(8,128)(2,1)S(1)}, bf16[4,3,16,1024]{3,2,1,0:T(8,128)(2,1)S(1)}, u32[]{:S(2)}, u32[]{:S(2)}) collective-permute-start(bf16[4,3,16,1024]{3,2,1,0:T(8,128)(2,1)S(1)} %collective-permute-done.3.refs_2_), channel_id=1, source_target_pairs={{0,8},{8,16},{16,24},{24,32},{32,40},{40,48},{48,56},{56,0},{1,9},... | collective-permute-start | bytes 1179656 | tf_op jit(solution)/shard_map/ppermute | solution.py:110
  84.7 16.4 %collective-permute-start.8 = (bf16[4,3,16,1024]{3,2,1,0:T(8,128)(2,1)S(1)}, bf16[4,3,16,1024]{3,2,1,0:T(8,128)(2,1)S(1)}, u32[]{:S(2)}, u32[]{:S(2)}) collective-permute-start(bf16[4,3,16,1024]{3,2,1,0:T(8,128)(2,1)S(1)} %bitcast.37), channel_id=1, source_target_pairs={{0,4},{4,0},{1,5},{5,1},{2,6},{6,2},{3,7},{7,3},{8,12},{12,8},{9,1... | collective-permute-start | bytes 1179656 | tf_op jit(solution)/shard_map/ppermute | solution.py:150
  88.6 14.8 %collective-permute-start.15 = (bf16[4,3,16,1024]{3,2,1,0:T(8,128)(2,1)S(1)}, bf16[4,3,16,1024]{3,2,1,0:T(8,128)(2,1)S(1)}, u32[]{:S(2)}, u32[]{:S(2)}) collective-permute-start(bf16[4,3,16,1024]{3,2,1,0:T(8,128)(2,1)S(1)} %collective-permute-done.2.refs_7_), channel_id=1, source_target_pairs={{0,4},{4,0},{1,5},{5,1},{2,6},{6,2},{3,7},{7,3},{8,12},{12,8},{9,1... | collective-permute-start | bytes 1179656 | tf_op jit(solution)/shard_map/ppermute | solution.py:150
  90.6 15.0 %collective-permute-start.9 = (bf16[4,3,16,1024]{3,2,1,0:T(8,128)(2,1)S(1)}, bf16[4,3,16,1024]{3,2,1,0:T(8,128)(2,1)S(1)}, u32[]{:S(2)}, u32[]{:S(2)}) collective-permute-start(bf16[4,3,16,1024]{3,2,1,0:T(8,128)(2,1)S(1)} %collective-permute-done.1.refs_1_), channel_id=1, source_target_pairs={{0,4},{4,0},{1,5},{5,1},{2,6},{6,2},{3,7},{7,3},{8,12},{12,8},{9,1... | collective-permute-start | bytes 1179656 | tf_op jit(solution)/shard_map/ppermute | solution.py:150
  93.0 14.8 %collective-permute-start.7 = (bf16[4,3,16,1024]{3,2,1,0:T(8,128)(2,1)S(1)}, bf16[4,3,16,1024]{3,2,1,0:T(8,128)(2,1)}, u32[]{:S(2)}, u32[]{:S(2)}) collective-permute-start(bf16[4,3,16,1024]{3,2,1,0:T(8,128)(2,1)S(1)} %collective-permute-done.6.refs_6_), channel_id=1, source_target_pairs={{0,56},{8,0},{16,8},{24,16},{32,24},{40,32},{48,40},{56,48},{1,57}... | collective-permute-start | bytes 1179656 | tf_op jit(solution)/shard_map/ppermute | solution.py:110
  97.9 13.6 %collective-permute-start.5 = (bf16[4,3,16,1024]{3,2,1,0:T(8,128)(2,1)S(1)}, bf16[4,3,16,1024]{3,2,1,0:T(8,128)(2,1)}, u32[]{:S(2)}, u32[]{:S(2)}) collective-permute-start(bf16[4,3,16,1024]{3,2,1,0:T(8,128)(2,1)S(1)} %collective-permute-done.4.refs_3_), channel_id=1, source_target_pairs={{0,8},{8,16},{16,24},{24,32},{32,40},{40,48},{48,56},{56,0},{1,9},... | collective-permute-start | bytes 1179656 | tf_op jit(solution)/shard_map/ppermute | solution.py:110
  99.8 16.3 %copy-start = (bf16[2,1024,1024]{2,1,0:T(8,128)(2,1)S(1)}, bf16[2,1024,1024]{2,1,0:T(8,128)(2,1)}, u32[]{:S(2)}) copy-start(bf16[2,1024,1024]{2,1,0:T(8,128)(2,1)} %all-gather.2.cloned.1.call-done.whole) | copy-start | bytes 12582916
  101.1 15.0 %collective-permute-start.10 = (bf16[4,3,16,1024]{3,2,1,0:T(8,128)(2,1)S(1)}, bf16[4,3,16,1024]{3,2,1,0:T(8,128)(2,1)S(1)}, u32[]{:S(2)}, u32[]{:S(2)}) collective-permute-start(bf16[4,3,16,1024]{3,2,1,0:T(8,128)(2,1)S(1)} %collective-permute-done.3.refs_2_), channel_id=1, source_target_pairs={{0,4},{4,0},{1,5},{5,1},{2,6},{6,2},{3,7},{7,3},{8,12},{12,8},{9,1... | collective-permute-start | bytes 1179656 | tf_op jit(solution)/shard_map/ppermute | solution.py:150
  103.4 12.7 %collective-permute-start.14 = (bf16[4,3,16,1024]{3,2,1,0:T(8,128)(2,1)S(1)}, bf16[4,3,16,1024]{3,2,1,0:T(8,128)(2,1)S(1)}, u32[]{:S(2)}, u32[]{:S(2)}) collective-permute-start(bf16[4,3,16,1024]{3,2,1,0:T(8,128)(2,1)S(1)} %collective-permute-done.6.refs_6_), channel_id=1, source_target_pairs={{0,4},{4,0},{1,5},{5,1},{2,6},{6,2},{3,7},{7,3},{8,12},{12,8},{9,1... | collective-permute-start | bytes 1179656 | tf_op jit(solution)/shard_map/ppermute | solution.py:150
  105.6 10.5 %collective-permute-start.11 = (bf16[4,3,16,1024]{3,2,1,0:T(8,128)(2,1)S(1)}, bf16[4,3,16,1024]{3,2,1,0:T(8,128)(2,1)S(1)}, u32[]{:S(2)}, u32[]{:S(2)}) collective-permute-start(bf16[4,3,16,1024]{3,2,1,0:T(8,128)(2,1)S(1)} %collective-permute-done.4.refs_3_), channel_id=1, source_target_pairs={{0,4},{4,0},{1,5},{5,1},{2,6},{6,2},{3,7},{7,3},{8,12},{12,8},{9,1... | collective-permute-start | bytes 1179656 | tf_op jit(solution)/shard_map/ppermute | solution.py:150
  107.8 8.3 %collective-permute-start.13 = (bf16[4,3,16,1024]{3,2,1,0:T(8,128)(2,1)}, bf16[4,3,16,1024]{3,2,1,0:T(8,128)(2,1)S(1)}, u32[]{:S(2)}, u32[]{:S(2)}) collective-permute-start(bf16[4,3,16,1024]{3,2,1,0:T(8,128)(2,1)} %collective-permute-done.7.refs_5_), channel_id=1, source_target_pairs={{0,4},{4,0},{1,5},{5,1},{2,6},{6,2},{3,7},{7,3},{8,12},{12,8},{9,1... | collective-permute-start | bytes 1179656 | tf_op jit(solution)/shard_map/ppermute | solution.py:150
  111.5 4.6 %collective-permute-start.12 = (bf16[4,3,16,1024]{3,2,1,0:T(8,128)(2,1)}, bf16[4,3,16,1024]{3,2,1,0:T(8,128)(2,1)S(1)}, u32[]{:S(2)}, u32[]{:S(2)}) collective-permute-start(bf16[4,3,16,1024]{3,2,1,0:T(8,128)(2,1)} %collective-permute-done.5.refs_4_), channel_id=1, source_target_pairs={{0,4},{4,0},{1,5},{5,1},{2,6},{6,2},{3,7},{7,3},{8,12},{12,8},{9,1... | collective-permute-start | bytes 1179656 | tf_op jit(solution)/shard_map/ppermute | solution.py:150
  116.1 1.0 copy-start.1
  117.1 0.9 copy-start.2
Sparse Core Ops, SparseCore 0:
  10.1 63.7 all-gather.1

commit v8 on v7

--- a/solution.py
+++ b/solution.py
@@ -12,8 +12,10 @@
 BLOCK = 128
 
 
-def factor_kernel(ys, at_ref, whole, *refs):
-    pieces, others, refs = refs[:ys], refs[ys : 2 * ys], refs[2 * ys :]
+def factor_kernel(ys, near, rest, at_ref, whole, *refs):
+    pieces, far_near, far_rest, refs = refs[:ys], refs[ys], refs[ys + 1], refs[ys + 2 :]
+    others = {k: far_near.at[i] for i, k in enumerate(near)}
+    others |= {k: far_rest.at[i] for i, k in enumerate(rest)}
     side_one, side_two, gram, right, factor, solved, trailing, residual = refs[:8]
     inv, head, panels, minuend, top, first, updated, second, sems = refs[8:]
     y, core, own = at_ref[0], at_ref[1], at_ref[2]
@@ -106,6 +108,30 @@
     return out.reshape((size,) + block.shape)
 
 
+def stack_kernel(*refs):
+    pieces, stacked, sems = refs[:-2], refs[-2], refs[-1]
+    copies = [
+        pltpu.make_async_copy(ref, stacked.at[i], sems.at[i]) for i, ref in enumerate(pieces)
+    ]
+    for copy in copies:
+        copy.start()
+    for copy in copies:
+        copy.wait()
+
+
+def stack(pieces):
+    anywhere = pl.BlockSpec(memory_space=pl.ANY)
+    return pl.pallas_call(
+        stack_kernel,
+        name="stack",
+        out_shape=jax.ShapeDtypeStruct((len(pieces),) + pieces[0].shape, pieces[0].dtype),
+        in_specs=[anywhere] * len(pieces),
+        out_specs=anywhere,
+        scratch_shapes=[pltpu.SemaphoreType.DMA((len(pieces),))],
+        compiler_params=pltpu.CompilerParams(vmem_limit_bytes=1 << 20),
+    )(*pieces)
+
+
 def shift(block, axis, size, by):
     return lax.ppermute(block, axis, [(i, (i + by) % size) for i in range(size)])
 
@@ -133,7 +159,7 @@
     blocks = swapped.reshape(2, width, cores * voxes, cols).transpose(2, 0, 1, 3)
 
     up = down = panels
-    pieces, others = {0: panels}, {}
+    pieces = {0: panels}
     for k in range(1, ys // 2 + 1):
         if k == 2:
             up, down, blocks = lax.optimization_barrier((up, down, blocks))
@@ -146,14 +172,16 @@
         pieces[k] = up = shift(up, "y", ys, 1)
         if k < ys - k:
             pieces[ys - k] = down = shift(down, "y", ys, -1)
-    for k in range(ys):
-        others[k] = lax.ppermute(pieces[k], "core", other)
+        if k == 3:
+            near = sorted(j % ys for j in range(-2, 3))
+            far_near = lax.ppermute(stack([pieces[j] for j in near]), "core", other)
+    rest = [k for k in range(ys) if k not in near]
+    far_rest = lax.ppermute(stack([pieces[k] for k in rest]), "core", other)
     matching = jnp.moveaxis(matching, 2, 0)
     matching = matching.reshape(2, size, cols)
     sides = [jnp.concatenate([matching[k], right_top[k]], axis=1) for k in range(2)]
     sides = [side.reshape(ys, 2, voxes, width, 2 * cols) for side in sides]
     pieces = [pieces[k] for k in range(ys)]
-    others = [others[k] for k in range(ys)]
 
     own = ((y * cores + core) * voxes + vox) * width
     where = jnp.stack([y, core, own]).astype(jnp.int32)
@@ -163,14 +191,14 @@
     vmem = pltpu.VMEM
     flops = 2 * size * size * (4 * size + 10 * cols)
     factor, solved, trailing, residual = pl.pallas_call(
-        functools.partial(factor_kernel, ys),
+        functools.partial(factor_kernel, ys, near, rest),
         out_shape=(
             jax.ShapeDtypeStruct((2, width, height), bf16),
             jax.ShapeDtypeStruct((2, size, cols), bf16),
             jax.ShapeDtypeStruct((height, cols), jnp.float32),
             jax.ShapeDtypeStruct((height, cols), jnp.float32),
         ),
-        in_specs=[pl.BlockSpec(memory_space=pltpu.SMEM)] + [any_space] * (5 + 2 * ys),
+        in_specs=[pl.BlockSpec(memory_space=pltpu.SMEM)] + [any_space] * (7 + ys),
         out_specs=(local,) * 4,
         scratch_shapes=[
             vmem((2, size, size), bf16),
@@ -183,10 +211,10 @@
             vmem((size, height + 2 * cols), bf16),
             pltpu.SemaphoreType.DMA((6 * ys + 6,)),
         ],
-        compiler_params=pltpu.CompilerParams(vmem_limit_bytes=40 * 1024 * 1024),
+        compiler_params=pltpu.CompilerParams(vmem_limit_bytes=56 * 1024 * 1024),
         cost_estimate=pl.CostEstimate(flops=flops, bytes_accessed=14 << 20, transcendentals=0),
         name="factor_and_update",
-    )(where, whole, *pieces, *others, *sides, gram_rest, right_low)
+    )(where, whole, *pieces, far_near, far_rest, *sides, gram_rest, right_low)
     return (factor.transpose(0, 2, 1), solved, trailing, residual)
 
 

time: 139 us -> 141 us (1.014)
  starting transfers between devices: 67.3 us -> 56.9 us
  waiting for transfers between devices: 13.8 us -> 21.7 us
  Pallas kernels: 13.4 us -> 16 us
  other arithmetic: 1.83 us -> 3.43 us
    ppermute x8 -> x2, starting transfers between devices: 20.3 us -> 8.66 us  [the longest x1 5.26 us: per_device(): far_rest = lax.ppermute(stack([pieces[k] for k in rest]), 'core', other)]
    ppermute x7, waiting for transfers between devices: 7.66 us -> 15.6 us  [shift(): lax.ppermute(block, axis, [(i, (i + by) % size) for i in range(size)])]
    pallas_call x1 -> x3, Pallas kernels: 13.4 us -> 16 us  [the longest x1 13.8 us: per_device(): pl.pallas_call(functools.partial(factor_kernel, ys, near, rest), out_shap...]
  transfers between devices with their start and end apart: 19 -> 13, of which waited for: 3 -> 5; matrix products, arithmetic and copies ran while one was open for 5% -> 6% of each run, Pallas kernels for 0% -> 2%
where the time goes in v8:
time: 141 us; the launch traced here: 140 us
  starting transfers between devices  56.9 us (40%)
  waiting for transfers between devices  21.7 us (15%)
  blocking collectives  21.2 us (15%)
  Pallas kernels  16 us (11%)
  between operations  14.3 us (10%)
  local copies, waits for them, and re-layouts  6.24 us (4%)
  other arithmetic  3.43 us (2%)
    ppermute x7, starting transfers between devices, shift(): lax.ppermute(block, axis, [(i, (i + by) % size) for i in range(size)])  24.4 us
    all_to_all x2, starting transfers between devices, gather_small(): out = lax.all_to_all(jnp.tile(flat, (size, 1, 1)), axis, 0, 0, tiled=True)  23.1 us
    ppermute x7, waiting for transfers between devices, shift(): lax.ppermute(block, axis, [(i, (i + by) % size) for i in range(size)])  15.6 us
    pallas_call x1, Pallas kernels, per_device(): pl.pallas_call(functools.partial(factor_kernel, ys, near, rest), out_shap...  13.8 us
    all_to_all x1, blocking collectives, per_device(): blocks = lax.all_to_all(blocks, ('core', 'vox'), 0, 0, tiled=True)  11.1 us
    all_to_all x1, blocking collectives, gather_small(): out = lax.all_to_all(jnp.tile(flat, (size, 1, 1)), axis, 0, 0, tiled=True)  10.1 us
    all_to_all x2, waiting for transfers between devices, gather_small(): out = lax.all_to_all(jnp.tile(flat, (size, 1, 1)), axis, 0, 0, tiled=True)  5.44 us
    ppermute x1, starting transfers between devices, per_device(): far_rest = lax.ppermute(stack([pieces[k] for k in rest]), 'core', other)  5.26 us
  transfers between devices with their start and end apart: 13, of which 5 were waited for; matrix products, arithmetic and copies ran while one was open for 6% of the time, Pallas kernels for 2%

profile of v8, /device:TPU:1, one launch (start us, length us, event | category | flops | bytes accessed | tf_op | source)
XLA Modules:
  0.0 139.7 jit_solution(7912983451941340739)
XLA Ops:
  7.2 0.0 all-gather.2.cloned.1.call-start
  7.2 0.7 all-gather.2.cloned.1.call-update
  7.9 1.3 tile.10
  9.2 10.9 %all-to-all-start = ((bf16[8,16,128]{2,1,0:T(8,128)(2,1)}), bf16[8,16,128]{2,1,0:T(8,128)(2,1)S(1)}, u32[]{:S(2)}, u32[]{:S(2)}) async-start(bf16[8,16,128]{2,1,0:T(8,128)(2,1)} %tile.10), calls=%async_computation | async-start | bytes 65536 | tf_op jit(solution)/shard_map/all_to_all | solution.py:107
  20.1 0.8 pad_maximum_fusion.3
  20.9 0.7 collective-permute-start
  21.5 5.4 %all-to-all-done = bf16[8,16,128]{2,1,0:T(8,128)(2,1)S(1)} async-done(((bf16[8,16,128]{2,1,0:T(8,128)(2,1)}), bf16[8,16,128]{2,1,0:T(8,128)(2,1)S(1)}, u32[]{:S(2)}, u32[]{:S(2)}) %all-to-all-start) | async-done | bytes 32800 | tf_op jit(solution)/shard_map/all_to_all | solution.py:107
  27.0 0.0 collective-permute-done
  27.0 0.8 pad_maximum_fusion.2
  27.8 10.1 %all_to_all.20 = bf16[4,48,1024]{2,1,0:T(8,128)(2,1)S(1)} all-to-all(bf16[4,48,1024]{2,1,0:T(8,128)(2,1)S(1)} %tile.24), channel_id=1, replica_groups=mesh['row'=8,'y'=8,'core'=2,'vox'=4] {'vox'}, dimensions={0} | all-to-all | bytes 786432 | tf_op jit(solution)/shard_map/all_to_all | solution.py:107
  37.9 3.3 %collective-permute-start.1 = (bf16[4,3,16,1024]{3,2,1,0:T(8,128)(2,1)S(1)}, bf16[4,3,16,1024]{3,2,1,0:T(8,128)(2,1)S(1)}, u32[]{:S(2)}, u32[]{:S(2)}) collective-permute-start(bf16[4,3,16,1024]{3,2,1,0:T(8,128)(2,1)S(1)} %bitcast.35), channel_id=1, source_target_pairs={{0,8},{8,16},{16,24},{24,32},{32,40},{40,48},{48,56},{56,0},{1,9},... | collective-permute-start | bytes 1179656 | tf_op jit(solution)/shard_map/ppermute | solution.py:136
  41.2 6.0 %collective-permute-start.2 = (bf16[4,3,16,1024]{3,2,1,0:T(8,128)(2,1)S(1)}, bf16[4,3,16,1024]{3,2,1,0:T(8,128)(2,1)S(1)}, u32[]{:S(2)}, u32[]{:S(2)}) collective-permute-start(bf16[4,3,16,1024]{3,2,1,0:T(8,128)(2,1)S(1)} %bitcast.36), channel_id=1, source_target_pairs={{0,56},{8,0},{16,8},{24,16},{32,24},{40,32},{48,40},{56,48},{1,57}... | collective-permute-start | bytes 1179656 | tf_op jit(solution)/shard_map/ppermute | solution.py:136
  47.2 11.1 %all_to_all.21 = bf16[8,2,16,128]{3,2,1,0:T(8,128)(2,1)S(1)} all-to-all(bf16[8,2,16,128]{3,2,1,0:T(8,128)(2,1)S(1)} %copy.14), channel_id=1, replica_groups=mesh['row'=8,'y'=8,'core'=2,'vox'=4] {'core','vox'}, dimensions={0} | all-to-all | bytes 131072 | tf_op jit(solution)/shard_map/all_to_all | solution.py:169
  58.3 0.0 collective-permute-done.1.refs_1_
  58.3 0.0 collective-permute-done.2.refs_4_.refs_7_
  58.3 0.0 copy-start.6
  58.3 1.0 tile.26
  59.3 12.2 %all-to-all-start.3 = ((bf16[8,256,128]{2,1,0:T(8,128)(2,1)}), bf16[8,256,128]{2,1,0:T(8,128)(2,1)}, u32[]{:S(2)}, u32[]{:S(2)}) async-start(bf16[8,256,128]{2,1,0:T(8,128)(2,1)} %tile.26), calls=%async_computation.3 | async-start | bytes 1048576 | tf_op jit(solution)/shard_map/all_to_all | solution.py:107
  71.5 1.9 %collective-permute-start.3 = (bf16[4,3,16,1024]{3,2,1,0:T(8,128)(2,1)S(1)}, bf16[4,3,16,1024]{3,2,1,0:T(8,128)(2,1)S(1)}, u32[]{:S(2)}, u32[]{:S(2)}) collective-permute-start(bf16[4,3,16,1024]{3,2,1,0:T(8,128)(2,1)S(1)} %collective-permute-done.1.refs_1_), channel_id=1, source_target_pairs={{0,8},{8,16},{16,24},{24,32},{32,40},{40,48},{48,56},{56,0},{1,9},... | collective-permute-start | bytes 1179656 | tf_op jit(solution)/shard_map/ppermute | solution.py:136
  73.4 4.6 %collective-permute-start.6 = (bf16[4,3,16,1024]{3,2,1,0:T(8,128)(2,1)S(1)}, bf16[4,3,16,1024]{3,2,1,0:T(8,128)(2,1)}, u32[]{:S(2)}, u32[]{:S(2)}) collective-permute-start(bf16[4,3,16,1024]{3,2,1,0:T(8,128)(2,1)S(1)} %collective-permute-done.2.refs_4_.refs_7_), channel_id=1, source_target_pairs={{0,56},{8,0},{16,8},{24,16},{32,24},{40,32},{48,40},{56,48},{1,57}... | collective-permute-start | bytes 1179656 | tf_op jit(solution)/shard_map/ppermute | solution.py:136
  78.0 6.6 %collective-permute-done.3.refs_2_ = bf16[4,3,16,1024]{3,2,1,0:T(8,128)(2,1)S(1)} collective-permute-done((bf16[4,3,16,1024]{3,2,1,0:T(8,128)(2,1)S(1)}, bf16[4,3,16,1024]{3,2,1,0:T(8,128)(2,1)S(1)}, u32[]{:S(2)}, u32[]{:S(2)}) %collective-permute-start.3) | collective-permute-done | bytes 393248 | tf_op jit(solution)/shard_map/ppermute | solution.py:136
  84.6 1.9 %collective-permute-start.4 = (bf16[4,3,16,1024]{3,2,1,0:T(8,128)(2,1)S(1)}, bf16[4,3,16,1024]{3,2,1,0:T(8,128)(2,1)S(1)}, u32[]{:S(2)}, u32[]{:S(2)}) collective-permute-start(bf16[4,3,16,1024]{3,2,1,0:T(8,128)(2,1)S(1)} %collective-permute-done.3.refs_2_), channel_id=1, source_target_pairs={{0,8},{8,16},{16,24},{24,32},{32,40},{40,48},{48,56},{56,0},{1,9},... | collective-permute-start | bytes 1179656 | tf_op jit(solution)/shard_map/ppermute | solution.py:136
  86.6 0.0 collective-permute-done.6.refs_3_.refs_6_
  86.6 1.6 %stack.40 = bf16[5,4,3,16,1024]{4,3,2,1,0:T(8,128)(2,1)S(1)} custom-call(bf16[4,3,16,1024]{3,2,1,0:T(8,128)(2,1)S(1)} %bitcast.37, bf16[4,3,16,1024]{3,2,1,0:T(8,128)(2,1)S(1)} %collective-permute-done.1.refs_1_, bf16[4,3,16,1024]{3,2,1,0:T(8,128)(2,1)S(1)} %collective-permute-done.3.refs_2_, ...), custom_call_target="tpu_custom_call" | custom-call | tf_op jit(solution)/shard_map/stack/pallas_call | solution.py:124
  88.2 0.0 copy-done
  88.2 0.0 copy-done.5
  88.2 0.0 copy-done.6
  88.2 0.0 copy-done.7
  88.2 3.4 %collective-permute-start.8 = (bf16[5,4,3,16,1024]{4,3,2,1,0:T(8,128)(2,1)S(1)}, bf16[5,4,3,16,1024]{4,3,2,1,0:T(8,128)(2,1)}, u32[]{:S(2)}, u32[]{:S(2)}) collective-permute-start(bf16[5,4,3,16,1024]{4,3,2,1,0:T(8,128)(2,1)S(1)} %stack.40), channel_id=1, source_target_pairs={{0,4},{4,0},{1,5},{5,1},{2,6},{6,2},{3,7},{7,3},{8,12},{12,8},{9,1... | collective-permute-start | bytes 5898248 | tf_op jit(solution)/shard_map/ppermute | solution.py:177
  91.6 4.9 %collective-permute-start.7 = (bf16[4,3,16,1024]{3,2,1,0:T(8,128)(2,1)}, bf16[4,3,16,1024]{3,2,1,0:T(8,128)(2,1)S(1)}, u32[]{:S(2)}, u32[]{:S(2)}) collective-permute-start(bf16[4,3,16,1024]{3,2,1,0:T(8,128)(2,1)} %collective-permute-done.6.refs_3_.refs_6_), channel_id=1, source_target_pairs={{0,56},{8,0},{16,8},{24,16},{32,24},{40,32},{48,40},{56,48},{1,57}... | collective-permute-start | bytes 1179656 | tf_op jit(solution)/shard_map/ppermute | solution.py:136
  96.5 0.3 collective-permute-done.4.refs_0_.refs_3_
  96.8 0.0 all-to-all-done.3
  96.8 1.9 %collective-permute-start.5 = (bf16[4,3,16,1024]{3,2,1,0:T(8,128)(2,1)S(1)}, bf16[4,3,16,1024]{3,2,1,0:T(8,128)(2,1)S(1)}, u32[]{:S(2)}, u32[]{:S(2)}) collective-permute-start(bf16[4,3,16,1024]{3,2,1,0:T(8,128)(2,1)S(1)} %collective-permute-done.4.refs_0_.refs_3_), channel_id=1, source_target_pairs={{0,8},{8,16},{16,24},{24,32},{32,40},{40,48},{48,56},{56,0},{1,9},... | collective-permute-start | bytes 1179656 | tf_op jit(solution)/shard_map/ppermute | solution.py:136
  98.8 6.6 %collective-permute-done.7.refs_2_.refs_5_ = bf16[4,3,16,1024]{3,2,1,0:T(8,128)(2,1)S(1)} collective-permute-done((bf16[4,3,16,1024]{3,2,1,0:T(8,128)(2,1)}, bf16[4,3,16,1024]{3,2,1,0:T(8,128)(2,1)S(1)}, u32[]{:S(2)}, u32[]{:S(2)}) %collective-permute-start.7) | collective-permute-done | bytes 393248 | tf_op jit(solution)/shard_map/ppermute | solution.py:136
  105.3 0.7 copy-done.2
  106.1 2.1 %collective-permute-done.5.refs_1_.refs_4_ = bf16[4,3,16,1024]{3,2,1,0:T(8,128)(2,1)S(1)} collective-permute-done((bf16[4,3,16,1024]{3,2,1,0:T(8,128)(2,1)S(1)}, bf16[4,3,16,1024]{3,2,1,0:T(8,128)(2,1)S(1)}, u32[]{:S(2)}, u32[]{:S(2)}) %collective-permute-start.5) | collective-permute-done | bytes 393248 | tf_op jit(solution)/shard_map/ppermute | solution.py:136
  108.1 1.0 copy-done.3
  109.1 0.6 stack.41
  109.7 5.3 %collective-permute-start.9 = (bf16[3,4,3,16,1024]{4,3,2,1,0:T(8,128)(2,1)S(1)}, bf16[3,4,3,16,1024]{4,3,2,1,0:T(8,128)(2,1)}, u32[]{:S(2)}, u32[]{:S(2)}) collective-permute-start(bf16[3,4,3,16,1024]{4,3,2,1,0:T(8,128)(2,1)S(1)} %stack.41), channel_id=1, source_target_pairs={{0,4},{4,0},{1,5},{5,1},{2,6},{6,2},{3,7},{7,3},{8,12},{12,8},{9,1... | collective-permute-start | bytes 3538952 | tf_op jit(solution)/shard_map/ppermute | solution.py:179
  115.0 0.0 copy-done.4
  115.0 0.6 pad_add_fusion.at_ref
  115.6 1.1 fusion.1
  116.7 1.1 fusion
  117.8 0.0 copy-done.1
  117.8 1.2 pad_maximum_fusion
  119.0 0.0 collective-permute-done.8.refs_8_
  119.0 0.0 collective-permute-done.9.refs_9_
  119.0 13.8 %factor_and_update.1 = (bf16[2,16,1024]{2,1,0:T(8,128)(2,1)}, bf16[2,1024,128]{2,1,0:T(8,128)(2,1)}, f32[1024,128]{1,0:T(8,128)}, f32[1024,128]{1,0:T(8,128)}) custom-call(s32[3]{0:T(128)} %pad_add_fusion.at_ref, bf16[2,1024,1024]{2,1,0:T(8,128)(2,1)} %all-gather.2.cloned.1.call-done.whole, bf16[4,3,16,1024]{3,2,1,0:T(8,128)(2,1)} %bitcast.38, ...), custom_call_target="tpu_custom_call" | custom-call | flops 11274289152 | bytes 14680064 | tf_op jit(solution)/shard_map/factor_and_update/pallas_call | solution.py:193
  (13 shorter events, 0.1 us)
Async XLA Ops:
  7.2 89.7 %all-gather.2.cloned.1.call-start = ((), (), s32[]{:S(2)}) async-start(), calls=%async_computation.4 | async-start | bytes 4718592 | tf_op jit(solution)/shard_map/all_gather | solution.py:151
  9.2 17.7 %all-to-all-start = ((bf16[8,16,128]{2,1,0:T(8,128)(2,1)}), bf16[8,16,128]{2,1,0:T(8,128)(2,1)S(1)}, u32[]{:S(2)}, u32[]{:S(2)}) async-start(bf16[8,16,128]{2,1,0:T(8,128)(2,1)} %tile.10), calls=%async_computation | async-start | bytes 65536 | tf_op jit(solution)/shard_map/all_to_all | solution.py:107
  20.9 6.1 %collective-permute-start = (bf16[2,16,1024]{2,1,0:T(8,128)(2,1)S(1)}, bf16[2,16,1024]{2,1,0:T(8,128)(2,1)S(1)}, u32[]{:S(2)}, u32[]{:S(2)}) collective-permute-start(bf16[2,16,1024]{2,1,0:T(8,128)(2,1)S(1)} %pad_maximum_fusion.3), channel_id=1, source_target_pairs={{0,0},{1,1},{2,2},{3,3},{4,4},{5,5},{6,6},{7,7},{8,64},{9,65},{10,... | collective-permute-start | bytes 196616 | tf_op jit(solution)/shard_map/ppermute | solution.py:154
  37.9 50.3 %copy-start = (bf16[4,48,1024]{2,1,0:T(8,128)(2,1)}, bf16[4,48,1024]{2,1,0:T(8,128)(2,1)S(1)}, u32[]{:S(2)}) copy-start(bf16[4,48,1024]{2,1,0:T(8,128)(2,1)S(1)} %all_to_all.20) | copy-start | bytes 1179652
  37.9 20.4 %collective-permute-start.1 = (bf16[4,3,16,1024]{3,2,1,0:T(8,128)(2,1)S(1)}, bf16[4,3,16,1024]{3,2,1,0:T(8,128)(2,1)S(1)}, u32[]{:S(2)}, u32[]{:S(2)}) collective-permute-start(bf16[4,3,16,1024]{3,2,1,0:T(8,128)(2,1)S(1)} %bitcast.35), channel_id=1, source_target_pairs={{0,8},{8,16},{16,24},{24,32},{32,40},{40,48},{48,56},{56,0},{1,9},... | collective-permute-start | bytes 1179656 | tf_op jit(solution)/shard_map/ppermute | solution.py:136
  41.2 17.1 %collective-permute-start.2 = (bf16[4,3,16,1024]{3,2,1,0:T(8,128)(2,1)S(1)}, bf16[4,3,16,1024]{3,2,1,0:T(8,128)(2,1)S(1)}, u32[]{:S(2)}, u32[]{:S(2)}) collective-permute-start(bf16[4,3,16,1024]{3,2,1,0:T(8,128)(2,1)S(1)} %bitcast.36), channel_id=1, source_target_pairs={{0,56},{8,0},{16,8},{24,16},{32,24},{40,32},{48,40},{56,48},{1,57}... | collective-permute-start | bytes 1179656 | tf_op jit(solution)/shard_map/ppermute | solution.py:136
  58.3 29.9 %copy-start.5 = (bf16[4,3,16,1024]{3,2,1,0:T(8,128)(2,1)}, bf16[4,3,16,1024]{3,2,1,0:T(8,128)(2,1)S(1)}, u32[]{:S(2)}) copy-start(bf16[4,3,16,1024]{3,2,1,0:T(8,128)(2,1)S(1)} %collective-permute-done.1.refs_1_) | copy-start | bytes 1179652
  58.3 29.9 %copy-start.6 = (bf16[4,3,16,1024]{3,2,1,0:T(8,128)(2,1)}, bf16[4,3,16,1024]{3,2,1,0:T(8,128)(2,1)S(1)}, u32[]{:S(2)}) copy-start(bf16[4,3,16,1024]{3,2,1,0:T(8,128)(2,1)S(1)} %collective-permute-done.2.refs_4_.refs_7_) | copy-start | bytes 1179652
  59.3 37.6 %all-to-all-start.3 = ((bf16[8,256,128]{2,1,0:T(8,128)(2,1)}), bf16[8,256,128]{2,1,0:T(8,128)(2,1)}, u32[]{:S(2)}, u32[]{:S(2)}) async-start(bf16[8,256,128]{2,1,0:T(8,128)(2,1)} %tile.26), calls=%async_computation.3 | async-start | bytes 1048576 | tf_op jit(solution)/shard_map/all_to_all | solution.py:107
  71.5 13.1 %collective-permute-start.3 = (bf16[4,3,16,1024]{3,2,1,0:T(8,128)(2,1)S(1)}, bf16[4,3,16,1024]{3,2,1,0:T(8,128)(2,1)S(1)}, u32[]{:S(2)}, u32[]{:S(2)}) collective-permute-start(bf16[4,3,16,1024]{3,2,1,0:T(8,128)(2,1)S(1)} %collective-permute-done.1.refs_1_), channel_id=1, source_target_pairs={{0,8},{8,16},{16,24},{24,32},{32,40},{40,48},{48,56},{56,0},{1,9},... | collective-permute-start | bytes 1179656 | tf_op jit(solution)/shard_map/ppermute | solution.py:136
  73.4 13.1 %collective-permute-start.6 = (bf16[4,3,16,1024]{3,2,1,0:T(8,128)(2,1)S(1)}, bf16[4,3,16,1024]{3,2,1,0:T(8,128)(2,1)}, u32[]{:S(2)}, u32[]{:S(2)}) collective-permute-start(bf16[4,3,16,1024]{3,2,1,0:T(8,128)(2,1)S(1)} %collective-permute-done.2.refs_4_.refs_7_), channel_id=1, source_target_pairs={{0,56},{8,0},{16,8},{24,16},{32,24},{40,32},{48,40},{56,48},{1,57}... | collective-permute-start | bytes 1179656 | tf_op jit(solution)/shard_map/ppermute | solution.py:136
  84.6 3.6 %copy-start.7 = (bf16[4,3,16,1024]{3,2,1,0:T(8,128)(2,1)}, bf16[4,3,16,1024]{3,2,1,0:T(8,128)(2,1)S(1)}, u32[]{:S(2)}) copy-start(bf16[4,3,16,1024]{3,2,1,0:T(8,128)(2,1)S(1)} %collective-permute-done.3.refs_2_) | copy-start | bytes 1179652
  84.6 12.2 %collective-permute-start.4 = (bf16[4,3,16,1024]{3,2,1,0:T(8,128)(2,1)S(1)}, bf16[4,3,16,1024]{3,2,1,0:T(8,128)(2,1)S(1)}, u32[]{:S(2)}, u32[]{:S(2)}) collective-permute-start(bf16[4,3,16,1024]{3,2,1,0:T(8,128)(2,1)S(1)} %collective-permute-done.3.refs_2_), channel_id=1, source_target_pairs={{0,8},{8,16},{16,24},{24,32},{32,40},{40,48},{48,56},{56,0},{1,9},... | collective-permute-start | bytes 1179656 | tf_op jit(solution)/shard_map/ppermute | solution.py:136
  88.2 30.8 %collective-permute-start.8 = (bf16[5,4,3,16,1024]{4,3,2,1,0:T(8,128)(2,1)S(1)}, bf16[5,4,3,16,1024]{4,3,2,1,0:T(8,128)(2,1)}, u32[]{:S(2)}, u32[]{:S(2)}) collective-permute-start(bf16[5,4,3,16,1024]{4,3,2,1,0:T(8,128)(2,1)S(1)} %stack.40), channel_id=1, source_target_pairs={{0,4},{4,0},{1,5},{5,1},{2,6},{6,2},{3,7},{7,3},{8,12},{12,8},{9,1... | collective-permute-start | bytes 5898248 | tf_op jit(solution)/shard_map/ppermute | solution.py:177
  91.6 13.7 %collective-permute-start.7 = (bf16[4,3,16,1024]{3,2,1,0:T(8,128)(2,1)}, bf16[4,3,16,1024]{3,2,1,0:T(8,128)(2,1)S(1)}, u32[]{:S(2)}, u32[]{:S(2)}) collective-permute-start(bf16[4,3,16,1024]{3,2,1,0:T(8,128)(2,1)} %collective-permute-done.6.refs_3_.refs_6_), channel_id=1, source_target_pairs={{0,56},{8,0},{16,8},{24,16},{32,24},{40,32},{48,40},{56,48},{1,57}... | collective-permute-start | bytes 1179656 | tf_op jit(solution)/shard_map/ppermute | solution.py:136
  96.8 20.9 %copy-start.1 = (bf16[4,3,16,1024]{3,2,1,0:T(8,128)(2,1)}, bf16[4,3,16,1024]{3,2,1,0:T(8,128)(2,1)S(1)}, u32[]{:S(2)}) copy-start(bf16[4,3,16,1024]{3,2,1,0:T(8,128)(2,1)S(1)} %collective-permute-done.4.refs_0_.refs_3_) | copy-start | bytes 1179652
  96.8 11.3 %collective-permute-start.5 = (bf16[4,3,16,1024]{3,2,1,0:T(8,128)(2,1)S(1)}, bf16[4,3,16,1024]{3,2,1,0:T(8,128)(2,1)S(1)}, u32[]{:S(2)}, u32[]{:S(2)}) collective-permute-start(bf16[4,3,16,1024]{3,2,1,0:T(8,128)(2,1)S(1)} %collective-permute-done.4.refs_0_.refs_3_), channel_id=1, source_target_pairs={{0,8},{8,16},{16,24},{24,32},{32,40},{40,48},{48,56},{56,0},{1,9},... | collective-permute-start | bytes 1179656 | tf_op jit(solution)/shard_map/ppermute | solution.py:136
  105.3 0.8 copy-start.2
  108.1 1.0 copy-start.3
  109.1 5.9 %copy-start.4 = (bf16[4,3,16,1024]{3,2,1,0:T(8,128)(2,1)}, bf16[4,3,16,1024]{3,2,1,0:T(8,128)(2,1)S(1)}, u32[]{:S(2)}) copy-start(bf16[4,3,16,1024]{3,2,1,0:T(8,128)(2,1)S(1)} %collective-permute-done.5.refs_1_.refs_4_) | copy-start | bytes 1179652
  109.7 9.3 %collective-permute-start.9 = (bf16[3,4,3,16,1024]{4,3,2,1,0:T(8,128)(2,1)S(1)}, bf16[3,4,3,16,1024]{4,3,2,1,0:T(8,128)(2,1)}, u32[]{:S(2)}, u32[]{:S(2)}) collective-permute-start(bf16[3,4,3,16,1024]{4,3,2,1,0:T(8,128)(2,1)S(1)} %stack.41), channel_id=1, source_target_pairs={{0,4},{4,0},{1,5},{5,1},{2,6},{6,2},{3,7},{7,3},{8,12},{12,8},{9,1... | collective-permute-start | bytes 3538952 | tf_op jit(solution)/shard_map/ppermute | solution.py:179
Sparse Core Ops, SparseCore 0:
  10.1 63.7 all-gather.1
